TPU v7x, 32 devices: a whole 2x2x4 slice. The times are simulated.
32 devices in a mesh: grp: 4 (over y, core), lat: 2 (over x), lon: 4 (over z).
Axes of the slice: x: 2, y: 2, z: 4, core: 2. Of those that a mesh axis runs over, the one named last changes fastest.
Arguments:
- layer_source_tensor: bfloat16 [8, 32, 64, 768], P(('grp', 'lat'), None, 'lon'), may hold values from -6 to 6
- horizon_class: int32 [8], P(('grp', 'lat')), may hold values from 0 to 23
- field_selector: int32 [8, 69], P(('grp', 'lat')), may hold values 0 or 1
- model_predictions: bfloat16 [8, 32, 64, 2, 4416], P(('grp', 'lat'), None, 'lon'), may hold values from -6 to 6
- loss_sensitivity: bfloat16 [8, 32, 64, 4416], P(('grp', 'lat'), None, 'lon'), may hold values from -6 to 6
- initial_standardize_gain: float32 [768], replicated, may hold values from 0.5 to 1.5
- initial_standardize_shift: float32 [768], replicated, may hold values from -1.75 to 1.75
- horizon_vectors: float32 [24, 768], replicated, may hold values from -3 to 3
- projection_triple_matrix: bfloat16 [768, 2304], replicated, may hold values from -0.21875 to 0.21875
- context_projector_matrix: bfloat16 [768, 768], replicated, may hold values from -4 to 4
- later_standardize_gain: float32 [768], replicated, may hold values from 0.5 to 1.5
- later_standardize_shift: float32 [768], replicated, may hold values from -1.75 to 1.75
- expand_matrix: bfloat16 [768, 3072], replicated, may hold values from -0.21875 to 0.21875
- expand_shift_vector: float32 [3072], replicated, may hold values from -1.75 to 1.75
- shrink_matrix: bfloat16 [3072, 768], replicated, may hold values from -0.109375 to 0.109375
- shrink_shift_vector: float32 [768], replicated, may hold values from -1.75 to 1.75
- mixing_predictor_matrix: bfloat16 [768, 138], replicated, may hold values from -0.09375 to 0.09375
- shift_predictor_matrix: bfloat16 [768, 69], replicated, may hold values from -0.09375 to 0.09375
Outputs:
- blended: bfloat16 [8, 32, 64, 4416], P(('grp', 'lat'), None, 'lon')
- x_grad: float32 [8, 32, 64, 768], P(('grp', 'lat'), None, 'lon')
- ln1_gain_grad: float32 [768], P(('lat', 'lon'))
- ln1_bias_grad: float32 [768], P(('lat', 'lon'))
- lead_table_grad: float32 [24, 768], P(None, ('lat', 'lon'))
- w_qkv_grad: float32 [768, 2304], P(('lat', 'lon'))
- w_out_grad: float32 [768, 768], P(('lat', 'lon'))
- ln2_gain_grad: float32 [768], P(('lat', 'lon'))
- ln2_bias_grad: float32 [768], P(('lat', 'lon'))
- w_up_grad: float32 [768, 3072], P(('lat', 'lon'))
- b_up_grad: float32 [3072], P(('lat', 'lon'))
- w_down_grad: float32 [3072, 768], P(('lat', 'lon'))
- b_down_grad: float32 [768], P(('lat', 'lon'))
- w_gate_grad: float32 [768, 138], P(('lat', 'lon'))
- w_bias_grad: float32 [768, 69], P(('lat', 'lon'))
Inputs may be any that keep to these rules, and one draw needn't show every extreme that they name: `field_selector`: 1 where a channel is blended, 0 where it takes the first expert's forecast.
All inputs are finite; a program needn't handle non-finite values. No bound on the sum of `field_selector` on one device may be relied on, other than what follows from the above.
Results may differ from a plain program's by a relative error of at most 0.018.
The roundings to bfloat16 on the way count: a program that leaves them out, or rounds other values in their place, can miss the bound.
Values may be sent and summed in bfloat16 or wider, within the bound.
No kernel may reach another device: no remote copies, remote signals or barrier semaphores. Data moves between devices by JAX's collectives and lax.ppermute only.
A program may use at most 704 MiB of HBM per device.

v0:
```python
import functools
import math

import jax
import jax.numpy as jnp
from jax import lax
from jax.experimental import pallas as pl
from jax.experimental.pallas import tpu as pltpu
from jax.sharding import PartitionSpec as P

H = 12
DH = 64
RESULT_FIELDS = 69
TILE_AREA = 64
LEADS = 24
EPSILON = 1e-06
HIGH = lax.Precision.HIGHEST
SCALE = 0.125
SCALE_TWO = SCALE * math.log2(math.e)
ROOT = math.sqrt(2.0 / math.pi)
CUBE = 0.044715
NN = (((1,), (0,)), ((), ()))
NT = (((1,), (1,)), ((), ()))
TN = (((0,), (0,)), ((), ()))
BF = jnp.bfloat16
F32 = jnp.float32
PARAMS = pltpu.CompilerParams(vmem_limit_bytes=60 * 1024 * 1024)
FULL = pltpu.CompilerParams(vmem_limit_bytes=63 * 1024 * 1024 + 512 * 1024)


def dot(left, right, dims=NN):
    return lax.dot_general(left, right, dims, preferred_element_type=F32)


def project_kernel(own, *refs):
    if own:
        a_ref, gain_ref, shift_ref, lead_ref, wq_ref, wk_ref, wv_ref, mixed_ref, kv_ref, q_ref = refs
        value = a_ref[...]
    else:
        flag_ref, a_ref, b_ref, gain_ref, shift_ref, lead_ref, wk_ref, wv_ref = refs[:8]
        mixed_ref, kv_ref, x_ref = refs[8:]
        value = jnp.where(flag_ref[0] != 0, a_ref[...], b_ref[...])
        x_ref[...] = value
    normed, _ = layer_norm(value.astype(F32))
    mixed = (normed * gain_ref[...][None] + shift_ref[...][None] + lead_ref[...]).astype(BF)
    mixed_ref[...] = mixed
    width = mixed.shape[1]
    kv_ref[:, :width] = dot(mixed, wk_ref[...]).astype(BF)
    kv_ref[:, width:] = dot(mixed, wv_ref[...]).astype(BF)
    if own:
        q_ref[...] = dot(mixed, wq_ref[...]).astype(BF)


def project(flag, sources, gain, shift, lead, weights):
    own = flag is None
    rows, width = sources[0].shape
    block = math.gcd(rows, 256)
    row = pl.BlockSpec((block, width), lambda i: (i, 0))
    vector = pl.BlockSpec((width,), lambda i: (0,))

    def columns(group):
        return pl.BlockSpec((width, width), lambda i: (0, group))

    groups = (0, 1, 2) if own else (1, 2)
    return pl.pallas_call(
        functools.partial(project_kernel, own),
        grid=(rows // block,),
        in_specs=([] if own else [pl.BlockSpec(memory_space=pltpu.SMEM)])
        + [row] * len(sources)
        + [vector, vector, pl.BlockSpec((1, width), lambda i: (0, 0))]
        + [columns(g) for g in groups],
        out_specs=[row, pl.BlockSpec((block, 2 * width), lambda i: (i, 0)), row],
        out_shape=[
            jax.ShapeDtypeStruct((rows, width), BF),
            jax.ShapeDtypeStruct((rows, 2 * width), BF),
            jax.ShapeDtypeStruct((rows, width), BF),
        ],
        compiler_params=PARAMS,
        name="project",
        cost_estimate=pl.CostEstimate(
            flops=rows * width * width, transcendentals=0, bytes_accessed=rows * width
        ),
    )(*([] if own else [flag]), *sources, gain, shift, lead, *([weights] * len(groups)))


def attend_kernel(count, chained, final, *refs):
    q_ref = refs[0]
    k_refs = refs[1 : 1 + count]
    v_refs = refs[1 + count : 1 + 2 * count]
    o_ref, l_ref = refs[-2:]
    outs = []
    for h in range(2):
        part = slice(h * DH, h * DH + DH)
        q = q_ref[0, :, part]
        scores = [dot(k[0, :, part], q, NT) for k in k_refs]
        top = functools.reduce(
            jnp.maximum, [jnp.max(s, axis=0, keepdims=True) for s in scores]
        )
        top = top * SCALE_TWO
        total = None
        mixed = None
        for s, v in zip(scores, v_refs):
            raised = jnp.exp2(s * SCALE_TWO - top)
            some = jnp.sum(raised, axis=0, keepdims=True)
            term = dot(v[0, :, part], raised.astype(BF), TN)
            total = some if total is None else total + some
            mixed = term if mixed is None else mixed + term
        mixed = mixed * (1.0 / total)
        log = top + jnp.log2(total)
        if chained:
            before_ref, before_log_ref = refs[1 + 2 * count : 3 + 2 * count]
            before = before_log_ref[0, 0, h : h + 1, :]
            high = jnp.maximum(before, log)
            joint = high + jnp.log2(jnp.exp2(before - high) + jnp.exp2(log - high))
            mixed = mixed * jnp.exp2(log - joint) + before_ref[0, part, :] * jnp.exp2(
                before - joint
            )
            log = joint
        l_ref[0, 0, h : h + 1, :] = log
        if final:
            outs.append(mixed)
        else:
            o_ref[0, part, :] = mixed
    if final:
        o_ref[0] = jnp.concatenate(outs, axis=0).T.astype(BF)


def attend(queries, shards, before, final):
    frames, rows, width = queries.shape
    count = len(shards)
    keys = shards[0].shape[1]
    pairs = width // 128
    turned = pl.BlockSpec((1, 128, rows), lambda f, p: (f, p, 0))
    row = pl.BlockSpec((1, rows, 128), lambda f, p: (f, 0, p))
    log = pl.BlockSpec((1, 1, 2, rows), lambda f, p: (f, p, 0, 0))
    chained = before is not None
    return pl.pallas_call(
        functools.partial(attend_kernel, count, chained, final),
        grid=(frames, pairs),
        in_specs=[row]
        + [pl.BlockSpec((1, keys, 128), lambda f, p: (f, 0, p))] * count
        + [pl.BlockSpec((1, keys, 128), lambda f, p: (f, 0, p + pairs))] * count
        + ([turned, log] if chained else []),
        out_specs=[row if final else turned, log],
        out_shape=[
            jax.ShapeDtypeStruct((frames, rows, width), BF)
            if final
            else jax.ShapeDtypeStruct((frames, width, rows), F32),
            jax.ShapeDtypeStruct((frames, pairs, 2, rows), F32),
        ],
        compiler_params=PARAMS,
        name="attend",
        cost_estimate=pl.CostEstimate(
            flops=2 * frames * rows * count * keys * width,
            transcendentals=0,
            bytes_accessed=frames * rows * width,
        ),
    )(queries, *shards, *shards, *(before if chained else ()))


def column_sums(total, values):
    normed, _ = layer_norm(values.astype(F32))
    return jnp.concatenate(
        (
            jnp.sum(total * normed, axis=0, keepdims=True),
            jnp.sum(total, axis=0, keepdims=True),
        )
    )


def attend_back_kernel(
    q_ref,
    g_ref,
    o_ref,
    l_ref,
    k_ref,
    v_ref,
    wk_ref,
    wv_ref,
    x_ref,
    before_ref,
    dq_ref,
    dkv_ref,
    term_ref,
    sums_ref,
):
    pair = pl.program_id(1)
    key_terms = []
    value_terms = []
    query_terms = []
    for h in range(2):
        part = slice(h * DH, h * DH + DH)
        q = q_ref[0, :, part]
        g = g_ref[0, :, part]
        k = k_ref[0, :, part]
        v = v_ref[0, :, part]
        product = g.astype(F32) * o_ref[0, :, part].astype(F32)
        high, low = split_two(product)
        ones = jnp.ones((8, DH), BF)
        delta = (dot(ones, high, NT) + dot(ones, low, NT))[0:1]
        probs = jnp.exp2(dot(k, q, NT) * SCALE_TWO - l_ref[0, 0, h : h + 1, :])
        grad_probs = dot(v, g, NT)
        grad_scores = (probs * (grad_probs - delta)).astype(BF)
        value_terms.append(dot(probs.astype(BF), g))
        key_terms.append(dot(grad_scores, q))
        grad_query = dot(k, grad_scores, TN) * SCALE + before_ref[0, part, :]
        query_terms.append(grad_query)
    grad_key = (jnp.concatenate(key_terms, axis=1) * SCALE).astype(BF)
    grad_value = jnp.concatenate(value_terms, axis=1).astype(BF)
    grad_query = jnp.concatenate(query_terms, axis=0).astype(dq_ref.dtype)
    width = wk_ref.shape[0]
    dkv_ref[0, :, pl.ds(pl.multiple_of(pair * 128, 128), 128)] = grad_key
    dkv_ref[0, :, pl.ds(pl.multiple_of(width + pair * 128, 128), 128)] = grad_value
    dq_ref[0] = grad_query

    @pl.when(pair == pl.num_programs(1) - 1)
    def _():
        total = dot(dkv_ref[0, :, :width], wk_ref[...], NT)
        total = total + dot(dkv_ref[0, :, width:], wv_ref[...], NT)
        term_ref[0] = total.astype(term_ref.dtype)
        sums_ref[0] = column_sums(total, x_ref[0])


def attend_back(queries, grad_out, out, logs, shard, weights, source, before):
    frames, rows, width = queries.shape
    keys = shard.shape[1]
    pairs = width // 128
    row = pl.BlockSpec((1, rows, 128), lambda f, p: (f, 0, p))
    key = pl.BlockSpec((1, keys, 128), lambda f, p: (f, 0, p))
    value = pl.BlockSpec((1, keys, 128), lambda f, p: (f, 0, p + pairs))
    turned = pl.BlockSpec((1, 128, rows), lambda f, p: (f, p, 0))
    log = pl.BlockSpec((1, 1, 2, rows), lambda f, p: (f, p, 0, 0))

    def columns(group):
        return pl.BlockSpec((width, width), lambda f, p: (0, group))

    def whole(*shape):
        return pl.BlockSpec((1,) + shape, lambda f, p: (f, 0, 0))

    in_specs = [row, row, row, log, key, value, columns(1), columns(2), whole(keys, width)]
    operands = [queries, grad_out, out, logs, shard, shard, weights, weights, source]
    aliases = {len(operands): 0}
    in_specs.append(turned)
    operands.append(before)
    out_specs = [turned, whole(keys, 2 * width), whole(keys, width), whole(2, width)]
    out_shape = [
        jax.ShapeDtypeStruct((frames, width, rows), F32),
        jax.ShapeDtypeStruct((frames, keys, 2 * width), BF),
        jax.ShapeDtypeStruct((frames, keys, width), BF),
        jax.ShapeDtypeStruct((frames, 2, width), F32),
    ]
    return pl.pallas_call(
        attend_back_kernel,
        grid=(frames, pairs),
        in_specs=in_specs,
        out_specs=out_specs,
        out_shape=out_shape,
        input_output_aliases=aliases,
        compiler_params=PARAMS,
        name="attend_back",
        cost_estimate=pl.CostEstimate(
            flops=4 * frames * rows * keys * width,
            transcendentals=0,
            bytes_accessed=frames * rows * width,
        ),
    )(*operands)


def query_back_kernel(dq_ref, w_ref, x_ref, low_ref, term_ref, sums_ref):
    low = dq_ref[0].astype(BF)
    low_ref[0] = low
    total = dot(low, w_ref[...], (((0,), (1,)), ((), ())))
    term_ref[0] = total
    sums_ref[0] = column_sums(total, x_ref[0])


def query_back(grad_query, weights, source):
    frames, width, rows = grad_query.shape

    def whole(*shape):
        return pl.BlockSpec((1,) + shape, lambda f: (f, 0, 0))

    return pl.pallas_call(
        query_back_kernel,
        grid=(frames,),
        in_specs=[
            whole(width, rows),
            pl.BlockSpec((width, width), lambda f: (0, 0)),
            whole(rows, width),
        ],
        out_specs=[whole(width, rows), whole(rows, width), whole(2, width)],
        out_shape=[
            jax.ShapeDtypeStruct((frames, width, rows), BF),
            jax.ShapeDtypeStruct((frames, rows, width), F32),
            jax.ShapeDtypeStruct((frames, 2, width), F32),
        ],
        compiler_params=PARAMS,
        name="query_back",
        cost_estimate=pl.CostEstimate(
            flops=frames * rows * width * width, transcendentals=0, bytes_accessed=rows * width
        ),
    )(grad_query, weights, source)


def between_kernel(
    x_ref,
    att_ref,
    wo_ref,
    wu_ref,
    wd_ref,
    head_ref,
    gain_ref,
    shift_ref,
    bu_ref,
    bd_ref,
    mask_ref,
    sens_ref,
    one_ref,
    two_ref,
    hidden_ref,
    act_ref,
    up_ref,
    down_ref,
    final_ref,
    heads_ref,
    attn_ref,
    gres_ref,
    gatt_ref,
    first_ref,
    second_ref,
    added_ref,
    vec_ref,
    bup_ref,
    slope_ref,
    sum_ref,
    ups_ref,
):
    residual = x_ref[...].astype(F32) + dot(att_ref[...], wo_ref[...])
    normed, inverse = layer_norm(residual)
    gain = gain_ref[...][None]
    hidden = (normed * gain + shift_ref[...][None]).astype(BF)
    hidden_ref[...] = hidden
    wide = 512
    steps = wu_ref.shape[1] // wide
    sum_ref[...] = residual + bd_ref[...][None]

    def chunk(j):
        return pl.ds(pl.multiple_of(j * wide, wide), wide)

    @pl.loop(0, steps)
    def _(j):
        part = chunk(j)
        up = dot(hidden, wu_ref[:, part]) + bu_ref[part][None]
        square = up * up
        tanh = jnp.tanh(ROOT * up * (1.0 + CUBE * square))
        half = 0.5 * (1.0 + tanh)
        act = (up * half).astype(BF)
        slope_ref[:, part] = half + 0.5 * up * (1.0 - tanh * tanh) * (
            ROOT + 3.0 * ROOT * CUBE * square
        )
        act_ref[:, part] = act
        sum_ref[...] += dot(act, wd_ref[part, :])

    final = sum_ref[...]
    final_low = final.astype(BF)
    final_ref[...] = final_low
    logits = dot(final_low, head_ref[...], NT)
    one = logits[:, :128]
    two = logits[:, 128:256]
    offset = logits[:, 256:]
    top = jnp.maximum(one, two)
    one = jnp.exp(one - top)
    two = jnp.exp(two - top)
    total = one + two
    one = one / total
    two = two / total
    mask = mask_ref[0]
    first_ref[...] = mask * one + (1.0 - mask)
    second_ref[...] = mask * two
    added_ref[...] = mask * offset
    grad_one = mask * one_ref[...]
    grad_two = mask * two_ref[...]
    mean = one * grad_one + two * grad_two
    heads = jnp.concatenate(
        (one * (grad_one - mean), two * (grad_two - mean), mask * sens_ref[...]), axis=1
    ).astype(BF)
    heads_ref[...] = heads
    grad_final = dot(heads, head_ref[...])
    down = grad_final.astype(BF)
    down_ref[...] = down
    sum_ref[...] = jnp.zeros_like(sum_ref)

    @pl.loop(0, steps)
    def _(j):
        part = chunk(j)
        grad_up = (dot(down, wd_ref[part, :], NT) * slope_ref[:, part]).astype(BF)
        up_ref[:, part] = grad_up
        ups_ref[:, part] = jnp.sum(grad_up.astype(F32), axis=0, keepdims=True)
        sum_ref[...] += dot(grad_up, wu_ref[:, part], NT)

    grad_hidden = sum_ref[...]
    grad_normed = grad_hidden * gain
    grad_residual = grad_final + norm_back(grad_normed, normed, inverse)
    gres_ref[...] = grad_residual
    attn = grad_residual.astype(BF)
    attn_ref[...] = attn
    gatt_ref[...] = dot(attn, wo_ref[...], NT).astype(BF)
    vectors = jnp.concatenate(
        (
            jnp.sum(grad_hidden * normed, axis=0, keepdims=True),
            jnp.sum(grad_hidden, axis=0, keepdims=True),
            jnp.sum(down.astype(F32), axis=0, keepdims=True),
        )
    )
    ups = ups_ref[...]

    @pl.when(pl.program_id(0) == 0)
    def _():
        vec_ref[...] = vectors
        bup_ref[...] = ups

    @pl.when(pl.program_id(0) > 0)
    def _():
        vec_ref[...] += vectors
        bup_ref[...] += ups


def between(x, attended, w_out, w_up, w_down, heads, gain, shift, b_up, b_down, mask, sums, local):
    rows, width = x.shape
    hidden = w_up.shape[1]
    block = math.gcd(local, 256)

    def row(columns):
        return pl.BlockSpec((block, columns), lambda i: (i, 0))

    def whole(values):
        zeros = (0,) * values.ndim
        return pl.BlockSpec(values.shape, lambda i: zeros, pipeline_mode=pl.Buffered(1))

    def shape(columns, kind=BF):
        return jax.ShapeDtypeStruct((rows, columns), kind)

    fixed = [w_out, w_up, w_down, heads, gain, shift, b_up, b_down]
    return pl.pallas_call(
        between_kernel,
        grid=(rows // block,),
        in_specs=[row(width), row(width)]
        + [whole(v) for v in fixed]
        + [pl.BlockSpec((1, 1, 128), lambda i: (i * block // local, 0, 0))]
        + [row(128)] * 3,
        out_specs=[
            row(width),
            row(hidden),
            row(hidden),
            row(width),
            row(width),
            row(384),
            row(width),
            row(width),
            row(width),
            row(128),
            row(128),
            row(128),
            pl.BlockSpec((3, width), lambda i: (0, 0)),
            pl.BlockSpec((1, hidden), lambda i: (0, 0)),
        ],
        out_shape=[
            shape(width),
            shape(hidden),
            shape(hidden),
            shape(width),
            shape(width),
            shape(384),
            shape(width),
            shape(width, F32),
            shape(width),
            shape(128, F32),
            shape(128, F32),
            shape(128, F32),
            jax.ShapeDtypeStruct((3, width), F32),
            jax.ShapeDtypeStruct((1, hidden), F32),
        ],
        scratch_shapes=[
            pltpu.VMEM((block, hidden), F32),
            pltpu.VMEM((block, width), F32),
            pltpu.VMEM((1, hidden), F32),
        ],
        compiler_params=PARAMS,
        name="between",
        cost_estimate=pl.CostEstimate(
            flops=rows * width * hidden, transcendentals=0, bytes_accessed=rows * hidden
        ),
    )(x, attended, *fixed, mask, *sums)


def deal(place, result, mine_ref, sent_ref):
    halves = result.reshape(mine_ref.shape[0], 2, *mine_ref.shape[1:]).astype(BF)
    low = halves[:, 0]
    high = halves[:, 1]
    even = place == 0
    mine_ref[...] = jnp.where(even, low, high)
    sent_ref[...] = jnp.where(even, high, low)


def columns_of(vectors, start):
    count = vectors.shape[0]
    place = lax.broadcasted_iota(jnp.int32, (count, 256), 1)
    which = lax.broadcasted_iota(jnp.int32, (count, 256), 0)
    chosen = (place == which + start).astype(F32).astype(BF)
    high, rest = split_two(vectors)
    return dot(high, chosen, TN) + dot(rest, chosen, TN)


def early_grads_kernel(
    place_ref,
    h_ref,
    a_ref,
    f_ref,
    up_ref,
    attn_ref,
    head_ref,
    vec_ref,
    mine_in_ref,
    sent_in_ref,
    mine_ref,
    sent_ref,
    turn_ref,
):
    step = pl.program_id(0)
    last = pl.num_programs(0) - 1
    place = place_ref[0]
    wide = up_ref.shape[1]

    @pl.when(step == 0)
    def _():
        turn_ref[...] = h_ref[...].T

    @pl.when(step < last - 1)
    def _():
        deal(place, dot(turn_ref[...], up_ref[...]), mine_ref, sent_ref)

    @pl.when(step == last - 1)
    def _():
        turned = a_ref[...].T
        turn_ref[...] = turned
        deal(place, dot(turned, attn_ref[:, :wide]), mine_ref, sent_ref)

    @pl.when(step == last)
    def _():
        out = dot(turn_ref[...], attn_ref[:, wide:])
        heads = dot(f_ref[...].T, head_ref[...]) + columns_of(vec_ref[...], 3 * RESULT_FIELDS)
        deal(place, jnp.concatenate((out, heads), axis=1), mine_ref, sent_ref)


def early_grads(place, hidden, attended, final, up, attn, heads, vectors, mine, sent):
    rows, width = hidden.shape
    wide = 512
    steps = up.shape[1] // wide + 2
    count = width // 96
    skip = mine.shape[2] // wide - steps

    def whole(values):
        return pl.BlockSpec(values.shape, lambda i: (0, 0))

    out = pl.BlockSpec((count, 48, wide), lambda i: (0, 0, i + skip))
    untouched = pl.BlockSpec(memory_space=pl.ANY)
    return pl.pallas_call(
        early_grads_kernel,
        grid=(steps,),
        in_specs=[
            pl.BlockSpec(memory_space=pltpu.SMEM),
            whole(hidden),
            whole(attended),
            whole(final),
            pl.BlockSpec((rows, wide), lambda i: (0, jnp.minimum(i, steps - 3))),
            whole(attn),
            whole(heads),
            whole(vectors),
            untouched,
            untouched,
        ],
        out_specs=[out, out],
        out_shape=[jax.ShapeDtypeStruct(mine.shape, BF)] * 2,
        input_output_aliases={8: 0, 9: 1},
        scratch_shapes=[pltpu.VMEM((width, rows), BF)],
        compiler_params=PARAMS,
        name="early_grads",
        cost_estimate=pl.CostEstimate(
            flops=2 * rows * width * wide * steps,
            transcendentals=0,
            bytes_accessed=2 * rows * wide * steps + 2 * width * wide * steps,
        ),
    )(place, hidden, attended, final, up, attn, heads, vectors, mine, sent)


def down_grads_kernel(place_ref, act_ref, down_ref, mine_ref, sent_ref):
    result = dot(act_ref[...], down_ref[...], TN).astype(BF)
    block = result.shape[0] // 2
    piece = block // 8
    halves = []
    for c in range(2):
        groups = [
            jnp.concatenate(
                [
                    result[c * block + y * 4 * piece + g * piece :][:piece]
                    for y in range(2)
                ],
                axis=0,
            )
            for g in range(4)
        ]
        halves.append(jnp.concatenate(groups, axis=1)[None])
    even = place_ref[0] == 0
    mine_ref[...] = jnp.where(even, halves[0], halves[1])
    sent_ref[...] = jnp.where(even, halves[1], halves[0])


def down_grads(place, activation, down, columns):
    rows, width = down.shape
    block = activation.shape[1] // 8
    piece = block // 16
    out = pl.BlockSpec((1, 2 * piece, 4 * width), lambda i: (i, 0, 0))
    return pl.pallas_call(
        down_grads_kernel,
        grid=(8,),
        in_specs=[
            pl.BlockSpec(memory_space=pltpu.SMEM),
            pl.BlockSpec((rows, block), lambda i: (0, i)),
            pl.BlockSpec((rows, width), lambda i: (0, 0)),
        ],
        out_specs=[out, out],
        out_shape=[jax.ShapeDtypeStruct((8, 2 * piece, columns), BF)] * 2,
        compiler_params=PARAMS,
        name="down_grads",
        cost_estimate=pl.CostEstimate(
            flops=2 * rows * width * block, transcendentals=0, bytes_accessed=width * block
        ),
    )(place, activation, down)


def late_grads_kernel(count, place_ref, *refs):
    mixed_refs = refs[:count]
    query_ref = refs[count]
    both_refs = refs[count + 1 : 2 * count + 1]
    vec_ref, mine_ref, sent_ref, turn_ref = refs[2 * count + 1 :]
    step = pl.program_id(0)
    third = (pl.num_programs(0) - 1) // 3
    place = place_ref[0]

    @pl.when(step == 0)
    def _():
        for s in range(count):
            turn_ref[s] = mixed_refs[s][...].T

    @pl.when(step < third)
    def _():
        deal(place, dot(turn_ref[0], query_ref[...], NT), mine_ref, sent_ref)

    @pl.when((step >= third) & (step < 3 * third))
    def _():
        joint = sum(dot(turn_ref[s], both_refs[s][...]) for s in range(count))
        deal(place, joint, mine_ref, sent_ref)

    @pl.when(step == 3 * third)
    def _():
        deal(place, columns_of(vec_ref[...], 0), mine_ref, sent_ref)


def late_grads(place, mixed, query, both, vectors):
    rows, width = mixed[0].shape
    count = len(mixed)
    wide = 256
    third = width // wide
    groups = width // 96

    whole = pl.BlockSpec((rows, width), lambda i: (0, 0))
    out = pl.BlockSpec((groups, 48, wide), lambda i: (0, 0, i))
    return pl.pallas_call(
        functools.partial(late_grads_kernel, count),
        grid=(3 * third + 1,),
        in_specs=[pl.BlockSpec(memory_space=pltpu.SMEM)]
        + [whole] * count
        + [pl.BlockSpec((wide, rows), lambda i: (jnp.clip(i, 0, third - 1), 0))]
        + [pl.BlockSpec((rows, wide), lambda i: (0, jnp.clip(i - third, 0, 2 * third - 1)))] * count
        + [pl.BlockSpec(vectors.shape, lambda i: (0, 0))],
        out_specs=[out, out],
        out_shape=[jax.ShapeDtypeStruct((groups, 48, wide * (3 * third + 1)), BF)] * 2,
        scratch_shapes=[pltpu.VMEM((count, width, rows), BF)],
        compiler_params=PARAMS,
        name="late_grads",
        cost_estimate=pl.CostEstimate(
            flops=2 * rows * width * width * (2 * count + 1),
            transcendentals=0,
            bytes_accessed=2 * rows * width * 4 * count + 12 * width * width,
        ),
    )(place, *mixed, query, *both, vectors)


def block_sums_kernel(counts, dealt, where_ref, *refs):
    total_in = sum(len(group) for group in counts)
    ins, outs = refs[:total_in], refs[total_in:]
    at = 0
    for o, group in enumerate(counts):
        shape = ins[at].shape[-2:] if dealt else outs[o].shape
        value = None
        for use in group:
            term = ins[at][...].astype(F32).reshape(shape)
            if use is not None:
                term = jnp.where(use(pl.program_id(0), where_ref), term, 0.0)
            value = term if value is None else value + term
            at += 1
        if dealt:
            for k, out in enumerate(outs):

                @pl.when(pl.program_id(0) == k)
                def _(out=out, value=value, o=o):
                    out[o] = value.astype(BF)
        else:
            outs[o][...] = value.astype(BF)


def block_sums(where, steps, groups, dealt=False):
    counts = [[term[3] if len(term) > 3 else None for term in terms] for _, terms in groups]
    operands = [term[0] for _, terms in groups for term in terms]
    in_specs = [pl.BlockSpec(term[1], term[2]) for _, terms in groups for term in terms]
    if dealt:
        shape = (len(groups),) + groups[0][0]
        zeros = (0,) * len(shape)
        out_specs = [pl.BlockSpec(shape, lambda i, w: zeros)] * steps
        out_shape = [jax.ShapeDtypeStruct(shape, BF)] * steps
    else:
        out_specs = [pl.BlockSpec(out[1], out[2]) for out, _ in groups]
        out_shape = [jax.ShapeDtypeStruct(out[0], BF) for out, _ in groups]
    return pl.pallas_call(
        functools.partial(block_sums_kernel, counts, dealt),
        grid_spec=pltpu.PrefetchScalarGridSpec(
            num_scalar_prefetch=1, grid=(steps,), in_specs=in_specs, out_specs=out_specs
        ),
        out_shape=out_shape,
        compiler_params=FULL,
        name="block_sums",
        cost_estimate=pl.CostEstimate(flops=1 << 20, transcendentals=0, bytes_accessed=1 << 20),
    )(where, *operands)


class Reduction:
    def __init__(self, where, terms, by_columns):
        self.where = where
        self.terms = terms
        self.by_columns = by_columns
        self.depth, self.columns = terms[0].shape[3:]
        self.steps = 4 if by_columns else 2
        if by_columns:
            self.columns //= 2

    def at(self, part, x, z, y, sizes):
        block = sizes + (self.depth, self.columns)
        column = part if self.by_columns else 0
        shift = 0 if self.by_columns else 2 * part // sizes[1]

        def index(i, w):
            return (x(w), z(i, w) + shift, y(w), 0, column)

        return [(t, block, index) for t in self.terms]

    def one(self):
        n, tail = self.steps, (self.depth, self.columns)
        ahead = lambda i, w: i
        sent = block_sums(
            self.where,
            n // 2,
            [
                (
                    ((n, 2) + tail, (2, 2) + tail, lambda i, w: (i, 0, 0, 0)),
                    self.at(0, lambda w: 1 - w[0], ahead, lambda w: 0, (1, 2, 2)),
                ),
                (
                    ((2, n) + tail, (2, 2) + tail, lambda i, w: (0, i, 0, 0)),
                    self.at(1, lambda w: 0, ahead, lambda w: 1 - w[1], (2, 2, 1)),
                ),
            ],
        )
        return list(sent)

    def trade_one(self, sent):
        self.got_one = [swap(sent[0], "lat", 1), swap(sent[1], "grp", 2)]

    def two(self):
        n, tail = self.steps, (self.depth, self.columns)
        ahead = lambda i, w: i
        out = ((n,) + tail, (2,) + tail, lambda i, w: (i, 0, 0))
        sent = block_sums(
            self.where,
            n // 2,
            [
                (
                    out,
                    self.at(0, lambda w: w[0], ahead, lambda w: 1 - w[1], (1, 2, 1))
                    + [(self.got_one[0], (2, 1) + tail, lambda i, w: (i, 1 - w[1], 0, 0))],
                ),
                (
                    out,
                    self.at(1, lambda w: 1 - w[0], ahead, lambda w: w[1], (1, 2, 1))
                    + [(self.got_one[1], (1, 2) + tail, lambda i, w: (1 - w[0], i, 0, 0))],
                ),
            ],
        )
        return list(sent)

    def trade_two(self, sent):
        self.got_two = [swap(sent[0], "grp", 2), swap(sent[1], "lat", 1)]

    def quarters(self):
        tail = (self.depth, self.columns)
        x = lambda w: w[0]
        y = lambda w: w[1]
        if self.by_columns:
            place = lambda i, w: w[2] ^ i
            groups = []
            for part in (0, 1):
                terms = self.at(part, x, place, y, (1, 1, 1))
                if part == 0:
                    one = lambda i, w: (w[2] ^ i, w[1], 0, 0)
                else:
                    one = lambda i, w: (w[0], w[2] ^ i, 0, 0)
                terms.append((self.got_one[part], (1, 1) + tail, one))
                terms.append((self.got_two[part], (1,) + tail, lambda i, w: (w[2] ^ i, 0, 0)))
                groups.append((tail, terms))
        else:
            low = lambda i, w: jnp.minimum(w[2] ^ i, 1)
            high = lambda i, w: jnp.maximum((w[2] ^ i) - 2, 0)
            first = lambda i, w: (w[2] ^ i) < 2
            second = lambda i, w: (w[2] ^ i) >= 2
            terms = self.at(0, x, lambda i, w: w[2] ^ i, y, (1, 1, 1))
            pair = (1, 1) + tail
            one = (1,) + tail
            terms += [
                (self.got_one[0], pair, lambda i, w: (low(i, w), w[1], 0, 0), first),
                (self.got_one[1], pair, lambda i, w: (w[0], high(i, w), 0, 0), second),
                (self.got_two[0], one, lambda i, w: (low(i, w), 0, 0), first),
                (self.got_two[1], one, lambda i, w: (high(i, w), 0, 0), second),
            ]
            groups = [(tail, terms)]
        return list(block_sums(self.where, 4, groups, True))


def early_unpack_kernel(place_ref, *refs):
    ins = refs[:4]
    down_ref, up_ref, out_ref, gate_ref, head_ref, gain_ref, bias_ref, bd_ref, bup_ref, misc_ref = refs[4:]
    width = down_ref.shape[1]
    hidden = up_ref.shape[1]
    for source, (c, y) in zip(ins, ((0, 0), (0, 1), (1, 0), (1, 1))):
        slot = jnp.bitwise_xor(place_ref[0], c) * 2 + jnp.bitwise_xor(place_ref[1], y)
        one = source[0].astype(F32)
        two = source[1].astype(F32)
        rows = one.shape[0]
        half = one.shape[1]
        for g in range(4):
            span = pl.ds(pl.multiple_of(slot * 4 * rows + g * rows, 8), rows)
            down_ref[span, :] = one[:, g * width : (g + 1) * width]
        span = pl.ds(pl.multiple_of(slot * rows, 8), rows)
        cut = half - 4 * width
        up_ref[span, :cut] = one[:, 4 * width :]
        up_ref[span, cut:] = two[:, : hidden - cut]
        out_ref[span, :] = two[:, hidden - cut : hidden - cut + width]
        misc_ref[span, :] = two[:, hidden - cut + width :]
    turned = misc_ref[...].T
    at = 0
    for ref in (gate_ref, head_ref, gain_ref, bias_ref, bd_ref, bup_ref):
        count = ref.shape[0]
        ref[...] = turned[at : at + count]
        at += count


def early_unpack(place, pieces, width, hidden):
    rows = pieces[0].shape[1]
    vmem = pl.BlockSpec(memory_space=pltpu.VMEM)
    return pl.pallas_call(
        early_unpack_kernel,
        in_specs=[pl.BlockSpec(memory_space=pltpu.SMEM)] + [vmem] * 4,
        out_specs=[vmem] * 9,
        out_shape=[
            jax.ShapeDtypeStruct((16 * rows, width), F32),
            jax.ShapeDtypeStruct((4 * rows, hidden), F32),
            jax.ShapeDtypeStruct((4 * rows, width), F32),
        ]
        + [
            jax.ShapeDtypeStruct((count, 4 * rows), F32)
            for count in (2 * RESULT_FIELDS, RESULT_FIELDS, 1, 1, 1, 4)
        ],
        scratch_shapes=[pltpu.VMEM((4 * rows, 256), F32)],
        compiler_params=PARAMS,
        name="early_unpack",
        cost_estimate=pl.CostEstimate(flops=1 << 20, transcendentals=0, bytes_accessed=1 << 20),
    )(place, *pieces)


def late_unpack_kernel(place_ref, *refs):
    ins = refs[:4]
    main_ref, gain_ref, bias_ref, lead_ref, misc_ref = refs[4:]
    for source, (c, y) in zip(ins, ((0, 0), (0, 1), (1, 0), (1, 1))):
        slot = jnp.bitwise_xor(place_ref[0], c) * 2 + jnp.bitwise_xor(place_ref[1], y)
        value = source[...].astype(F32)
        rows = value.shape[0]
        span = pl.ds(pl.multiple_of(slot * rows, 8), rows)
        main_ref[span, :] = value[:, : main_ref.shape[1]]
        misc_ref[span, :] = value[:, main_ref.shape[1] :]
    turned = misc_ref[...].T
    gain_ref[...] = turned[:1]
    bias_ref[...] = turned[1:2]
    lead_ref[...] = turned[2 : 2 + LEADS]


def late_unpack(place, pieces):
    rows, columns = pieces[0].shape
    vmem = pl.BlockSpec(memory_space=pltpu.VMEM)
    return pl.pallas_call(
        late_unpack_kernel,
        in_specs=[pl.BlockSpec(memory_space=pltpu.SMEM)] + [vmem] * 4,
        out_specs=[vmem] * 4,
        out_shape=[jax.ShapeDtypeStruct((4 * rows, columns - 256), F32)]
        + [jax.ShapeDtypeStruct((count, 4 * rows), F32) for count in (1, 1, LEADS)],
        scratch_shapes=[pltpu.VMEM((4 * rows, 256), F32)],
        compiler_params=PARAMS,
        name="late_unpack",
        cost_estimate=pl.CostEstimate(flops=1 << 20, transcendentals=0, bytes_accessed=1 << 20),
    )(place, *pieces)


def spread(rows, columns):
    pixel = lax.broadcasted_iota(jnp.int32, (rows, columns), 0)
    field = lax.broadcasted_iota(jnp.int32, (rows, columns), 1)
    return ((pixel // TILE_AREA) == field).astype(F32).astype(BF)


def split_two(values):
    high = values.astype(BF)
    return high, (values - high.astype(F32)).astype(BF)


def pixel_sums_kernel(f_ref, s_ref, sum_ref, first_ref, second_ref, field_ref):
    @pl.when(pl.program_id(0) == 0)
    def _():
        field_ref[...] = spread(*field_ref.shape)

    fields = field_ref[...]
    sens = s_ref[...]
    sum_ref[...] = dot(sens, fields)
    for e, out in ((0, first_ref), (1, second_ref)):
        out[...] = dot((sens.astype(F32) * f_ref[e].astype(F32)).astype(BF), fields)


def pixel_sums(forecasts, sensitivity):
    rows, pixels = sensitivity.shape
    block = math.gcd(rows, 64)
    out = pl.BlockSpec((block, 128), lambda i: (i, 0))
    return pl.pallas_call(
        pixel_sums_kernel,
        grid=(rows // block,),
        in_specs=[
            pl.BlockSpec((2, block, pixels), lambda i: (0, i, 0)),
            pl.BlockSpec((block, pixels), lambda i: (i, 0)),
        ],
        out_specs=[out] * 3,
        out_shape=[jax.ShapeDtypeStruct((rows, 128), F32)] * 3,
        scratch_shapes=[pltpu.VMEM((pixels, 128), BF)],
        compiler_params=PARAMS,
        name="pixel_sums",
        cost_estimate=pl.CostEstimate(
            flops=rows * pixels * 128, transcendentals=0, bytes_accessed=rows * pixels
        ),
    )(forecasts, sensitivity)


def blend_kernel(a_ref, b_ref, c_ref, f_ref, out_ref, field_ref):
    @pl.when(pl.program_id(0) == 0)
    def _():
        columns = field_ref.shape[1]
        field = lax.broadcasted_iota(jnp.int32, (256, columns), 0)
        pixel = lax.broadcasted_iota(jnp.int32, (256, columns), 1)
        field_ref[...] = ((pixel // TILE_AREA) == (field % 128)).astype(F32).astype(BF)

    fields = field_ref[...]

    def wide(ref):
        return dot(jnp.concatenate(split_two(ref[...]), axis=1), fields)

    total = wide(a_ref) * f_ref[0].astype(F32) + wide(b_ref) * f_ref[1].astype(F32)
    out_ref[...] = (total + wide(c_ref)).astype(BF)


def blend(first, second, added, forecasts):
    _, rows, pixels = forecasts.shape
    block = math.gcd(rows, 128)
    thin = pl.BlockSpec((block, 128), lambda i: (i, 0))
    return pl.pallas_call(
        blend_kernel,
        grid=(rows // block,),
        in_specs=[thin] * 3 + [pl.BlockSpec((2, block, pixels), lambda i: (0, i, 0))],
        out_specs=pl.BlockSpec((block, pixels), lambda i: (i, 0)),
        out_shape=jax.ShapeDtypeStruct((rows, pixels), BF),
        scratch_shapes=[pltpu.VMEM((256, pixels), BF)],
        compiler_params=PARAMS,
        name="blend",
        cost_estimate=pl.CostEstimate(
            flops=rows * pixels * 128, transcendentals=0, bytes_accessed=rows * pixels
        ),
    )(first, second, added, forecasts)


def swap(values, axis, bit):
    count = lax.axis_size(axis)
    return lax.ppermute(values, axis, [(i, i ^ bit) for i in range(count)])


def add(*terms):
    return sum(t.astype(F32) for t in terms).astype(BF)


def hold(*values):
    return lax.optimization_barrier(values)


def layer_norm(values):
    centred = values - jnp.mean(values, axis=-1, keepdims=True)
    inverse = lax.rsqrt(jnp.mean(centred * centred, axis=-1, keepdims=True) + EPSILON)
    return centred * inverse, inverse


def norm_back(grad_normed, normed, inverse):
    return inverse * (
        grad_normed
        - jnp.mean(grad_normed, axis=-1, keepdims=True)
        - normed * jnp.mean(grad_normed * normed, axis=-1, keepdims=True)
    )


def pad_lanes(values):
    return jnp.pad(values, ((0, 0), (0, 128 - values.shape[1])))


def per_device(
    layer_source_tensor,
    horizon_class,
    field_selector,
    model_predictions,
    loss_sensitivity,
    gain_one,
    shift_one,
    horizon_vectors,
    w_qkv,
    w_out,
    gain_two,
    shift_two,
    w_up,
    b_up,
    w_down,
    b_down,
    w_gate,
    w_bias,
):
    frames, lat_rows, lon_cols, width = layer_source_tensor.shape
    local = lat_rows * lon_cols
    rows = frames * local
    pixels = loss_sensitivity.shape[-1]
    sizes = (lax.axis_size("grp"), lax.axis_size("lat"), lax.axis_size("lon"))
    small = sizes == (4, 2, 4) and frames == 1

    source = layer_source_tensor.reshape(frames, local, width)
    place = lax.axis_index("lon")
    edge = (place == 0) | (place == lax.axis_size("lon") - 1)
    send = functools.partial(lax.ppermute, axis_name="lon")
    if small:
        right = send(source, perm=[(0, 1), (1, 2), (2, 3)])
        left = send(source, perm=[(3, 2), (2, 1), (1, 0)])
    else:
        shards = [lax.all_gather(source, "lon", axis=1, tiled=True)]

    forecasts = jnp.transpose(model_predictions.reshape(rows, 2, pixels), (1, 0, 2))
    sensitivity = loss_sensitivity.reshape(rows, pixels)

    onehot = (horizon_class[:, None] == jnp.arange(LEADS, dtype=jnp.int32)[None, :]).astype(F32)
    lead_rows = jnp.dot(onehot, horizon_vectors, precision=HIGH)

    def mixed_of(values):
        normed, _ = layer_norm(values.astype(F32))
        return (normed * gain_one + shift_one + lead_rows[:, None, :]).astype(BF)

    wq = w_qkv[:, :width]
    wkv = w_qkv[:, width:]

    def keys_of(values):
        return dot(values.reshape(-1, width), wkv).astype(BF).reshape(frames, -1, 2 * width)

    if small:

        def flat(values):
            return values.reshape(rows, width)

        def shard_of(flag, yes, no):
            m, kv, x = project(
                flag.astype(jnp.int32)[None],
                [flat(yes), flat(no)],
                gain_one,
                shift_one,
                lead_rows,
                w_qkv,
            )
            return m, kv[None], x[None]

        mixed_own, own_kv, queries = project(
            None, [flat(source)], gain_one, shift_one, lead_rows, w_qkv
        )
        queries = queries[None]
        mixed = [mixed_own]
        key_value = [own_kv[None]]
        right, left, forecasts, queries, key_value[0] = hold(
            right, left, forecasts, queries, key_value[0]
        )
        right_two = send(right, perm=[(1, 2), (2, 3)])
        left_two = send(left, perm=[(2, 1), (1, 0)])
        sums = pixel_sums(forecasts, sensitivity)
        m, kv, near = shard_of(place == 0, left, right)
        mixed.append(m)
        right_two, left_two, kv, *sums = hold(right_two, left_two, kv, *sums)
        key_value.append(kv)
        two = right_two + left_two
        two, middle = hold(two, left)
        three = send(two, perm=[(2, 3), (1, 0)])
        m, kv, middle = shard_of(edge, two, middle)
        mixed.append(m)
        key_value.append(kv)
        state = attend(queries, key_value, None, False)
        three, *state = hold(three, *state)
        m, kv, far = shard_of(edge, three, two)
        mixed.append(m)
        key_value.append(kv)
        attended, logs = attend(queries, key_value[3:], state, True)
        shards = [source, near, middle, far]
    else:
        mixed_own = mixed_of(source)
        queries = dot(mixed_own.reshape(rows, width), wq).astype(BF)
        queries = queries.reshape(frames, local, width)
        sums = pixel_sums(forecasts, sensitivity)
        mixed = [mixed_of(shards[0])]
        key_value = [keys_of(mixed[0])]
        attended, logs = attend(queries, key_value, None, True)
    inputs = source.reshape(rows, width)
    attended_low = attended.reshape(rows, width)
    both = w_gate.T
    head_rows = jnp.concatenate(
        [
            jnp.pad(m, ((0, 128 - RESULT_FIELDS), (0, 0)))
            for m in (both[:RESULT_FIELDS], both[RESULT_FIELDS:], w_bias.T)
        ]
    )
    mask = pad_lanes(field_selector.astype(F32))[:, None]
    (
        hidden_low,
        activation_low,
        up_low,
        down_low,
        final_low,
        heads_low,
        attn_low,
        grad_residual,
        grad_attended,
        *blending,
        early_vectors,
        grad_bup,
    ) = between(
        inputs,
        attended_low,
        w_out,
        w_up,
        w_down,
        head_rows,
        gain_two,
        shift_two,
        b_up,
        b_down,
        mask,
        sums,
        local,
    )
    grad_attended = grad_attended.reshape(frames, local, width)
    fields = 3 * RESULT_FIELDS
    heads_low = jnp.concatenate(
        [heads_low[:, g * 128 : g * 128 + RESULT_FIELDS] for g in range(3)], axis=1
    )
    inputs = inputs.astype(F32)
    normed_one, inverse_one = layer_norm(inputs)

    def input_gradient(grad_mixed):
        return grad_residual + norm_back(
            grad_mixed.reshape(rows, width) * gain_one, normed_one, inverse_one
        )

    def back(shard, place, before):
        return attend_back(queries, grad_attended, attended, logs, shard, w_qkv, place, before)

    nothing = jnp.zeros((frames, width, local), F32)

    def late_vectors(sums):
        gain_column = sum(jnp.sum(s[:, 0], axis=0) for s in sums)
        column = sum(s[:, 1] for s in sums)
        lead = jnp.dot(onehot.T, column, precision=HIGH)
        zeros = jnp.zeros((6, width), F32)
        return jnp.concatenate((gain_column[None], jnp.sum(column, axis=0)[None], lead, zeros))

    if small:
        bup_rows = jnp.swapaxes(grad_bup.reshape(8, 4, -1), 0, 1).reshape(4, width)
        early_vectors = jnp.concatenate(
            (early_vectors, bup_rows, jnp.zeros((1, width), F32))
        )
        core = (lax.axis_index("grp") % 2).astype(jnp.int32)[None]
        where = jnp.stack(
            (lax.axis_index("lat"), lax.axis_index("grp") // 2, lax.axis_index("lon"))
        ).astype(jnp.int32)
        hidden = w_up.shape[1]
        mine, sent = down_grads(core, activation_low, down_low, 2 * hidden + width + 256)
        mine, sent = early_grads(
            core,
            hidden_low,
            attended_low,
            final_low,
            up_low,
            attn_low,
            jnp.pad(heads_low, ((0, 0), (0, 256 - fields))),
            early_vectors,
            mine,
            sent,
        )
        grad_attended, sent = hold(grad_attended, sent)
        got = swap(sent, "grp", 1)

        grad_query, dkv3, far, sums3 = back(key_value[3], shards[3], nothing)
        early = Reduction(where, [t.reshape(2, 4, 2, 24, -1) for t in (mine, got)], True)
        grad_query, far, *sent = hold(grad_query, far, *early.one())
        got = send(far, perm=[(0, 1), (3, 2)])
        early.trade_one(sent)

        grad_query, dkv2, middle, sums2 = back(key_value[2], shards[2], grad_query)
        value = jnp.where(edge, middle, add(got, far))
        grad_query, value = hold(grad_query, value)
        right = send(value, perm=[(0, 1), (1, 2)])
        left = send(value, perm=[(3, 2), (2, 1)])

        grad_query, dkv1, near, sums1 = back(key_value[1], shards[1], grad_query)
        forth = jnp.where(place == 0, near, add(right, middle))
        back_value = add(left, near)
        grad_query, forth, back_value, *sent = hold(
            grad_query, forth, back_value, *early.two()
        )
        right = send(forth, perm=[(0, 1), (1, 2), (2, 3)])
        left = send(back_value, perm=[(3, 2), (2, 1), (1, 0)])
        early.trade_two(sent)

        grad_query, dkv0, own, sums0, right, left, *early.got_two = hold(
            *back(key_value[0], shards[0], grad_query), right, left, *early.got_two
        )
        query_low, query_term, query_sums = query_back(grad_query, w_qkv, source)
        vectors = late_vectors([sums0, sums1, sums2, sums3, query_sums])
        late_mine, late_sent = late_grads(
            core,
            [m.reshape(rows, width) for m in mixed],
            query_low.reshape(width, rows),
            [d.reshape(rows, 2 * width) for d in (dkv0, dkv1, dkv2, dkv3)],
            vectors,
        )
        late_mine, late_sent, *early.got_two, own = hold(
            late_mine, late_sent, *early.got_two, own
        )
        got = swap(late_sent, "grp", 1)
        got, *parts = hold(got, *early.quarters())
        late = Reduction(where, [t.reshape(2, 4, 2, 24, -1) for t in (late_mine, got)], False)
        *sent, one, two, three = hold(*late.one(), *blending)
        late.trade_one(sent)
        early = [parts[0]] + [swap(parts[k], "lon", k) for k in (1, 2, 3)]
        blended = blend(one, two, three, forecasts)
        *late.got_one, blended = hold(*late.got_one, blended)
        *sent, own, early[0] = hold(*late.two(), own, early[0])
        late.trade_two(sent)
        grad_input = input_gradient(
            own.astype(F32) + query_term + right.astype(F32) + left.astype(F32)
        )
        *late.got_two, grad_input = hold(*late.got_two, grad_input)
        early[0], *parts = hold(early[0], *late.quarters())
        late = [parts[0]] + [swap(parts[k], "lon", k) for k in (1, 2, 3)]
        late[1], late[2], early[0] = hold(late[1], late[2], early[0])
        late = add(*[part[0] for part in late])
        late_y = swap(late, "grp", 2)
        late_c = swap(late, "grp", 1)
        early = add(*early)
        early_y = swap(early, "grp", 2)
        early_c = swap(early, "grp", 1)
        early_y, early_c, early, late_y, late_c, late = hold(
            early_y, early_c, early, late_y, late_c, late
        )
        early_yc = swap(early_y, "grp", 1)
        late_yc = swap(late_y, "grp", 1)
        place_two = jnp.stack((lax.axis_index("grp") % 2, lax.axis_index("grp") // 2))
        place_two = place_two.astype(jnp.int32)
        down_sum, up_sum, out_sum, gate_sum, head_sum, *early, bup_sum = early_unpack(
            place_two, [early, early_y, early_c, early_yc], width, hidden
        )
        late_yc, gate_sum = hold(late_yc, gate_sum)
        qkv_sum, *late, lead_sum = late_unpack(place_two, [late, late_y, late_c, late_yc])
        early = [e.reshape(-1) for e in early]
        late = [e.reshape(-1) for e in late]
        bup_sum = bup_sum.reshape(-1)
        gate_sum = gate_sum.T
        head_sum = head_sum.T
    else:
        blended = blend(*blending, forecasts)
        grad_query, dkv, term, sums = back(key_value[0], shards[0], nothing)
        query_low, query_term, query_sums = query_back(grad_query, w_qkv, source)
        grad_input = input_gradient(
            query_term + lax.psum_scatter(term.astype(F32), "lon", scatter_dimension=1, tiled=True)
        )

        def total_of(values, dim=0):
            share = lax.psum_scatter(values, ("lat", "lon"), scatter_dimension=dim, tiled=True)
            return lax.psum(share, "grp")

        flat = mixed[0].reshape(-1, width)
        qkv_sum = total_of(
            jnp.concatenate(
                (
                    jnp.einsum("frd,fer->de", mixed_own, query_low, preferred_element_type=F32),
                    dot(flat, dkv.reshape(-1, 2 * width), TN),
                ),
                axis=1,
            )
        )
        up_sum = total_of(dot(hidden_low, up_low, TN))
        out_sum = total_of(dot(attended_low, attn_low, TN))
        down_sum = total_of(dot(activation_low, down_low, TN))
        heads = total_of(dot(final_low, heads_low, TN))
        late = total_of(late_vectors([sums, query_sums])[: 2 + LEADS], 1)
        lead_sum = late[2:]
        gate_sum = heads[:, : 2 * RESULT_FIELDS]
        head_sum = heads[:, 2 * RESULT_FIELDS :]
        early = total_of(early_vectors, 1)
        bup_sum = total_of(grad_bup[0])

    return (
        blended.reshape(frames, lat_rows, lon_cols, pixels),
        grad_input.reshape(frames, lat_rows, lon_cols, width),
        late[0],
        late[1],
        lead_sum,
        qkv_sum,
        out_sum,
        early[0],
        early[1],
        up_sum,
        bup_sum,
        down_sum,
        early[2],
        gate_sum,
        head_sum,
    )


def solution(mesh):
    frame = ("grp", "lat")
    share = ("lat", "lon")
    image = P(frame, None, "lon", None)
    in_specs = (
        image,
        P(frame),
        P(frame, None),
        P(frame, None, "lon", None, None),
        image,
    ) + (P(),) * 13
    vector = P(share)
    matrix = P(share, None)
    out_specs = (
        image,
        image,
        vector,
        vector,
        P(None, share),
        matrix,
        matrix,
        vector,
        vector,
        matrix,
        vector,
        matrix,
        vector,
        matrix,
        matrix,
    )
    return jax.shard_map(
        per_device, mesh=mesh, in_specs=in_specs, out_specs=out_specs, check_vma=False
    )
```

profile of v0, /device:TPU:0, one launch (start us, length us, event | category | flops | bytes accessed | tf_op | source)
XLA Modules:
  0.0 339.4 jit_solution(9669891719374651753)
XLA Ops:
  0.7 5.1 %collective-permute-start = (bf16[1,512,768]{2,1,0:T(8,128)(2,1)}, bf16[1,512,768]{2,1,0:T(8,128)(2,1)S(1)}, u32[]{:S(2)}, u32[]{:S(2)}) collective-permute-start(bf16[1,512,768]{2,1,0:T(8,128)(2,1)} %bitcast.80), channel_id=1, source_target_pairs={{0,1},{1,2},{2,3},{4,5},{5,6},{6,7},{8,9},{9,10},{10,11},{12,13},{... | collective-permute-start | bytes 2359304 | tf_op jit(solution)/shard_map/ppermute | solution.py:1074
  7.8 8.3 %copy.41 = bf16[1,32,16,2,4416]{4,2,1,3,0:T(8,128)(2,1)} copy(bf16[1,32,16,2,4416]{4,3,2,1,0:T(2,128)(2,1)} %param.21) | data formatting | bytes 18087936 | tf_op args[3]
  16.8 5.8 %project.4 = (bf16[512,768]{1,0:T(8,128)(2,1)}, bf16[512,1536]{1,0:T(8,128)(2,1)}, bf16[512,768]{1,0:T(8,128)(2,1)}) custom-call(bf16[512,768]{1,0:T(8,128)(2,1)} %bitcast.82, f32[768]{0:T(1024)} %refs_3_.5, f32[768]{0:T(1024)} %refs_4_.7, f32[1,768]{1,0:T(1,128)} %fusion.15.refs_3_.refs_5_, bf16[768,2304]{1,0:T(8,128)(2,1)} %w_ref.1, ...), custom_call_target="tpu_custom_call" | custom-call | flops 301989888 | bytes 393216 | tf_op jit(solution)/shard_map/project/pallas_call | solution.py:65
  22.9 4.1 %collective-permute-done.1 = bf16[1,512,768]{2,1,0:T(8,128)(2,1)S(1)} collective-permute-done((bf16[1,512,768]{2,1,0:T(8,128)(2,1)}, bf16[1,512,768]{2,1,0:T(8,128)(2,1)S(1)}, u32[]{:S(2)}, u32[]{:S(2)}) %collective-permute-start.1) | collective-permute-done | bytes 786464 | tf_op jit(solution)/shard_map/ppermute | solution.py:1075
  28.9 10.4 %pixel_sums.1 = (f32[512,128]{1,0:T(8,128)}, f32[512,128]{1,0:T(8,128)}, f32[512,128]{1,0:T(8,128)}) custom-call(bf16[2,512,4416]{2,1,0:T(8,128)(2,1)} %bitcast.78, bf16[512,4416]{1,0:T(8,128)(2,1)} %bitcast.122), custom_call_target="tpu_custom_call" | custom-call | flops 289406976 | bytes 2260992 | tf_op jit(solution)/shard_map/pixel_sums/pallas_call | solution.py:957
  39.3 5.1 %project.5 = (bf16[512,768]{1,0:T(8,128)(2,1)}, bf16[512,1536]{1,0:T(8,128)(2,1)}, bf16[512,768]{1,0:T(8,128)(2,1)}) custom-call(s32[1]{0:T(128)} %bitcast.7.refs_0_, bf16[512,768]{1,0:T(8,128)(2,1)} %bitcast.123, bf16[512,768]{1,0:T(8,128)(2,1)} %bitcast.130, f32[768]{0:T(1024)} %refs_3_.5, f32[768]{0:T(1024)} %refs_4_.7, f32[1,768]{1,0:T(1,128)} %fusion.15.refs_3_.refs_5_, ...), custom_call_target="tpu_custom_call" | custom-call | flops 301989888 | bytes 393216 | tf_op jit(solution)/shard_map/project/pallas_call | solution.py:65
  44.4 5.6 %collective-permute-done.3 = bf16[1,512,768]{2,1,0:T(8,128)(2,1)S(1)} collective-permute-done((bf16[1,512,768]{2,1,0:T(8,128)(2,1)S(1)}, bf16[1,512,768]{2,1,0:T(8,128)(2,1)S(1)}, u32[]{:S(2)}, u32[]{:S(2)}) %collective-permute-start.3) | collective-permute-done | bytes 786464 | tf_op jit(solution)/shard_map/ppermute | solution.py:1121
  53.4 5.1 %project.6 = (bf16[512,768]{1,0:T(8,128)(2,1)}, bf16[512,1536]{1,0:T(8,128)(2,1)}, bf16[512,768]{1,0:T(8,128)(2,1)}) custom-call(s32[1]{0:T(128)} %bitcast.15.refs_0_, bf16[512,768]{1,0:T(8,128)(2,1)} %bitcast.119, bf16[512,768]{1,0:T(8,128)(2,1)} %bitcast.124, f32[768]{0:T(1024)} %refs_3_.5, f32[768]{0:T(1024)} %refs_4_.7, ...), custom_call_target="tpu_custom_call" | custom-call | flops 301989888 | bytes 393216 | tf_op jit(solution)/shard_map/project/pallas_call | solution.py:65
  58.4 18.2 %attend.2 = (f32[1,768,512]{2,1,0:T(8,128)}, f32[1,6,2,512]{3,2,1,0:T(2,128)}) custom-call(bf16[1,512,768]{2,1,0:T(8,128)(2,1)} %bitcast.93, bf16[1,512,1536]{2,1,0:T(8,128)(2,1)} %bitcast.99, bf16[1,512,1536]{2,1,0:T(8,128)(2,1)} %bitcast.103, bf16[1,512,1536]{2,1,0:T(8,128)(2,1)} %bitcast.107, bf16[1,512,1536]{2,1,0:T(8,128)(2,1)} %bitcast.100, ...), custom_call_target="tpu_custom_call" | custom-call | flops 1207959552 | bytes 393216 | tf_op jit(solution)/shard_map/attend/pallas_call | solution.py:137
  77.5 5.1 %project.7 = (bf16[512,768]{1,0:T(8,128)(2,1)}, bf16[512,1536]{1,0:T(8,128)(2,1)}, bf16[512,768]{1,0:T(8,128)(2,1)}) custom-call(s32[1]{0:T(128)} %bitcast.15.refs_0_, bf16[512,768]{1,0:T(8,128)(2,1)} %bitcast.129, bf16[512,768]{1,0:T(8,128)(2,1)} %bitcast.120, f32[768]{0:T(1024)} %refs_3_.5, f32[768]{0:T(1024)} %refs_4_.7, ...), custom_call_target="tpu_custom_call" | custom-call | flops 301989888 | bytes 393216 | tf_op jit(solution)/shard_map/project/pallas_call | solution.py:65
  82.6 9.5 %attend.3 = (bf16[1,512,768]{2,1,0:T(8,128)(2,1)}, f32[1,6,2,512]{3,2,1,0:T(2,128)}) custom-call(bf16[1,512,768]{2,1,0:T(8,128)(2,1)} %bitcast.94, bf16[1,512,1536]{2,1,0:T(8,128)(2,1)} %bitcast.111, bf16[1,512,1536]{2,1,0:T(8,128)(2,1)} %bitcast.112, f32[1,768,512]{2,1,0:T(8,128)} %get-tuple-element.205.refs_3_, f32[1,6,2,512]{3,2,1,0:T(2,128)} %get-tuple-element.206.refs_4_), custom_call_target="tpu_custom_call" | custom-call | flops 402653184 | bytes 393216 | tf_op jit(solution)/shard_map/attend/pallas_call | solution.py:137
  92.1 31.6 %between.1 = (bf16[512,768]{1,0:T(8,128)(2,1)}, bf16[512,3072]{1,0:T(8,128)(2,1)}, bf16[512,3072]{1,0:T(8,128)(2,1)}, bf16[512,768]{1,0:T(8,128)(2,1)}, bf16[512...) custom-call(bf16[512,768]{1,0:T(8,128)(2,1)} %bitcast.83, ...), custom_call_target="tpu_custom_call" | custom-call | flops 1207959552 | bytes 1572864 | tf_op jit(solution)/shard_map/between/pallas_call | solution.py:444
  128.4 8.6 %down_grads.1 = (bf16[8,48,7168]{2,1,0:T(8,128)(2,1)}, bf16[8,48,7168]{2,1,0:T(8,128)(2,1)}) custom-call(s32[1]{0:T(128)} %bitcast.3.place_ref, bf16[512,3072]{1,0:T(8,128)(2,1)} %get-tuple-element.219.act_ref, bf16[512,768]{1,0:T(8,128)(2,1)} %get-tuple-element.220.down_ref), custom_call_target="tpu_custom_call" | custom-call | flops 301989888 | bytes 294912 | tf_op jit(solution)/shard_map/down_grads/pallas_call | solution.py:623
  137.0 10.2 %early_grads.1 = (bf16[8,48,7168]{2,1,0:T(8,128)(2,1)}, bf16[8,48,7168]{2,1,0:T(8,128)(2,1)}) custom-call(s32[1]{0:T(128)} %bitcast.3.place_ref, bf16[512,768]{1,0:T(8,128)(2,1)} %get-tuple-element.212.h_ref, bf16[512,768]{1,0:T(8,128)(2,1)} %bitcast.92, bf16[512,768]{1,0:T(8,128)(2,1)} %get-tuple-element.213.f_ref, ...), custom_call_target="tpu_custom_call", output_to_operand_aliasing={{0}: (8, {}), {1}: (9, {})} | custom-call | flops 3221225472 | bytes 10485760 | tf_op jit(solution)/shard_map/early_grads/pallas_call | solution.py:567
  149.2 15.7 %attend_back.4 = (f32[1,768,512]{2,1,0:T(8,128)}, bf16[1,512,1536]{2,1,0:T(8,128)(2,1)}, bf16[1,512,768]{2,1,0:T(8,128)(2,1)}, f32[1,2,768]{2,1,0:T(2,128)}) custom-call(bf16[1,512,768]{2,1,0:T(8,128)(2,1)} %bitcast.95, bf16[1,512,768]{2,1,0:T(8,128)(2,1)} %bitcast.115, ...), custom_call_target="tpu_custom_call", output_to_operand_aliasing={{0}: (9, {})} | custom-call | flops 805306368 | bytes 393216 | tf_op jit(solution)/shard_map/attend_back/pallas_call | solution.py:252
  164.9 4.6 %block_sums.6 = (bf16[4,2,24,3584]{3,2,1,0:T(8,128)(2,1)}, bf16[2,4,24,3584]{3,2,1,0:T(8,128)(2,1)}) custom-call(s32[3]{0:T(128)} %pad_add_fusion.where_ref, bf16[2,4,2,24,7168]{4,3,2,1,0:T(8,128)(2,1)} %bitcast.72, bf16[2,4,2,24,7168]{4,3,2,1,0:T(8,128)(2,1)} %bitcast.33.refs_1_.refs_3_.refs_4_.refs_5_, bf16[2,4,2,24,7168]{4,3,2,1,0:T(8,128)(2,1)} %bitcast.73, ...), custom_call_target="tpu_custom_call" | custom-call | flops 1048576 | bytes 1048576 | tf_op jit(solution)/shard_map/block_sums/pallas_call | solution.py:734
  169.5 4.6 %collective-permute-start.6 = (bf16[1,512,768]{2,1,0:T(8,128)(2,1)}, bf16[1,512,768]{2,1,0:T(8,128)(2,1)S(1)}, u32[]{:S(2)}, u32[]{:S(2)}) collective-permute-start(bf16[1,512,768]{2,1,0:T(8,128)(2,1)} %get-tuple-element.238), channel_id=1, source_target_pairs={{0,1},{3,2},{4,5},{7,6},{8,9},{11,10},{12,13},{15,14},{16,17},{19,... | collective-permute-start | bytes 2359304 | tf_op jit(solution)/shard_map/ppermute | solution.py:1240
  177.2 15.6 %attend_back.5 = (f32[1,768,512]{2,1,0:T(8,128)}, bf16[1,512,1536]{2,1,0:T(8,128)(2,1)}, bf16[1,512,768]{2,1,0:T(8,128)(2,1)}, f32[1,2,768]{2,1,0:T(2,128)}) custom-call(bf16[1,512,768]{2,1,0:T(8,128)(2,1)} %bitcast.96, bf16[1,512,768]{2,1,0:T(8,128)(2,1)} %bitcast.116, ...), custom_call_target="tpu_custom_call", output_to_operand_aliasing={{0}: (9, {})} | custom-call | flops 805306368 | bytes 393216 | tf_op jit(solution)/shard_map/attend_back/pallas_call | solution.py:252
  195.2 3.1 collective-permute-start.7
  199.8 15.5 %attend_back.6 = (f32[1,768,512]{2,1,0:T(8,128)}, bf16[1,512,1536]{2,1,0:T(8,128)(2,1)}, bf16[1,512,768]{2,1,0:T(8,128)(2,1)}, f32[1,2,768]{2,1,0:T(2,128)}) custom-call(bf16[1,512,768]{2,1,0:T(8,128)(2,1)} %bitcast.97, bf16[1,512,768]{2,1,0:T(8,128)(2,1)} %bitcast.117, ...), custom_call_target="tpu_custom_call", output_to_operand_aliasing={{0}: (9, {})} | custom-call | flops 805306368 | bytes 393216 | tf_op jit(solution)/shard_map/attend_back/pallas_call | solution.py:252
  215.3 3.9 %block_sums.7 = (bf16[4,24,3584]{2,1,0:T(8,128)(2,1)}, bf16[4,24,3584]{2,1,0:T(8,128)(2,1)}) custom-call(s32[3]{0:T(128)} %pad_add_fusion.where_ref, bf16[2,4,2,24,7168]{4,3,2,1,0:T(8,128)(2,1)} %bitcast.74, bf16[2,4,2,24,7168]{4,3,2,1,0:T(8,128)(2,1)} %bitcast.33.refs_1_.refs_3_.refs_4_.refs_5_, bf16[4,2,24,3584]{3,2,1,0:T(8,128)(2,1)} %collective-permute-done.9.refs_2_, ...), custom_call_target="tpu_custom_call" | custom-call | flops 1048576 | bytes 1048576 | tf_op jit(solution)/shard_map/block_sums/pallas_call | solution.py:734
  228.4 15.7 %attend_back.7 = (f32[1,768,512]{2,1,0:T(8,128)}, bf16[1,512,1536]{2,1,0:T(8,128)(2,1)}, bf16[1,512,768]{2,1,0:T(8,128)(2,1)}, f32[1,2,768]{2,1,0:T(2,128)}) custom-call(bf16[1,512,768]{2,1,0:T(8,128)(2,1)} %bitcast.98, bf16[1,512,768]{2,1,0:T(8,128)(2,1)} %bitcast.118, ...), custom_call_target="tpu_custom_call", output_to_operand_aliasing={{0}: (9, {})} | custom-call | flops 805306368 | bytes 393216 | tf_op jit(solution)/shard_map/attend_back/pallas_call | solution.py:252
  244.8 4.4 %query_back.1 = (bf16[1,768,512]{2,1,0:T(8,128)(2,1)}, f32[1,512,768]{2,1,0:T(8,128)}, f32[1,2,768]{2,1,0:T(2,128)}) custom-call(f32[1,768,512]{2,1,0:T(8,128)} %get-tuple-element.256.dq_ref, bf16[768,2304]{1,0:T(8,128)(2,1)} %w_ref.1, bf16[1,512,768]{2,1,0:T(8,128)(2,1)} %bitcast.85), custom_call_target="tpu_custom_call" | custom-call | flops 301989888 | bytes 393216 | tf_op jit(solution)/shard_map/query_back/pallas_call | solution.py:283
  250.8 13.4 %late_grads.1 = (bf16[8,48,2560]{2,1,0:T(8,128)(2,1)}, bf16[8,48,2560]{2,1,0:T(8,128)(2,1)}) custom-call(s32[1]{0:T(128)} %bitcast.3.place_ref, bf16[512,768]{1,0:T(8,128)(2,1)} %get-tuple-element.180.refs_0_, bf16[512,768]{1,0:T(8,128)(2,1)} %get-tuple-element.185.refs_1_, bf16[512,768]{1,0:T(8,128)(2,1)} %get-tuple-element.195.refs_2_, ...), custom_call_target="tpu_custom_call" | custom-call | flops 5435817984 | bytes 19660800 | tf_op jit(solution)/shard_map/late_grads/pallas_call | solution.py:678
  264.3 5.7 %block_sums.8 = (bf16[2,24,3584]{2,1,0:T(8,128)(2,1)}, bf16[2,24,3584]{2,1,0:T(8,128)(2,1)}, bf16[2,24,3584]{2,1,0:T(8,128)(2,1)}, bf16[2,24,3584]{2,1,0:T(8,128)(2,1)}) custom-call(s32[3]{0:T(128)} %pad_add_fusion.where_ref, bf16[2,4,2,24,7168]{4,3,2,1,0:T(8,128)(2,1)} %bitcast.76, bf16[2,4,2,24,7168]{4,3,2,1,0:T(8,128)(2,1)} %bitcast.33.refs_1_.refs_3_.refs_4_.refs_5_, ...), custom_call_target="tpu_custom_call" | custom-call | flops 1048576 | bytes 1048576 | tf_op jit(solution)/shard_map/block_sums/pallas_call | solution.py:734
  270.1 3.2 block_sums.9
  282.4 9.3 %blend.1 = bf16[512,4416]{1,0:T(8,128)(2,1)} custom-call(f32[512,128]{1,0:T(8,128)} %get-tuple-element.288.a_ref, f32[512,128]{1,0:T(8,128)} %get-tuple-element.289.b_ref, f32[512,128]{1,0:T(8,128)} %get-tuple-element.290.c_ref, bf16[2,512,4416]{2,1,0:T(8,128)(2,1)} %bitcast.79), custom_call_target="tpu_custom_call" | custom-call | flops 289406976 | bytes 2260992 | tf_op jit(solution)/shard_map/blend/pallas_call | solution.py:996
  291.7 3.0 block_sums.10
  295.8 3.3 fusion.21
  302.2 4.5 %block_sums.11 = (bf16[1,24,2560]{2,1,0:T(8,128)(2,1)}, bf16[1,24,2560]{2,1,0:T(8,128)(2,1)}, bf16[1,24,2560]{2,1,0:T(8,128)(2,1)}, bf16[1,24,2560]{2,1,0:T(8,128)(2,1)}) custom-call(s32[3]{0:T(128)} %pad_add_fusion.where_ref, bf16[2,4,2,24,2560]{4,3,2,1,0:T(8,128)(2,1)} %bitcast.90, bf16[2,4,2,24,2560]{4,3,2,1,0:T(8,128)(2,1)} %bitcast.43.refs_1_.refs_3_.refs_4_, ...), custom_call_target="tpu_custom_call" | custom-call | flops 1048576 | bytes 1048576 | tf_op jit(solution)/shard_map/block_sums/pallas_call | solution.py:734
  309.7 5.0 %collective-permute-done.20 = bf16[1,24,2560]{2,1,0:T(8,128)(2,1)S(1)} collective-permute-done((bf16[1,24,2560]{2,1,0:T(8,128)(2,1)}, bf16[1,24,2560]{2,1,0:T(8,128)(2,1)S(1)}, u32[]{:S(2)}, u32[]{:S(2)}) %collective-permute-start.20) | collective-permute-done | bytes 122912 | tf_op jit(solution)/shard_map/ppermute | solution.py:1013
  322.8 7.2 %collective-permute-done.28.refs_1_ = bf16[24,2560]{1,0:T(8,128)(2,1)S(1)} collective-permute-done((bf16[24,2560]{1,0:T(8,128)(2,1)S(1)}, bf16[24,2560]{1,0:T(8,128)(2,1)S(1)}, u32[]{:S(2)}, u32[]{:S(2)}) %collective-permute-start.28) | collective-permute-done | bytes 122912 | tf_op jit(solution)/shard_map/ppermute | solution.py:1013
  (166 shorter events, 66.8 us)
Async XLA Ops:
  0.7 22.2 %collective-permute-start = (bf16[1,512,768]{2,1,0:T(8,128)(2,1)}, bf16[1,512,768]{2,1,0:T(8,128)(2,1)S(1)}, u32[]{:S(2)}, u32[]{:S(2)}) collective-permute-start(bf16[1,512,768]{2,1,0:T(8,128)(2,1)} %bitcast.80), channel_id=1, source_target_pairs={{0,1},{1,2},{2,3},{4,5},{5,6},{6,7},{8,9},{9,10},{10,11},{12,13},{... | collective-permute-start | bytes 2359304 | tf_op jit(solution)/shard_map/ppermute | solution.py:1074
  5.8 21.1 %collective-permute-start.1 = (bf16[1,512,768]{2,1,0:T(8,128)(2,1)}, bf16[1,512,768]{2,1,0:T(8,128)(2,1)S(1)}, u32[]{:S(2)}, u32[]{:S(2)}) collective-permute-start(bf16[1,512,768]{2,1,0:T(8,128)(2,1)} %bitcast.81), channel_id=1, source_target_pairs={{3,2},{2,1},{1,0},{7,6},{6,5},{5,4},{11,10},{10,9},{9,8},{15,14},{... | collective-permute-start | bytes 2359304 | tf_op jit(solution)/shard_map/ppermute | solution.py:1075
  26.9 17.5 %collective-permute-start.2 = (bf16[1,512,768]{2,1,0:T(8,128)(2,1)S(1)}, bf16[1,512,768]{2,1,0:T(8,128)(2,1)S(1)}, u32[]{:S(2)}, u32[]{:S(2)}) collective-permute-start(bf16[1,512,768]{2,1,0:T(8,128)(2,1)S(1)} %collective-permute-done), channel_id=1, source_target_pairs={{1,2},{2,3},{5,6},{6,7},{9,10},{10,11},{13,14},{14,15},{17,18},{18... | collective-permute-start | bytes 2359304 | tf_op jit(solution)/shard_map/ppermute | solution.py:1120
  27.6 22.4 %collective-permute-start.3 = (bf16[1,512,768]{2,1,0:T(8,128)(2,1)S(1)}, bf16[1,512,768]{2,1,0:T(8,128)(2,1)S(1)}, u32[]{:S(2)}, u32[]{:S(2)}) collective-permute-start(bf16[1,512,768]{2,1,0:T(8,128)(2,1)S(1)} %collective-permute-done.1), channel_id=1, source_target_pairs={{2,1},{1,0},{6,5},{5,4},{10,9},{9,8},{14,13},{13,12},{18,17},{17,1... | collective-permute-start | bytes 2359304 | tf_op jit(solution)/shard_map/ppermute | solution.py:1121
  50.2 26.4 %collective-permute-start.4 = (bf16[1,512,768]{2,1,0:T(8,128)(2,1)S(1)}, bf16[1,512,768]{2,1,0:T(8,128)(2,1)S(1)}, u32[]{:S(2)}, u32[]{:S(2)}) collective-permute-start(bf16[1,512,768]{2,1,0:T(8,128)(2,1)S(1)} %add.184), channel_id=1, source_target_pairs={{2,3},{1,0},{6,7},{5,4},{10,11},{9,8},{14,15},{13,12},{18,19},{17,... | collective-permute-start | bytes 2359304 | tf_op jit(solution)/shard_map/ppermute | solution.py:1129
  147.3 17.6 %collective-permute-start.5 = (bf16[8,48,7168]{2,1,0:T(8,128)(2,1)}, bf16[8,48,7168]{2,1,0:T(8,128)(2,1)}, u32[]{:S(2)}, u32[]{:S(2)}) collective-permute-start(bf16[8,48,7168]{2,1,0:T(8,128)(2,1)} %get-tuple-element.232), channel_id=1, source_target_pairs={{0,8},{8,0},{16,24},{24,16},{1,9},{9,1},{17,25},{25,17},{2,10},{10... | collective-permute-start | bytes 16515080 | tf_op jit(solution)/shard_map/ppermute | solution.py:1013
  169.5 23.3 %collective-permute-start.6 = (bf16[1,512,768]{2,1,0:T(8,128)(2,1)}, bf16[1,512,768]{2,1,0:T(8,128)(2,1)S(1)}, u32[]{:S(2)}, u32[]{:S(2)}) collective-permute-start(bf16[1,512,768]{2,1,0:T(8,128)(2,1)} %get-tuple-element.238), channel_id=1, source_target_pairs={{0,1},{3,2},{4,5},{7,6},{8,9},{11,10},{12,13},{15,14},{16,17},{19,... | collective-permute-start | bytes 2359304 | tf_op jit(solution)/shard_map/ppermute | solution.py:1240
  174.1 41.2 %collective-permute-start.9 = (bf16[4,2,24,3584]{3,2,1,0:T(8,128)(2,1)}, bf16[4,2,24,3584]{3,2,1,0:T(8,128)(2,1)}, u32[]{:S(2)}, u32[]{:S(2)}) collective-permute-start(bf16[4,2,24,3584]{3,2,1,0:T(8,128)(2,1)} %get-tuple-element.243), channel_id=1, source_target_pairs={{0,4},{4,0},{1,5},{5,1},{2,6},{6,2},{3,7},{7,3},{8,12},{12,8},{9,1... | collective-permute-start | bytes 4128776 | tf_op jit(solution)/shard_map/ppermute | solution.py:1013
  175.7 39.6 %collective-permute-start.10 = (bf16[2,4,24,3584]{3,2,1,0:T(8,128)(2,1)}, bf16[2,4,24,3584]{3,2,1,0:T(8,128)(2,1)}, u32[]{:S(2)}, u32[]{:S(2)}) collective-permute-start(bf16[2,4,24,3584]{3,2,1,0:T(8,128)(2,1)} %get-tuple-element.244), channel_id=1, source_target_pairs={{0,16},{8,24},{16,0},{24,8},{1,17},{9,25},{17,1},{25,9},{2,18},{10... | collective-permute-start | bytes 4128776 | tf_op jit(solution)/shard_map/ppermute | solution.py:1013
  195.2 24.0 %collective-permute-start.7 = (bf16[1,512,768]{2,1,0:T(8,128)(2,1)}, bf16[1,512,768]{2,1,0:T(8,128)(2,1)}, u32[]{:S(2)}, u32[]{:S(2)}) collective-permute-start(bf16[1,512,768]{2,1,0:T(8,128)(2,1)} %fusion.5), channel_id=1, source_target_pairs={{0,1},{1,2},{4,5},{5,6},{8,9},{9,10},{12,13},{13,14},{16,17},{17,1... | collective-permute-start | bytes 2359304 | tf_op jit(solution)/shard_map/ppermute | solution.py:1246
  198.3 22.9 %collective-permute-start.8 = (bf16[1,512,768]{2,1,0:T(8,128)(2,1)}, bf16[1,512,768]{2,1,0:T(8,128)(2,1)}, u32[]{:S(2)}, u32[]{:S(2)}) collective-permute-start(bf16[1,512,768]{2,1,0:T(8,128)(2,1)} %fusion.5), channel_id=1, source_target_pairs={{3,2},{2,1},{7,6},{6,5},{11,10},{10,9},{15,14},{14,13},{19,18},{18... | collective-permute-start | bytes 2359304 | tf_op jit(solution)/shard_map/ppermute | solution.py:1247
  222.6 21.6 %collective-permute-start.11 = (bf16[1,512,768]{2,1,0:T(8,128)(2,1)S(1)}, bf16[1,512,768]{2,1,0:T(8,128)(2,1)S(1)}, u32[]{:S(2)}, u32[]{:S(2)}) collective-permute-start(bf16[1,512,768]{2,1,0:T(8,128)(2,1)S(1)} %fusion.6), channel_id=1, source_target_pairs={{0,1},{1,2},{2,3},{4,5},{5,6},{6,7},{8,9},{9,10},{10,11},{12,13},{... | collective-permute-start | bytes 2359304 | tf_op jit(solution)/shard_map/ppermute | solution.py:1255
  223.9 20.8 %collective-permute-start.12 = (bf16[1,512,768]{2,1,0:T(8,128)(2,1)S(1)}, bf16[1,512,768]{2,1,0:T(8,128)(2,1)S(1)}, u32[]{:S(2)}, u32[]{:S(2)}) collective-permute-start(bf16[1,512,768]{2,1,0:T(8,128)(2,1)S(1)} %add_convert_fusion), channel_id=1, source_target_pairs={{3,2},{2,1},{1,0},{7,6},{6,5},{5,4},{11,10},{10,9},{9,8},{15,14},{... | collective-permute-start | bytes 2359304 | tf_op jit(solution)/shard_map/ppermute | solution.py:1256
  225.2 18.9 %collective-permute-start.13 = (bf16[4,24,3584]{2,1,0:T(8,128)(2,1)}, bf16[4,24,3584]{2,1,0:T(8,128)(2,1)S(1)}, u32[]{:S(2)}, u32[]{:S(2)}) collective-permute-start(bf16[4,24,3584]{2,1,0:T(8,128)(2,1)} %get-tuple-element.254), channel_id=1, source_target_pairs={{0,16},{8,24},{16,0},{24,8},{1,17},{9,25},{17,1},{25,9},{2,18},{10... | collective-permute-start | bytes 2064392 | tf_op jit(solution)/shard_map/ppermute | solution.py:1013
  226.8 17.3 %collective-permute-start.14 = (bf16[4,24,3584]{2,1,0:T(8,128)(2,1)}, bf16[4,24,3584]{2,1,0:T(8,128)(2,1)}, u32[]{:S(2)}, u32[]{:S(2)}) collective-permute-start(bf16[4,24,3584]{2,1,0:T(8,128)(2,1)} %get-tuple-element.255), channel_id=1, source_target_pairs={{0,4},{4,0},{1,5},{5,1},{2,6},{6,2},{3,7},{7,3},{8,12},{12,8},{9,1... | collective-permute-start | bytes 2064392 | tf_op jit(solution)/shard_map/ppermute | solution.py:1013
  264.1 5.9 %collective-permute-start.15 = (bf16[8,48,2560]{2,1,0:T(8,128)(2,1)}, bf16[8,48,2560]{2,1,0:T(8,128)(2,1)}, u32[]{:S(2)}, u32[]{:S(2)}) collective-permute-start(bf16[8,48,2560]{2,1,0:T(8,128)(2,1)} %get-tuple-element.273), channel_id=1, source_target_pairs={{0,8},{8,0},{16,24},{24,16},{1,9},{9,1},{17,25},{25,17},{2,10},{10... | collective-permute-start | bytes 5898248 | tf_op jit(solution)/shard_map/ppermute | solution.py:1013
  273.3 18.4 %collective-permute-start.16 = (bf16[2,2,24,2560]{3,2,1,0:T(8,128)(2,1)}, bf16[2,2,24,2560]{3,2,1,0:T(8,128)(2,1)}, u32[]{:S(2)}, u32[]{:S(2)}) collective-permute-start(bf16[2,2,24,2560]{3,2,1,0:T(8,128)(2,1)} %get-tuple-element.286), channel_id=1, source_target_pairs={{0,4},{4,0},{1,5},{5,1},{2,6},{6,2},{3,7},{7,3},{8,12},{12,8},{9,1... | collective-permute-start | bytes 1474568 | tf_op jit(solution)/shard_map/ppermute | solution.py:1013
  274.8 16.9 %collective-permute-start.17 = (bf16[2,2,24,2560]{3,2,1,0:T(8,128)(2,1)}, bf16[2,2,24,2560]{3,2,1,0:T(8,128)(2,1)}, u32[]{:S(2)}, u32[]{:S(2)}) collective-permute-start(bf16[2,2,24,2560]{3,2,1,0:T(8,128)(2,1)} %get-tuple-element.287), channel_id=1, source_target_pairs={{0,16},{8,24},{16,0},{24,8},{1,17},{9,25},{17,1},{25,9},{2,18},{10... | collective-permute-start | bytes 1474568 | tf_op jit(solution)/shard_map/ppermute | solution.py:1013
  278.0 38.6 %collective-permute-start.24 = (bf16[2,24,3584]{2,1,0:T(8,128)(2,1)}, bf16[2,24,3584]{2,1,0:T(8,128)(2,1)}, u32[]{:S(2)}, u32[]{:S(2)}) collective-permute-start(bf16[2,24,3584]{2,1,0:T(8,128)(2,1)} %get-tuple-element.319), channel_id=1, source_target_pairs={{0,3},{1,2},{2,1},{3,0},{4,7},{5,6},{6,5},{7,4},{8,11},{9,10},{10,... | collective-permute-start | bytes 1032200 | tf_op jit(solution)/shard_map/ppermute | solution.py:1013
  279.4 37.2 %collective-permute-start.23 = (bf16[2,24,3584]{2,1,0:T(8,128)(2,1)}, bf16[2,24,3584]{2,1,0:T(8,128)(2,1)}, u32[]{:S(2)}, u32[]{:S(2)}) collective-permute-start(bf16[2,24,3584]{2,1,0:T(8,128)(2,1)} %get-tuple-element.318), channel_id=1, source_target_pairs={{0,2},{1,3},{2,0},{3,1},{4,6},{5,7},{6,4},{7,5},{8,10},{9,11},{10,... | collective-permute-start | bytes 1032200 | tf_op jit(solution)/shard_map/ppermute | solution.py:1013
  281.0 35.6 %collective-permute-start.22 = (bf16[2,24,3584]{2,1,0:T(8,128)(2,1)}, bf16[2,24,3584]{2,1,0:T(8,128)(2,1)}, u32[]{:S(2)}, u32[]{:S(2)}) collective-permute-start(bf16[2,24,3584]{2,1,0:T(8,128)(2,1)} %get-tuple-element.317), channel_id=1, source_target_pairs={{0,1},{1,0},{2,3},{3,2},{4,5},{5,4},{6,7},{7,6},{8,9},{9,8},{10,11... | collective-permute-start | bytes 1032200 | tf_op jit(solution)/shard_map/ppermute | solution.py:1013
  294.7 7.3 %collective-permute-start.18 = (bf16[2,24,2560]{2,1,0:T(8,128)(2,1)}, bf16[2,24,2560]{2,1,0:T(8,128)(2,1)}, u32[]{:S(2)}, u32[]{:S(2)}) collective-permute-start(bf16[2,24,2560]{2,1,0:T(8,128)(2,1)} %get-tuple-element.298), channel_id=1, source_target_pairs={{0,16},{8,24},{16,0},{24,8},{1,17},{9,25},{17,1},{25,9},{2,18},{10... | collective-permute-start | bytes 737288 | tf_op jit(solution)/shard_map/ppermute | solution.py:1013
  295.2 7.0 %collective-permute-start.19 = (bf16[2,24,2560]{2,1,0:T(8,128)(2,1)}, bf16[2,24,2560]{2,1,0:T(8,128)(2,1)}, u32[]{:S(2)}, u32[]{:S(2)}) collective-permute-start(bf16[2,24,2560]{2,1,0:T(8,128)(2,1)} %get-tuple-element.299), channel_id=1, source_target_pairs={{0,4},{4,0},{1,5},{5,1},{2,6},{6,2},{3,7},{7,3},{8,12},{12,8},{9,1... | collective-permute-start | bytes 737288 | tf_op jit(solution)/shard_map/ppermute | solution.py:1013
  306.7 8.0 %collective-permute-start.20 = (bf16[1,24,2560]{2,1,0:T(8,128)(2,1)}, bf16[1,24,2560]{2,1,0:T(8,128)(2,1)S(1)}, u32[]{:S(2)}, u32[]{:S(2)}) collective-permute-start(bf16[1,24,2560]{2,1,0:T(8,128)(2,1)} %get-tuple-element.313), channel_id=1, source_target_pairs={{0,1},{1,0},{2,3},{3,2},{4,5},{5,4},{6,7},{7,6},{8,9},{9,8},{10,11... | collective-permute-start | bytes 368648 | tf_op jit(solution)/shard_map/ppermute | solution.py:1013
  307.7 8.9 %collective-permute-start.21 = (bf16[1,24,2560]{2,1,0:T(8,128)(2,1)}, bf16[1,24,2560]{2,1,0:T(8,128)(2,1)S(1)}, u32[]{:S(2)}, u32[]{:S(2)}) collective-permute-start(bf16[1,24,2560]{2,1,0:T(8,128)(2,1)} %get-tuple-element.314), channel_id=1, source_target_pairs={{0,2},{1,3},{2,0},{3,1},{4,6},{5,7},{6,4},{7,5},{8,10},{9,11},{10,... | collective-permute-start | bytes 368648 | tf_op jit(solution)/shard_map/ppermute | solution.py:1013
  314.7 7.4 %collective-permute-start.27 = (bf16[1,24,2560]{2,1,0:T(8,128)(2,1)}, bf16[1,24,2560]{2,1,0:T(8,128)(2,1)S(1)}, u32[]{:S(2)}, u32[]{:S(2)}) collective-permute-start(bf16[1,24,2560]{2,1,0:T(8,128)(2,1)} %get-tuple-element.323), channel_id=1, source_target_pairs={{0,3},{1,2},{2,1},{3,0},{4,7},{5,6},{6,5},{7,4},{8,11},{9,10},{10,... | collective-permute-start | bytes 368648 | tf_op jit(solution)/shard_map/ppermute | solution.py:1013
  318.1 11.9 %collective-permute-start.25 = (bf16[2,24,3584]{2,1,0:T(8,128)(2,1)S(1)}, bf16[2,24,3584]{2,1,0:T(8,128)(2,1)S(1)}, u32[]{:S(2)}, u32[]{:S(2)}) collective-permute-start(bf16[2,24,3584]{2,1,0:T(8,128)(2,1)S(1)} %add_convert_fusion.3.refs_0_), channel_id=1, source_target_pairs={{0,16},{8,24},{16,0},{24,8},{1,17},{9,25},{17,1},{25,9},{2,18},{10... | collective-permute-start | bytes 1032200 | tf_op jit(solution)/shard_map/ppermute | solution.py:1013
  319.5 10.5 %collective-permute-start.26 = (bf16[2,24,3584]{2,1,0:T(8,128)(2,1)S(1)}, bf16[2,24,3584]{2,1,0:T(8,128)(2,1)S(1)}, u32[]{:S(2)}, u32[]{:S(2)}) collective-permute-start(bf16[2,24,3584]{2,1,0:T(8,128)(2,1)S(1)} %add_convert_fusion.3.refs_0_), channel_id=1, source_target_pairs={{0,8},{8,0},{16,24},{24,16},{1,9},{9,1},{17,25},{25,17},{2,10},{10... | collective-permute-start | bytes 1032200 | tf_op jit(solution)/shard_map/ppermute | solution.py:1013
  322.1 7.8 %collective-permute-start.28 = (bf16[24,2560]{1,0:T(8,128)(2,1)S(1)}, bf16[24,2560]{1,0:T(8,128)(2,1)S(1)}, u32[]{:S(2)}, u32[]{:S(2)}) collective-permute-start(bf16[24,2560]{1,0:T(8,128)(2,1)S(1)} %fusion.14.refs_0_), channel_id=1, source_target_pairs={{0,16},{8,24},{16,0},{24,8},{1,17},{9,25},{17,1},{25,9},{2,18},{10... | collective-permute-start | bytes 368648 | tf_op jit(solution)/shard_map/ppermute | solution.py:1013
  322.7 7.2 %collective-permute-start.29 = (bf16[24,2560]{1,0:T(8,128)(2,1)S(1)}, bf16[24,2560]{1,0:T(8,128)(2,1)S(1)}, u32[]{:S(2)}, u32[]{:S(2)}) collective-permute-start(bf16[24,2560]{1,0:T(8,128)(2,1)S(1)} %fusion.14.refs_0_), channel_id=1, source_target_pairs={{0,8},{8,0},{16,24},{24,16},{1,9},{9,1},{17,25},{25,17},{2,10},{10... | collective-permute-start | bytes 368648 | tf_op jit(solution)/shard_map/ppermute | solution.py:1013
  330.0 1.7 collective-permute-start.31
  330.1 5.3 %collective-permute-start.30 = (bf16[24,2560]{1,0:T(8,128)(2,1)S(1)}, bf16[24,2560]{1,0:T(8,128)(2,1)S(1)}, u32[]{:S(2)}, u32[]{:S(2)}) collective-permute-start(bf16[24,2560]{1,0:T(8,128)(2,1)S(1)} %collective-permute-done.28.refs_1_), channel_id=1, source_target_pairs={{0,8},{8,0},{16,24},{24,16},{1,9},{9,1},{17,25},{25,17},{2,10},{10... | collective-permute-start | bytes 368648 | tf_op jit(solution)/shard_map/ppermute | solution.py:1013
  (34 other events, 257.8 us)
where the time goes:
time: 345 us; the launch traced here: 339 us
  Pallas kernels  229 us (66%)
  starting transfers between devices  44 us (13%)
  waiting for transfers between devices  27.2 us (8%)
  other arithmetic  20.8 us (6%)
  local copies, waits for them, and re-layouts  15.3 us (4%)
    pallas_call x4, Pallas kernels, attend_back(): pl.pallas_call(attend_back_kernel, grid=(frames, pairs), in_specs=in_spec...  62.4 us
    pallas_call x1, Pallas kernels, between(): pl.pallas_call(between_kernel, grid=(rows // block,), in_specs=[row(width...  31.6 us
    pallas_call x2, Pallas kernels, attend(): pl.pallas_call(functools.partial(attend_kernel, count, chained, final), g...  27.7 us
    pallas_call x6, Pallas kernels, block_sums(): pl.pallas_call(functools.partial(block_sums_kernel, counts, dealt), grid_...  24.9 us
    ppermute x22, starting transfers between devices, swap(): return lax.ppermute(values, axis, [(i, i ^ bit) for i in range(count)])  22.2 us
    pallas_call x4, Pallas kernels, project(): pl.pallas_call(functools.partial(project_kernel, own), grid=(rows // bloc...  21 us
    ppermute x22, waiting for transfers between devices, swap(): return lax.ppermute(values, axis, [(i, i ^ bit) for i in range(count)])  16.7 us
    pallas_call x1, Pallas kernels, late_grads(): pl.pallas_call(functools.partial(late_grads_kernel, count), grid=(3 * thi...  13.4 us
  transfers between devices with their start and end apart: 32, of which 10 were waited for; matrix products, arithmetic and copies ran while one was open for 8% of the time, Pallas kernels for 40%

commit v1 on v0

--- a/solution.py
+++ b/solution.py
@@ -158,14 +158,24 @@
     )(queries, *shards, *shards, *(before if chained else ()))
 
 
-def column_sums(total, values):
-    normed, _ = layer_norm(values.astype(F32))
-    return jnp.concatenate(
-        (
-            jnp.sum(total * normed, axis=0, keepdims=True),
-            jnp.sum(total, axis=0, keepdims=True),
-        )
-    )
+def column_sums(total_ref, x_ref, term_ref=None):
+    rows, width = total_ref.shape
+    block = math.gcd(rows, 64)
+
+    def step(i, sums):
+        span = pl.ds(pl.multiple_of(i * block, block), block)
+        total = total_ref[span, :]
+        if term_ref is not None:
+            term_ref[span, :] = total.astype(term_ref.dtype)
+        normed, _ = layer_norm(x_ref[span, :].astype(F32))
+        return sums + jnp.concatenate(
+            (
+                jnp.sum(total * normed, axis=0, keepdims=True),
+                jnp.sum(total, axis=0, keepdims=True),
+            )
+        )
+
+    return lax.fori_loop(0, rows // block, step, jnp.zeros((2, width), F32))
 
 
 def attend_back_kernel(
@@ -183,6 +193,7 @@
     dkv_ref,
     term_ref,
     sums_ref,
+    total_ref,
 ):
     pair = pl.program_id(1)
     key_terms = []
@@ -216,9 +227,8 @@
     @pl.when(pair == pl.num_programs(1) - 1)
     def _():
         total = dot(dkv_ref[0, :, :width], wk_ref[...], NT)
-        total = total + dot(dkv_ref[0, :, width:], wv_ref[...], NT)
-        term_ref[0] = total.astype(term_ref.dtype)
-        sums_ref[0] = column_sums(total, x_ref[0])
+        total_ref[...] = total + dot(dkv_ref[0, :, width:], wv_ref[...], NT)
+        sums_ref[0] = column_sums(total_ref, x_ref.at[0], term_ref.at[0])
 
 
 def attend_back(queries, grad_out, out, logs, shard, weights, source, before):
@@ -255,6 +265,7 @@
         in_specs=in_specs,
         out_specs=out_specs,
         out_shape=out_shape,
+        scratch_shapes=[pltpu.VMEM((keys, width), F32)],
         input_output_aliases=aliases,
         compiler_params=PARAMS,
         name="attend_back",
@@ -271,7 +282,7 @@
     low_ref[0] = low
     total = dot(low, w_ref[...], (((0,), (1,)), ((), ())))
     term_ref[0] = total
-    sums_ref[0] = column_sums(total, x_ref[0])
+    sums_ref[0] = column_sums(term_ref.at[0], x_ref.at[0])
 
 
 def query_back(grad_query, weights, source):
@@ -300,6 +311,31 @@
             flops=frames * rows * width * width, transcendentals=0, bytes_accessed=rows * width
         ),
     )(grad_query, weights, source)
+
+
+def input_back_kernel(
+    own_ref, query_ref, right_ref, left_ref, residual_ref, x_ref, gain_ref, out_ref
+):
+    total = own_ref[...].astype(F32) + query_ref[...]
+    total = total + right_ref[...].astype(F32) + left_ref[...].astype(F32)
+    normed, inverse = layer_norm(x_ref[...].astype(F32))
+    out_ref[...] = residual_ref[...] + norm_back(total * gain_ref[...][None], normed, inverse)
+
+
+def input_back(terms, residual, source, gain):
+    rows, width = source.shape
+    block = math.gcd(rows, 128)
+    row = pl.BlockSpec((block, width), lambda i: (i, 0))
+    return pl.pallas_call(
+        input_back_kernel,
+        grid=(rows // block,),
+        in_specs=[row] * 6 + [pl.BlockSpec((width,), lambda i: (0,))],
+        out_specs=row,
+        out_shape=jax.ShapeDtypeStruct((rows, width), F32),
+        compiler_params=PARAMS,
+        name="input_back",
+        cost_estimate=pl.CostEstimate(flops=1 << 20, transcendentals=0, bytes_accessed=1 << 20),
+    )(*terms, residual, source, gain)
 
 
 def between_kernel(
@@ -340,7 +376,7 @@
     gain = gain_ref[...][None]
     hidden = (normed * gain + shift_ref[...][None]).astype(BF)
     hidden_ref[...] = hidden
-    wide = 512
+    wide = 1024
     steps = wu_ref.shape[1] // wide
     sum_ref[...] = residual + bd_ref[...][None]
 
@@ -1189,9 +1225,8 @@
         [heads_low[:, g * 128 : g * 128 + RESULT_FIELDS] for g in range(3)], axis=1
     )
     inputs = inputs.astype(F32)
-    normed_one, inverse_one = layer_norm(inputs)
-
     def input_gradient(grad_mixed):
+        normed_one, inverse_one = layer_norm(inputs)
         return grad_residual + norm_back(
             grad_mixed.reshape(rows, width) * gain_one, normed_one, inverse_one
         )
@@ -1281,8 +1316,8 @@
         *late.got_one, blended = hold(*late.got_one, blended)
         *sent, own, early[0] = hold(*late.two(), own, early[0])
         late.trade_two(sent)
-        grad_input = input_gradient(
-            own.astype(F32) + query_term + right.astype(F32) + left.astype(F32)
+        grad_input = input_back(
+            [flat(t) for t in (own, query_term, right, left)], grad_residual, flat(source), gain_one
         )
         *late.got_two, grad_input = hold(*late.got_two, grad_input)
         early[0], *parts = hold(early[0], *late.quarters())

time: 345 us -> 366 us (1.061)
  waiting for transfers between devices: 27.2 us -> 46.6 us
  Pallas kernels: 229 us -> 239 us
  other arithmetic: 20.8 us -> 14.1 us
    ppermute x22, waiting for transfers between devices: 16.7 us -> 36.4 us  [swap(): return lax.ppermute(values, axis, [(i, i ^ bit) for i in range(count)])]
    pallas_call x4, Pallas kernels: 62.4 us -> 68.1 us  [attend_back(): pl.pallas_call(attend_back_kernel, grid=(frames, pairs), in_specs=in_spec...]
    pallas_call x0 -> x1, Pallas kernels: none -> 5.19 us  [input_back(): pl.pallas_call(input_back_kernel, grid=(rows // block,), in_specs=[row] *...]
    reduce_sum x3 -> x0, other arithmetic: 4.98 us -> none  [the longest x1 3.33 us: norm_back(): jnp.mean(grad_normed, axis=-1, keepdims=True)]
    unnamed x69 -> x61, local copies, waits for them, and re-layouts: 10 us -> 10 us
  transfers between devices with their start and end apart: 32 -> 32, of which waited for: 10 -> 10; matrix products, arithmetic and copies ran while one was open for 8% -> 5% of each run, Pallas kernels for 40% -> 40%
where the time goes in v1:
time: 366 us; the launch traced here: 360 us
  Pallas kernels  239 us (65%)
  waiting for transfers between devices  46.6 us (13%)
  starting transfers between devices  41.9 us (11%)
  local copies, waits for them, and re-layouts  15.1 us (4%)
  other arithmetic  14.1 us (4%)
    pallas_call x4, Pallas kernels, attend_back(): pl.pallas_call(attend_back_kernel, grid=(frames, pairs), in_specs=in_spec...  68.1 us
    ppermute x22, waiting for transfers between devices, swap(): return lax.ppermute(values, axis, [(i, i ^ bit) for i in range(count)])  36.4 us
    pallas_call x1, Pallas kernels, between(): pl.pallas_call(between_kernel, grid=(rows // block,), in_specs=[row(width...  28.5 us
    pallas_call x2, Pallas kernels, attend(): pl.pallas_call(functools.partial(attend_kernel, count, chained, final), g...  27.8 us
    pallas_call x6, Pallas kernels, block_sums(): pl.pallas_call(functools.partial(block_sums_kernel, counts, dealt), grid_...  25.1 us
    pallas_call x4, Pallas kernels, project(): pl.pallas_call(functools.partial(project_kernel, own), grid=(rows // bloc...  21 us
    ppermute x22, starting transfers between devices, swap(): return lax.ppermute(values, axis, [(i, i ^ bit) for i in range(count)])  20.7 us
    pallas_call x1, Pallas kernels, late_grads(): pl.pallas_call(functools.partial(late_grads_kernel, count), grid=(3 * thi...  13.3 us
  transfers between devices with their start and end apart: 32, of which 10 were waited for; matrix products, arithmetic and copies ran while one was open for 5% of the time, Pallas kernels for 40%

profile of v1, /device:TPU:0, one launch (start us, length us, event | category | flops | bytes accessed | tf_op | source)
XLA Modules:
  0.0 359.7 jit_solution(6485716134880303249)
XLA Ops:
  0.7 5.1 %collective-permute-start = (bf16[1,512,768]{2,1,0:T(8,128)(2,1)}, bf16[1,512,768]{2,1,0:T(8,128)(2,1)S(1)}, u32[]{:S(2)}, u32[]{:S(2)}) collective-permute-start(bf16[1,512,768]{2,1,0:T(8,128)(2,1)} %bitcast.108), channel_id=1, source_target_pairs={{0,1},{1,2},{2,3},{4,5},{5,6},{6,7},{8,9},{9,10},{10,11},{12,13},{... | collective-permute-start | bytes 2359304 | tf_op jit(solution)/shard_map/ppermute | solution.py:1110
  7.8 8.3 %copy.39 = bf16[1,32,16,2,4416]{4,2,1,3,0:T(8,128)(2,1)} copy(bf16[1,32,16,2,4416]{4,3,2,1,0:T(2,128)(2,1)} %param.21) | data formatting | bytes 18087936 | tf_op args[3]
  16.7 5.8 %project.4 = (bf16[512,768]{1,0:T(8,128)(2,1)}, bf16[512,1536]{1,0:T(8,128)(2,1)}, bf16[512,768]{1,0:T(8,128)(2,1)}) custom-call(bf16[512,768]{1,0:T(8,128)(2,1)} %bitcast.110, f32[768]{0:T(1024)} %gain_ref.3, f32[768]{0:T(1024)} %refs_4_.7, f32[1,768]{1,0:T(1,128)} %fusion.13.refs_3_.refs_5_, bf16[768,2304]{1,0:T(8,128)(2,1)} %w_ref.1, ...), custom_call_target="tpu_custom_call" | custom-call | flops 301989888 | bytes 393216 | tf_op jit(solution)/shard_map/project/pallas_call | solution.py:65
  22.9 4.1 %collective-permute-done.1 = bf16[1,512,768]{2,1,0:T(8,128)(2,1)S(1)} collective-permute-done((bf16[1,512,768]{2,1,0:T(8,128)(2,1)}, bf16[1,512,768]{2,1,0:T(8,128)(2,1)S(1)}, u32[]{:S(2)}, u32[]{:S(2)}) %collective-permute-start.1) | collective-permute-done | bytes 786464 | tf_op jit(solution)/shard_map/ppermute | solution.py:1111
  28.9 10.3 %pixel_sums.1 = (f32[512,128]{1,0:T(8,128)}, f32[512,128]{1,0:T(8,128)}, f32[512,128]{1,0:T(8,128)}) custom-call(bf16[2,512,4416]{2,1,0:T(8,128)(2,1)} %bitcast.77, bf16[512,4416]{1,0:T(8,128)(2,1)} %bitcast.122), custom_call_target="tpu_custom_call" | custom-call | flops 289406976 | bytes 2260992 | tf_op jit(solution)/shard_map/pixel_sums/pallas_call | solution.py:993
  39.3 5.1 %project.5 = (bf16[512,768]{1,0:T(8,128)(2,1)}, bf16[512,1536]{1,0:T(8,128)(2,1)}, bf16[512,768]{1,0:T(8,128)(2,1)}) custom-call(s32[1]{0:T(128)} %bitcast.7.refs_0_, bf16[512,768]{1,0:T(8,128)(2,1)} %bitcast.123, bf16[512,768]{1,0:T(8,128)(2,1)} %bitcast.134, f32[768]{0:T(1024)} %gain_ref.3, f32[768]{0:T(1024)} %refs_4_.7, ...), custom_call_target="tpu_custom_call" | custom-call | flops 301989888 | bytes 393216 | tf_op jit(solution)/shard_map/project/pallas_call | solution.py:65
  44.4 5.6 %collective-permute-done.3 = bf16[1,512,768]{2,1,0:T(8,128)(2,1)S(1)} collective-permute-done((bf16[1,512,768]{2,1,0:T(8,128)(2,1)S(1)}, bf16[1,512,768]{2,1,0:T(8,128)(2,1)S(1)}, u32[]{:S(2)}, u32[]{:S(2)}) %collective-permute-start.3) | collective-permute-done | bytes 786464 | tf_op jit(solution)/shard_map/ppermute | solution.py:1157
  53.4 5.1 %project.6 = (bf16[512,768]{1,0:T(8,128)(2,1)}, bf16[512,1536]{1,0:T(8,128)(2,1)}, bf16[512,768]{1,0:T(8,128)(2,1)}) custom-call(s32[1]{0:T(128)} %bitcast.15.refs_0_, bf16[512,768]{1,0:T(8,128)(2,1)} %bitcast.119, bf16[512,768]{1,0:T(8,128)(2,1)} %bitcast.124, f32[768]{0:T(1024)} %gain_ref.3, f32[768]{0:T(1024)} %refs_4_.7, ...), custom_call_target="tpu_custom_call" | custom-call | flops 301989888 | bytes 393216 | tf_op jit(solution)/shard_map/project/pallas_call | solution.py:65
  58.4 18.2 %attend.2 = (f32[1,768,512]{2,1,0:T(8,128)}, f32[1,6,2,512]{3,2,1,0:T(2,128)}) custom-call(bf16[1,512,768]{2,1,0:T(8,128)(2,1)} %bitcast.86, bf16[1,512,1536]{2,1,0:T(8,128)(2,1)} %bitcast.92, bf16[1,512,1536]{2,1,0:T(8,128)(2,1)} %bitcast.96, bf16[1,512,1536]{2,1,0:T(8,128)(2,1)} %bitcast.100, bf16[1,512,1536]{2,1,0:T(8,128)(2,1)} %bitcast.93, ...), custom_call_target="tpu_custom_call" | custom-call | flops 1207959552 | bytes 393216 | tf_op jit(solution)/shard_map/attend/pallas_call | solution.py:137
  77.5 5.1 %project.7 = (bf16[512,768]{1,0:T(8,128)(2,1)}, bf16[512,1536]{1,0:T(8,128)(2,1)}, bf16[512,768]{1,0:T(8,128)(2,1)}) custom-call(s32[1]{0:T(128)} %bitcast.15.refs_0_, bf16[512,768]{1,0:T(8,128)(2,1)} %bitcast.133, bf16[512,768]{1,0:T(8,128)(2,1)} %bitcast.120, f32[768]{0:T(1024)} %gain_ref.3, f32[768]{0:T(1024)} %refs_4_.7, ...), custom_call_target="tpu_custom_call" | custom-call | flops 301989888 | bytes 393216 | tf_op jit(solution)/shard_map/project/pallas_call | solution.py:65
  82.6 9.6 %attend.3 = (bf16[1,512,768]{2,1,0:T(8,128)(2,1)}, f32[1,6,2,512]{3,2,1,0:T(2,128)}) custom-call(bf16[1,512,768]{2,1,0:T(8,128)(2,1)} %bitcast.87, bf16[1,512,1536]{2,1,0:T(8,128)(2,1)} %bitcast.104, bf16[1,512,1536]{2,1,0:T(8,128)(2,1)} %bitcast.105, f32[1,768,512]{2,1,0:T(8,128)} %get-tuple-element.205.refs_3_, f32[1,6,2,512]{3,2,1,0:T(2,128)} %get-tuple-element.206.refs_4_), custom_call_target="tpu_custom_call" | custom-call | flops 402653184 | bytes 393216 | tf_op jit(solution)/shard_map/attend/pallas_call | solution.py:137
  92.1 28.5 %between.1 = (bf16[512,768]{1,0:T(8,128)(2,1)}, bf16[512,3072]{1,0:T(8,128)(2,1)}, bf16[512,3072]{1,0:T(8,128)(2,1)}, bf16[512,768]{1,0:T(8,128)(2,1)}, bf16[512...) custom-call(bf16[512,768]{1,0:T(8,128)(2,1)} %bitcast.111, ...), custom_call_target="tpu_custom_call" | custom-call | flops 1207959552 | bytes 1572864 | tf_op jit(solution)/shard_map/between/pallas_call | solution.py:480
  125.3 8.5 %down_grads.1 = (bf16[8,48,7168]{2,1,0:T(8,128)(2,1)}, bf16[8,48,7168]{2,1,0:T(8,128)(2,1)}) custom-call(s32[1]{0:T(128)} %bitcast.3.place_ref, bf16[512,3072]{1,0:T(8,128)(2,1)} %get-tuple-element.219.act_ref, bf16[512,768]{1,0:T(8,128)(2,1)} %get-tuple-element.220.down_ref), custom_call_target="tpu_custom_call" | custom-call | flops 301989888 | bytes 294912 | tf_op jit(solution)/shard_map/down_grads/pallas_call | solution.py:659
  133.9 10.4 %early_grads.1 = (bf16[8,48,7168]{2,1,0:T(8,128)(2,1)}, bf16[8,48,7168]{2,1,0:T(8,128)(2,1)}) custom-call(s32[1]{0:T(128)} %bitcast.3.place_ref, bf16[512,768]{1,0:T(8,128)(2,1)} %get-tuple-element.212.h_ref, bf16[512,768]{1,0:T(8,128)(2,1)} %bitcast.85, bf16[512,768]{1,0:T(8,128)(2,1)} %get-tuple-element.213.f_ref, ...), custom_call_target="tpu_custom_call", output_to_operand_aliasing={{0}: (8, {}), {1}: (9, {})} | custom-call | flops 3221225472 | bytes 10485760 | tf_op jit(solution)/shard_map/early_grads/pallas_call | solution.py:603
  146.2 17.0 %attend_back.4 = (f32[1,768,512]{2,1,0:T(8,128)}, bf16[1,512,1536]{2,1,0:T(8,128)(2,1)}, bf16[1,512,768]{2,1,0:T(8,128)(2,1)}, f32[1,2,768]{2,1,0:T(2,128)}) custom-call(bf16[1,512,768]{2,1,0:T(8,128)(2,1)} %bitcast.88, bf16[1,512,768]{2,1,0:T(8,128)(2,1)} %bitcast.115, ...), custom_call_target="tpu_custom_call", output_to_operand_aliasing={{0}: (9, {})} | custom-call | flops 805306368 | bytes 393216 | tf_op jit(solution)/shard_map/attend_back/pallas_call | solution.py:262
  163.2 4.6 %block_sums.6 = (bf16[4,2,24,3584]{3,2,1,0:T(8,128)(2,1)}, bf16[2,4,24,3584]{3,2,1,0:T(8,128)(2,1)}) custom-call(s32[3]{0:T(128)} %pad_add_fusion.where_ref, bf16[2,4,2,24,7168]{4,3,2,1,0:T(8,128)(2,1)} %bitcast.71, bf16[2,4,2,24,7168]{4,3,2,1,0:T(8,128)(2,1)} %bitcast.33.refs_1_.refs_3_.refs_4_.refs_5_, bf16[2,4,2,24,7168]{4,3,2,1,0:T(8,128)(2,1)} %bitcast.72, ...), custom_call_target="tpu_custom_call" | custom-call | flops 1048576 | bytes 1048576 | tf_op jit(solution)/shard_map/block_sums/pallas_call | solution.py:770
  167.9 4.6 %collective-permute-start.6 = (bf16[1,512,768]{2,1,0:T(8,128)(2,1)}, bf16[1,512,768]{2,1,0:T(8,128)(2,1)S(1)}, u32[]{:S(2)}, u32[]{:S(2)}) collective-permute-start(bf16[1,512,768]{2,1,0:T(8,128)(2,1)} %get-tuple-element.238), channel_id=1, source_target_pairs={{0,1},{3,2},{4,5},{7,6},{8,9},{11,10},{12,13},{15,14},{16,17},{19,... | collective-permute-start | bytes 2359304 | tf_op jit(solution)/shard_map/ppermute | solution.py:1275
  175.6 17.1 %attend_back.5 = (f32[1,768,512]{2,1,0:T(8,128)}, bf16[1,512,1536]{2,1,0:T(8,128)(2,1)}, bf16[1,512,768]{2,1,0:T(8,128)(2,1)}, f32[1,2,768]{2,1,0:T(2,128)}) custom-call(bf16[1,512,768]{2,1,0:T(8,128)(2,1)} %bitcast.89, bf16[1,512,768]{2,1,0:T(8,128)(2,1)} %bitcast.116, ...), custom_call_target="tpu_custom_call", output_to_operand_aliasing={{0}: (9, {})} | custom-call | flops 805306368 | bytes 393216 | tf_op jit(solution)/shard_map/attend_back/pallas_call | solution.py:262
  198.9 17.0 %attend_back.6 = (f32[1,768,512]{2,1,0:T(8,128)}, bf16[1,512,1536]{2,1,0:T(8,128)(2,1)}, bf16[1,512,768]{2,1,0:T(8,128)(2,1)}, f32[1,2,768]{2,1,0:T(2,128)}) custom-call(bf16[1,512,768]{2,1,0:T(8,128)(2,1)} %bitcast.90, bf16[1,512,768]{2,1,0:T(8,128)(2,1)} %bitcast.117, ...), custom_call_target="tpu_custom_call", output_to_operand_aliasing={{0}: (9, {})} | custom-call | flops 805306368 | bytes 393216 | tf_op jit(solution)/shard_map/attend_back/pallas_call | solution.py:262
  216.0 3.9 %block_sums.7 = (bf16[4,24,3584]{2,1,0:T(8,128)(2,1)}, bf16[4,24,3584]{2,1,0:T(8,128)(2,1)}) custom-call(s32[3]{0:T(128)} %pad_add_fusion.where_ref, bf16[2,4,2,24,7168]{4,3,2,1,0:T(8,128)(2,1)} %bitcast.73, bf16[2,4,2,24,7168]{4,3,2,1,0:T(8,128)(2,1)} %bitcast.33.refs_1_.refs_3_.refs_4_.refs_5_, bf16[4,2,24,3584]{3,2,1,0:T(8,128)(2,1)} %collective-permute-done.9.refs_2_, ...), custom_call_target="tpu_custom_call" | custom-call | flops 1048576 | bytes 1048576 | tf_op jit(solution)/shard_map/block_sums/pallas_call | solution.py:770
  228.6 17.0 %attend_back.7 = (f32[1,768,512]{2,1,0:T(8,128)}, bf16[1,512,1536]{2,1,0:T(8,128)(2,1)}, bf16[1,512,768]{2,1,0:T(8,128)(2,1)}, f32[1,2,768]{2,1,0:T(2,128)}) custom-call(bf16[1,512,768]{2,1,0:T(8,128)(2,1)} %bitcast.91, bf16[1,512,768]{2,1,0:T(8,128)(2,1)} %bitcast.118, ...), custom_call_target="tpu_custom_call", output_to_operand_aliasing={{0}: (9, {})} | custom-call | flops 805306368 | bytes 393216 | tf_op jit(solution)/shard_map/attend_back/pallas_call | solution.py:262
  245.9 6.4 %query_back.1 = (bf16[1,768,512]{2,1,0:T(8,128)(2,1)}, f32[1,512,768]{2,1,0:T(8,128)}, f32[1,2,768]{2,1,0:T(2,128)}) custom-call(f32[1,768,512]{2,1,0:T(8,128)} %get-tuple-element.256.dq_ref, bf16[768,2304]{1,0:T(8,128)(2,1)} %w_ref.1, bf16[1,512,768]{2,1,0:T(8,128)(2,1)} %bitcast.113), custom_call_target="tpu_custom_call" | custom-call | flops 301989888 | bytes 393216 | tf_op jit(solution)/shard_map/query_back/pallas_call | solution.py:294
  253.9 13.3 %late_grads.1 = (bf16[8,48,2560]{2,1,0:T(8,128)(2,1)}, bf16[8,48,2560]{2,1,0:T(8,128)(2,1)}) custom-call(s32[1]{0:T(128)} %bitcast.3.place_ref, bf16[512,768]{1,0:T(8,128)(2,1)} %get-tuple-element.180.refs_0_, bf16[512,768]{1,0:T(8,128)(2,1)} %get-tuple-element.185.refs_1_, bf16[512,768]{1,0:T(8,128)(2,1)} %get-tuple-element.195.refs_2_, ...), custom_call_target="tpu_custom_call" | custom-call | flops 5435817984 | bytes 19660800 | tf_op jit(solution)/shard_map/late_grads/pallas_call | solution.py:714
  267.2 5.7 %block_sums.8 = (bf16[2,24,3584]{2,1,0:T(8,128)(2,1)}, bf16[2,24,3584]{2,1,0:T(8,128)(2,1)}, bf16[2,24,3584]{2,1,0:T(8,128)(2,1)}, bf16[2,24,3584]{2,1,0:T(8,128)(2,1)}) custom-call(s32[3]{0:T(128)} %pad_add_fusion.where_ref, bf16[2,4,2,24,7168]{4,3,2,1,0:T(8,128)(2,1)} %bitcast.75, bf16[2,4,2,24,7168]{4,3,2,1,0:T(8,128)(2,1)} %bitcast.33.refs_1_.refs_3_.refs_4_.refs_5_, ...), custom_call_target="tpu_custom_call" | custom-call | flops 1048576 | bytes 1048576 | tf_op jit(solution)/shard_map/block_sums/pallas_call | solution.py:770
  272.9 3.2 block_sums.9
  278.0 9.3 %blend.1 = bf16[512,4416]{1,0:T(8,128)(2,1)} custom-call(f32[512,128]{1,0:T(8,128)} %get-tuple-element.288.a_ref, f32[512,128]{1,0:T(8,128)} %get-tuple-element.289.b_ref, f32[512,128]{1,0:T(8,128)} %get-tuple-element.290.c_ref, bf16[2,512,4416]{2,1,0:T(8,128)(2,1)} %bitcast.78), custom_call_target="tpu_custom_call" | custom-call | flops 289406976 | bytes 2260992 | tf_op jit(solution)/shard_map/blend/pallas_call | solution.py:1032
  295.3 3.4 collective-permute-start.24
  299.8 5.2 %input_back.1 = f32[512,768]{1,0:T(8,128)} custom-call(bf16[512,768]{1,0:T(8,128)(2,1)} %bitcast.132, f32[512,768]{1,0:T(8,128)} %bitcast.126, bf16[512,768]{1,0:T(8,128)(2,1)} %bitcast.130, bf16[512,768]{1,0:T(8,128)(2,1)} %bitcast.131, f32[512,768]{1,0:T(8,128)} %get-tuple-element.304.residual_ref, bf16[512,768]{1,0:T(8,128)(2,1)} %bitcast.114, f32[768]{0:T(1024)} %gain_ref.3), custom_call_target="tpu_custom_call" | custom-call | flops 1048576 | bytes 1048576 | tf_op jit(solution)/shard_map/input_back/pallas_call | solution.py:329
  305.0 4.6 %block_sums.11 = (bf16[1,24,2560]{2,1,0:T(8,128)(2,1)}, bf16[1,24,2560]{2,1,0:T(8,128)(2,1)}, bf16[1,24,2560]{2,1,0:T(8,128)(2,1)}, bf16[1,24,2560]{2,1,0:T(8,128)(2,1)}) custom-call(s32[3]{0:T(128)} %pad_add_fusion.where_ref, bf16[2,4,2,24,2560]{4,3,2,1,0:T(8,128)(2,1)} %bitcast.83, bf16[2,4,2,24,2560]{4,3,2,1,0:T(8,128)(2,1)} %bitcast.43.refs_1_.refs_3_.refs_4_, ...), custom_call_target="tpu_custom_call" | custom-call | flops 1048576 | bytes 1048576 | tf_op jit(solution)/shard_map/block_sums/pallas_call | solution.py:770
  313.6 11.4 %collective-permute-done.20 = bf16[1,24,2560]{2,1,0:T(8,128)(2,1)S(1)} collective-permute-done((bf16[1,24,2560]{2,1,0:T(8,128)(2,1)}, bf16[1,24,2560]{2,1,0:T(8,128)(2,1)S(1)}, u32[]{:S(2)}, u32[]{:S(2)}) %collective-permute-start.20) | collective-permute-done | bytes 122912 | tf_op jit(solution)/shard_map/ppermute | solution.py:1049
  324.9 11.3 %collective-permute-done.21 = bf16[1,24,2560]{2,1,0:T(8,128)(2,1)S(1)} collective-permute-done((bf16[1,24,2560]{2,1,0:T(8,128)(2,1)}, bf16[1,24,2560]{2,1,0:T(8,128)(2,1)S(1)}, u32[]{:S(2)}, u32[]{:S(2)}) %collective-permute-start.21) | collective-permute-done | bytes 122912 | tf_op jit(solution)/shard_map/ppermute | solution.py:1049
  340.2 10.1 %collective-permute-done.28.refs_1_ = bf16[24,2560]{1,0:T(8,128)(2,1)S(1)} collective-permute-done((bf16[24,2560]{1,0:T(8,128)(2,1)S(1)}, bf16[24,2560]{1,0:T(8,128)(2,1)S(1)}, u32[]{:S(2)}, u32[]{:S(2)}) %collective-permute-start.28) | collective-permute-done | bytes 122912 | tf_op jit(solution)/shard_map/ppermute | solution.py:1049
  (150 shorter events, 62.6 us)
Async XLA Ops:
  0.7 22.2 %collective-permute-start = (bf16[1,512,768]{2,1,0:T(8,128)(2,1)}, bf16[1,512,768]{2,1,0:T(8,128)(2,1)S(1)}, u32[]{:S(2)}, u32[]{:S(2)}) collective-permute-start(bf16[1,512,768]{2,1,0:T(8,128)(2,1)} %bitcast.108), channel_id=1, source_target_pairs={{0,1},{1,2},{2,3},{4,5},{5,6},{6,7},{8,9},{9,10},{10,11},{12,13},{... | collective-permute-start | bytes 2359304 | tf_op jit(solution)/shard_map/ppermute | solution.py:1110
  5.8 21.1 %collective-permute-start.1 = (bf16[1,512,768]{2,1,0:T(8,128)(2,1)}, bf16[1,512,768]{2,1,0:T(8,128)(2,1)S(1)}, u32[]{:S(2)}, u32[]{:S(2)}) collective-permute-start(bf16[1,512,768]{2,1,0:T(8,128)(2,1)} %bitcast.109), channel_id=1, source_target_pairs={{3,2},{2,1},{1,0},{7,6},{6,5},{5,4},{11,10},{10,9},{9,8},{15,14},{... | collective-permute-start | bytes 2359304 | tf_op jit(solution)/shard_map/ppermute | solution.py:1111
  26.9 17.5 %collective-permute-start.2 = (bf16[1,512,768]{2,1,0:T(8,128)(2,1)S(1)}, bf16[1,512,768]{2,1,0:T(8,128)(2,1)S(1)}, u32[]{:S(2)}, u32[]{:S(2)}) collective-permute-start(bf16[1,512,768]{2,1,0:T(8,128)(2,1)S(1)} %collective-permute-done), channel_id=1, source_target_pairs={{1,2},{2,3},{5,6},{6,7},{9,10},{10,11},{13,14},{14,15},{17,18},{18... | collective-permute-start | bytes 2359304 | tf_op jit(solution)/shard_map/ppermute | solution.py:1156
  27.6 22.4 %collective-permute-start.3 = (bf16[1,512,768]{2,1,0:T(8,128)(2,1)S(1)}, bf16[1,512,768]{2,1,0:T(8,128)(2,1)S(1)}, u32[]{:S(2)}, u32[]{:S(2)}) collective-permute-start(bf16[1,512,768]{2,1,0:T(8,128)(2,1)S(1)} %collective-permute-done.1), channel_id=1, source_target_pairs={{2,1},{1,0},{6,5},{5,4},{10,9},{9,8},{14,13},{13,12},{18,17},{17,1... | collective-permute-start | bytes 2359304 | tf_op jit(solution)/shard_map/ppermute | solution.py:1157
  50.2 26.4 %collective-permute-start.4 = (bf16[1,512,768]{2,1,0:T(8,128)(2,1)S(1)}, bf16[1,512,768]{2,1,0:T(8,128)(2,1)S(1)}, u32[]{:S(2)}, u32[]{:S(2)}) collective-permute-start(bf16[1,512,768]{2,1,0:T(8,128)(2,1)S(1)} %add.160), channel_id=1, source_target_pairs={{2,3},{1,0},{6,7},{5,4},{10,11},{9,8},{14,15},{13,12},{18,19},{17,... | collective-permute-start | bytes 2359304 | tf_op jit(solution)/shard_map/ppermute | solution.py:1165
  144.3 18.9 %collective-permute-start.5 = (bf16[8,48,7168]{2,1,0:T(8,128)(2,1)}, bf16[8,48,7168]{2,1,0:T(8,128)(2,1)}, u32[]{:S(2)}, u32[]{:S(2)}) collective-permute-start(bf16[8,48,7168]{2,1,0:T(8,128)(2,1)} %get-tuple-element.232), channel_id=1, source_target_pairs={{0,8},{8,0},{16,24},{24,16},{1,9},{9,1},{17,25},{25,17},{2,10},{10... | collective-permute-start | bytes 16515080 | tf_op jit(solution)/shard_map/ppermute | solution.py:1049
  167.9 24.8 %collective-permute-start.6 = (bf16[1,512,768]{2,1,0:T(8,128)(2,1)}, bf16[1,512,768]{2,1,0:T(8,128)(2,1)S(1)}, u32[]{:S(2)}, u32[]{:S(2)}) collective-permute-start(bf16[1,512,768]{2,1,0:T(8,128)(2,1)} %get-tuple-element.238), channel_id=1, source_target_pairs={{0,1},{3,2},{4,5},{7,6},{8,9},{11,10},{12,13},{15,14},{16,17},{19,... | collective-permute-start | bytes 2359304 | tf_op jit(solution)/shard_map/ppermute | solution.py:1275
  172.5 43.4 %collective-permute-start.9 = (bf16[4,2,24,3584]{3,2,1,0:T(8,128)(2,1)}, bf16[4,2,24,3584]{3,2,1,0:T(8,128)(2,1)}, u32[]{:S(2)}, u32[]{:S(2)}) collective-permute-start(bf16[4,2,24,3584]{3,2,1,0:T(8,128)(2,1)} %get-tuple-element.243), channel_id=1, source_target_pairs={{0,4},{4,0},{1,5},{5,1},{2,6},{6,2},{3,7},{7,3},{8,12},{12,8},{9,1... | collective-permute-start | bytes 4128776 | tf_op jit(solution)/shard_map/ppermute | solution.py:1049
  174.1 41.9 %collective-permute-start.10 = (bf16[2,4,24,3584]{3,2,1,0:T(8,128)(2,1)}, bf16[2,4,24,3584]{3,2,1,0:T(8,128)(2,1)}, u32[]{:S(2)}, u32[]{:S(2)}) collective-permute-start(bf16[2,4,24,3584]{3,2,1,0:T(8,128)(2,1)} %get-tuple-element.244), channel_id=1, source_target_pairs={{0,16},{8,24},{16,0},{24,8},{1,17},{9,25},{17,1},{25,9},{2,18},{10... | collective-permute-start | bytes 4128776 | tf_op jit(solution)/shard_map/ppermute | solution.py:1049
  195.1 24.7 %collective-permute-start.7 = (bf16[1,512,768]{2,1,0:T(8,128)(2,1)}, bf16[1,512,768]{2,1,0:T(8,128)(2,1)}, u32[]{:S(2)}, u32[]{:S(2)}) collective-permute-start(bf16[1,512,768]{2,1,0:T(8,128)(2,1)} %fusion.3), channel_id=1, source_target_pairs={{0,1},{1,2},{4,5},{5,6},{8,9},{9,10},{12,13},{13,14},{16,17},{17,1... | collective-permute-start | bytes 2359304 | tf_op jit(solution)/shard_map/ppermute | solution.py:1281
  197.3 24.5 %collective-permute-start.8 = (bf16[1,512,768]{2,1,0:T(8,128)(2,1)}, bf16[1,512,768]{2,1,0:T(8,128)(2,1)}, u32[]{:S(2)}, u32[]{:S(2)}) collective-permute-start(bf16[1,512,768]{2,1,0:T(8,128)(2,1)} %fusion.3), channel_id=1, source_target_pairs={{3,2},{2,1},{7,6},{6,5},{11,10},{10,9},{15,14},{14,13},{19,18},{18... | collective-permute-start | bytes 2359304 | tf_op jit(solution)/shard_map/ppermute | solution.py:1282
  223.2 22.4 %collective-permute-start.11 = (bf16[1,512,768]{2,1,0:T(8,128)(2,1)S(1)}, bf16[1,512,768]{2,1,0:T(8,128)(2,1)S(1)}, u32[]{:S(2)}, u32[]{:S(2)}) collective-permute-start(bf16[1,512,768]{2,1,0:T(8,128)(2,1)S(1)} %fusion.4), channel_id=1, source_target_pairs={{0,1},{1,2},{2,3},{4,5},{5,6},{6,7},{8,9},{9,10},{10,11},{12,13},{... | collective-permute-start | bytes 2359304 | tf_op jit(solution)/shard_map/ppermute | solution.py:1290
  224.8 21.0 %collective-permute-start.12 = (bf16[1,512,768]{2,1,0:T(8,128)(2,1)S(1)}, bf16[1,512,768]{2,1,0:T(8,128)(2,1)S(1)}, u32[]{:S(2)}, u32[]{:S(2)}) collective-permute-start(bf16[1,512,768]{2,1,0:T(8,128)(2,1)S(1)} %add_convert_fusion), channel_id=1, source_target_pairs={{3,2},{2,1},{1,0},{7,6},{6,5},{5,4},{11,10},{10,9},{9,8},{15,14},{... | collective-permute-start | bytes 2359304 | tf_op jit(solution)/shard_map/ppermute | solution.py:1291
  226.1 19.5 %collective-permute-start.13 = (bf16[4,24,3584]{2,1,0:T(8,128)(2,1)}, bf16[4,24,3584]{2,1,0:T(8,128)(2,1)S(1)}, u32[]{:S(2)}, u32[]{:S(2)}) collective-permute-start(bf16[4,24,3584]{2,1,0:T(8,128)(2,1)} %get-tuple-element.254), channel_id=1, source_target_pairs={{0,16},{8,24},{16,0},{24,8},{1,17},{9,25},{17,1},{25,9},{2,18},{10... | collective-permute-start | bytes 2064392 | tf_op jit(solution)/shard_map/ppermute | solution.py:1049
  227.1 18.6 %collective-permute-start.14 = (bf16[4,24,3584]{2,1,0:T(8,128)(2,1)}, bf16[4,24,3584]{2,1,0:T(8,128)(2,1)}, u32[]{:S(2)}, u32[]{:S(2)}) collective-permute-start(bf16[4,24,3584]{2,1,0:T(8,128)(2,1)} %get-tuple-element.255), channel_id=1, source_target_pairs={{0,4},{4,0},{1,5},{5,1},{2,6},{6,2},{3,7},{7,3},{8,12},{12,8},{9,1... | collective-permute-start | bytes 2064392 | tf_op jit(solution)/shard_map/ppermute | solution.py:1049
  267.2 5.8 %collective-permute-start.15 = (bf16[8,48,2560]{2,1,0:T(8,128)(2,1)}, bf16[8,48,2560]{2,1,0:T(8,128)(2,1)}, u32[]{:S(2)}, u32[]{:S(2)}) collective-permute-start(bf16[8,48,2560]{2,1,0:T(8,128)(2,1)} %get-tuple-element.273), channel_id=1, source_target_pairs={{0,8},{8,0},{16,24},{24,16},{1,9},{9,1},{17,25},{25,17},{2,10},{10... | collective-permute-start | bytes 5898248 | tf_op jit(solution)/shard_map/ppermute | solution.py:1049
  276.1 13.9 %collective-permute-start.16 = (bf16[2,2,24,2560]{3,2,1,0:T(8,128)(2,1)}, bf16[2,2,24,2560]{3,2,1,0:T(8,128)(2,1)}, u32[]{:S(2)}, u32[]{:S(2)}) collective-permute-start(bf16[2,2,24,2560]{3,2,1,0:T(8,128)(2,1)} %get-tuple-element.286), channel_id=1, source_target_pairs={{0,4},{4,0},{1,5},{5,1},{2,6},{6,2},{3,7},{7,3},{8,12},{12,8},{9,1... | collective-permute-start | bytes 1474568 | tf_op jit(solution)/shard_map/ppermute | solution.py:1049
  276.7 13.7 %collective-permute-start.17 = (bf16[2,2,24,2560]{3,2,1,0:T(8,128)(2,1)}, bf16[2,2,24,2560]{3,2,1,0:T(8,128)(2,1)}, u32[]{:S(2)}, u32[]{:S(2)}) collective-permute-start(bf16[2,2,24,2560]{3,2,1,0:T(8,128)(2,1)} %get-tuple-element.287), channel_id=1, source_target_pairs={{0,16},{8,24},{16,0},{24,8},{1,17},{9,25},{17,1},{25,9},{2,18},{10... | collective-permute-start | bytes 1474568 | tf_op jit(solution)/shard_map/ppermute | solution.py:1049
  293.3 11.7 %collective-permute-start.18 = (bf16[2,24,2560]{2,1,0:T(8,128)(2,1)}, bf16[2,24,2560]{2,1,0:T(8,128)(2,1)}, u32[]{:S(2)}, u32[]{:S(2)}) collective-permute-start(bf16[2,24,2560]{2,1,0:T(8,128)(2,1)} %get-tuple-element.298), channel_id=1, source_target_pairs={{0,16},{8,24},{16,0},{24,8},{1,17},{9,25},{17,1},{25,9},{2,18},{10... | collective-permute-start | bytes 737288 | tf_op jit(solution)/shard_map/ppermute | solution.py:1049
  294.6 10.4 %collective-permute-start.19 = (bf16[2,24,2560]{2,1,0:T(8,128)(2,1)}, bf16[2,24,2560]{2,1,0:T(8,128)(2,1)}, u32[]{:S(2)}, u32[]{:S(2)}) collective-permute-start(bf16[2,24,2560]{2,1,0:T(8,128)(2,1)} %get-tuple-element.299), channel_id=1, source_target_pairs={{0,4},{4,0},{1,5},{5,1},{2,6},{6,2},{3,7},{7,3},{8,12},{12,8},{9,1... | collective-permute-start | bytes 737288 | tf_op jit(solution)/shard_map/ppermute | solution.py:1049
  295.3 40.9 %collective-permute-start.24 = (bf16[2,24,3584]{2,1,0:T(8,128)(2,1)}, bf16[2,24,3584]{2,1,0:T(8,128)(2,1)}, u32[]{:S(2)}, u32[]{:S(2)}) collective-permute-start(bf16[2,24,3584]{2,1,0:T(8,128)(2,1)} %get-tuple-element.319), channel_id=1, source_target_pairs={{0,3},{1,2},{2,1},{3,0},{4,7},{5,6},{6,5},{7,4},{8,11},{9,10},{10,... | collective-permute-start | bytes 1032200 | tf_op jit(solution)/shard_map/ppermute | solution.py:1049
  298.8 37.5 %collective-permute-start.23 = (bf16[2,24,3584]{2,1,0:T(8,128)(2,1)}, bf16[2,24,3584]{2,1,0:T(8,128)(2,1)}, u32[]{:S(2)}, u32[]{:S(2)}) collective-permute-start(bf16[2,24,3584]{2,1,0:T(8,128)(2,1)} %get-tuple-element.318), channel_id=1, source_target_pairs={{0,2},{1,3},{2,0},{3,1},{4,6},{5,7},{6,4},{7,5},{8,10},{9,11},{10,... | collective-permute-start | bytes 1032200 | tf_op jit(solution)/shard_map/ppermute | solution.py:1049
  299.5 36.8 %collective-permute-start.22 = (bf16[2,24,3584]{2,1,0:T(8,128)(2,1)}, bf16[2,24,3584]{2,1,0:T(8,128)(2,1)}, u32[]{:S(2)}, u32[]{:S(2)}) collective-permute-start(bf16[2,24,3584]{2,1,0:T(8,128)(2,1)} %get-tuple-element.317), channel_id=1, source_target_pairs={{0,1},{1,0},{2,3},{3,2},{4,5},{5,4},{6,7},{7,6},{8,9},{9,8},{10,11... | collective-permute-start | bytes 1032200 | tf_op jit(solution)/shard_map/ppermute | solution.py:1049
  309.6 15.3 %collective-permute-start.20 = (bf16[1,24,2560]{2,1,0:T(8,128)(2,1)}, bf16[1,24,2560]{2,1,0:T(8,128)(2,1)S(1)}, u32[]{:S(2)}, u32[]{:S(2)}) collective-permute-start(bf16[1,24,2560]{2,1,0:T(8,128)(2,1)} %get-tuple-element.313), channel_id=1, source_target_pairs={{0,1},{1,0},{2,3},{3,2},{4,5},{5,4},{6,7},{7,6},{8,9},{9,8},{10,11... | collective-permute-start | bytes 368648 | tf_op jit(solution)/shard_map/ppermute | solution.py:1049
  311.4 24.8 %collective-permute-start.21 = (bf16[1,24,2560]{2,1,0:T(8,128)(2,1)}, bf16[1,24,2560]{2,1,0:T(8,128)(2,1)S(1)}, u32[]{:S(2)}, u32[]{:S(2)}) collective-permute-start(bf16[1,24,2560]{2,1,0:T(8,128)(2,1)} %get-tuple-element.314), channel_id=1, source_target_pairs={{0,2},{1,3},{2,0},{3,1},{4,6},{5,7},{6,4},{7,5},{8,10},{9,11},{10,... | collective-permute-start | bytes 368648 | tf_op jit(solution)/shard_map/ppermute | solution.py:1049
  324.9 14.3 %collective-permute-start.27 = (bf16[1,24,2560]{2,1,0:T(8,128)(2,1)}, bf16[1,24,2560]{2,1,0:T(8,128)(2,1)S(1)}, u32[]{:S(2)}, u32[]{:S(2)}) collective-permute-start(bf16[1,24,2560]{2,1,0:T(8,128)(2,1)} %get-tuple-element.323), channel_id=1, source_target_pairs={{0,3},{1,2},{2,1},{3,0},{4,7},{5,6},{6,5},{7,4},{8,11},{9,10},{10,... | collective-permute-start | bytes 368648 | tf_op jit(solution)/shard_map/ppermute | solution.py:1049
  337.7 12.6 %collective-permute-start.25 = (bf16[2,24,3584]{2,1,0:T(8,128)(2,1)S(1)}, bf16[2,24,3584]{2,1,0:T(8,128)(2,1)S(1)}, u32[]{:S(2)}, u32[]{:S(2)}) collective-permute-start(bf16[2,24,3584]{2,1,0:T(8,128)(2,1)S(1)} %add_convert_fusion.3.refs_0_), channel_id=1, source_target_pairs={{0,16},{8,24},{16,0},{24,8},{1,17},{9,25},{17,1},{25,9},{2,18},{10... | collective-permute-start | bytes 1032200 | tf_op jit(solution)/shard_map/ppermute | solution.py:1049
  339.3 11.0 %collective-permute-start.26 = (bf16[2,24,3584]{2,1,0:T(8,128)(2,1)S(1)}, bf16[2,24,3584]{2,1,0:T(8,128)(2,1)S(1)}, u32[]{:S(2)}, u32[]{:S(2)}) collective-permute-start(bf16[2,24,3584]{2,1,0:T(8,128)(2,1)S(1)} %add_convert_fusion.3.refs_0_), channel_id=1, source_target_pairs={{0,8},{8,0},{16,24},{24,16},{1,9},{9,1},{17,25},{25,17},{2,10},{10... | collective-permute-start | bytes 1032200 | tf_op jit(solution)/shard_map/ppermute | solution.py:1049
  339.4 10.9 %collective-permute-start.28 = (bf16[24,2560]{1,0:T(8,128)(2,1)S(1)}, bf16[24,2560]{1,0:T(8,128)(2,1)S(1)}, u32[]{:S(2)}, u32[]{:S(2)}) collective-permute-start(bf16[24,2560]{1,0:T(8,128)(2,1)S(1)} %fusion.12.refs_0_), channel_id=1, source_target_pairs={{0,16},{8,24},{16,0},{24,8},{1,17},{9,25},{17,1},{25,9},{2,18},{10... | collective-permute-start | bytes 368648 | tf_op jit(solution)/shard_map/ppermute | solution.py:1049
  339.9 10.3 %collective-permute-start.29 = (bf16[24,2560]{1,0:T(8,128)(2,1)S(1)}, bf16[24,2560]{1,0:T(8,128)(2,1)S(1)}, u32[]{:S(2)}, u32[]{:S(2)}) collective-permute-start(bf16[24,2560]{1,0:T(8,128)(2,1)S(1)} %fusion.12.refs_0_), channel_id=1, source_target_pairs={{0,8},{8,0},{16,24},{24,16},{1,9},{9,1},{17,25},{25,17},{2,10},{10... | collective-permute-start | bytes 368648 | tf_op jit(solution)/shard_map/ppermute | solution.py:1049
  350.3 1.7 collective-permute-start.31
  350.4 5.4 %collective-permute-start.30 = (bf16[24,2560]{1,0:T(8,128)(2,1)S(1)}, bf16[24,2560]{1,0:T(8,128)(2,1)S(1)}, u32[]{:S(2)}, u32[]{:S(2)}) collective-permute-start(bf16[24,2560]{1,0:T(8,128)(2,1)S(1)} %collective-permute-done.28.refs_1_), channel_id=1, source_target_pairs={{0,8},{8,0},{16,24},{24,16},{1,9},{9,1},{17,25},{25,17},{2,10},{10... | collective-permute-start | bytes 368648 | tf_op jit(solution)/shard_map/ppermute | solution.py:1049
  (30 other events, 282.6 us)

commit v2 on v0

--- a/solution.py
+++ b/solution.py
@@ -340,7 +340,7 @@
     gain = gain_ref[...][None]
     hidden = (normed * gain + shift_ref[...][None]).astype(BF)
     hidden_ref[...] = hidden
-    wide = 512
+    wide = 1024
     steps = wu_ref.shape[1] // wide
     sum_ref[...] = residual + bd_ref[...][None]
 
@@ -1086,6 +1086,14 @@
         normed, _ = layer_norm(values.astype(F32))
         return (normed * gain_one + shift_one + lead_rows[:, None, :]).astype(BF)
 
+    both = w_gate.T
+    head_rows = jnp.concatenate(
+        [
+            jnp.pad(m, ((0, 128 - RESULT_FIELDS), (0, 0)))
+            for m in (both[:RESULT_FIELDS], both[RESULT_FIELDS:], w_bias.T)
+        ]
+    )
+    nothing = jnp.zeros((frames, width, local), F32)
     wq = w_qkv[:, :width]
     wkv = w_qkv[:, width:]
 
@@ -1122,7 +1130,9 @@
         sums = pixel_sums(forecasts, sensitivity)
         m, kv, near = shard_of(place == 0, left, right)
         mixed.append(m)
-        right_two, left_two, kv, *sums = hold(right_two, left_two, kv, *sums)
+        right_two, left_two, kv, nothing, head_rows, *sums = hold(
+            right_two, left_two, kv, nothing, head_rows, *sums
+        )
         key_value.append(kv)
         two = right_two + left_two
         two, middle = hold(two, left)
@@ -1147,13 +1157,6 @@
         attended, logs = attend(queries, key_value, None, True)
     inputs = source.reshape(rows, width)
     attended_low = attended.reshape(rows, width)
-    both = w_gate.T
-    head_rows = jnp.concatenate(
-        [
-            jnp.pad(m, ((0, 128 - RESULT_FIELDS), (0, 0)))
-            for m in (both[:RESULT_FIELDS], both[RESULT_FIELDS:], w_bias.T)
-        ]
-    )
     mask = pad_lanes(field_selector.astype(F32))[:, None]
     (
         hidden_low,
@@ -1199,8 +1202,6 @@
     def back(shard, place, before):
         return attend_back(queries, grad_attended, attended, logs, shard, w_qkv, place, before)
 
-    nothing = jnp.zeros((frames, width, local), F32)
-
     def late_vectors(sums):
         gain_column = sum(jnp.sum(s[:, 0], axis=0) for s in sums)
         column = sum(s[:, 1] for s in sums)

time: 345 us -> 341 us (0.988)
  transfers between devices with their start and end apart: 32 -> 32, of which waited for: 10 -> 11; matrix products, arithmetic and copies ran while one was open for 8% -> 8% of each run, Pallas kernels for 40% -> 41%
where the time goes in v2:
time: 341 us; the launch traced here: 335 us
  Pallas kernels  226 us (66%)
  starting transfers between devices  44 us (13%)
  waiting for transfers between devices  26.2 us (8%)
  other arithmetic  20.9 us (6%)
  local copies, waits for them, and re-layouts  15.3 us (4%)
    pallas_call x4, Pallas kernels, attend_back(): pl.pallas_call(attend_back_kernel, grid=(frames, pairs), in_specs=in_spec...  62.2 us
    pallas_call x1, Pallas kernels, between(): pl.pallas_call(between_kernel, grid=(rows // block,), in_specs=[row(width...  28.5 us
    pallas_call x2, Pallas kernels, attend(): pl.pallas_call(functools.partial(attend_kernel, count, chained, final), g...  27.7 us
    pallas_call x6, Pallas kernels, block_sums(): pl.pallas_call(functools.partial(block_sums_kernel, counts, dealt), grid_...  24.9 us
    ppermute x22, starting transfers between devices, swap(): return lax.ppermute(values, axis, [(i, i ^ bit) for i in range(count)])  22.2 us
    pallas_call x4, Pallas kernels, project(): pl.pallas_call(functools.partial(project_kernel, own), grid=(rows // bloc...  21 us
    ppermute x22, waiting for transfers between devices, swap(): return lax.ppermute(values, axis, [(i, i ^ bit) for i in range(count)])  16.6 us
    pallas_call x1, Pallas kernels, late_grads(): pl.pallas_call(functools.partial(late_grads_kernel, count), grid=(3 * thi...  13.4 us
  transfers between devices with their start and end apart: 32, of which 11 were waited for; matrix products, arithmetic and copies ran while one was open for 8% of the time, Pallas kernels for 41%

profile of v2, /device:TPU:0, one launch (start us, length us, event | category | flops | bytes accessed | tf_op | source)
XLA Modules:
  0.0 335.2 jit_solution(3982499638072890111)
XLA Ops:
  0.7 5.1 %collective-permute-start = (bf16[1,512,768]{2,1,0:T(8,128)(2,1)}, bf16[1,512,768]{2,1,0:T(8,128)(2,1)S(1)}, u32[]{:S(2)}, u32[]{:S(2)}) collective-permute-start(bf16[1,512,768]{2,1,0:T(8,128)(2,1)} %bitcast.80), channel_id=1, source_target_pairs={{0,1},{1,2},{2,3},{4,5},{5,6},{6,7},{8,9},{9,10},{10,11},{12,13},{... | collective-permute-start | bytes 2359304 | tf_op jit(solution)/shard_map/ppermute | solution.py:1074
  7.8 8.3 %copy.41 = bf16[1,32,16,2,4416]{4,2,1,3,0:T(8,128)(2,1)} copy(bf16[1,32,16,2,4416]{4,3,2,1,0:T(2,128)(2,1)} %param.21) | data formatting | bytes 18087936 | tf_op args[3]
  16.8 5.8 %project.4 = (bf16[512,768]{1,0:T(8,128)(2,1)}, bf16[512,1536]{1,0:T(8,128)(2,1)}, bf16[512,768]{1,0:T(8,128)(2,1)}) custom-call(bf16[512,768]{1,0:T(8,128)(2,1)} %bitcast.82, f32[768]{0:T(1024)} %refs_3_.5, f32[768]{0:T(1024)} %refs_4_.7, f32[1,768]{1,0:T(1,128)} %fusion.15.refs_3_.refs_5_, bf16[768,2304]{1,0:T(8,128)(2,1)} %w_ref.1, ...), custom_call_target="tpu_custom_call" | custom-call | flops 301989888 | bytes 393216 | tf_op jit(solution)/shard_map/project/pallas_call | solution.py:65
  22.9 4.1 %collective-permute-done.1 = bf16[1,512,768]{2,1,0:T(8,128)(2,1)S(1)} collective-permute-done((bf16[1,512,768]{2,1,0:T(8,128)(2,1)}, bf16[1,512,768]{2,1,0:T(8,128)(2,1)S(1)}, u32[]{:S(2)}, u32[]{:S(2)}) %collective-permute-start.1) | collective-permute-done | bytes 786464 | tf_op jit(solution)/shard_map/ppermute | solution.py:1075
  30.0 10.3 %pixel_sums.1 = (f32[512,128]{1,0:T(8,128)}, f32[512,128]{1,0:T(8,128)}, f32[512,128]{1,0:T(8,128)}) custom-call(bf16[2,512,4416]{2,1,0:T(8,128)(2,1)} %bitcast.78, bf16[512,4416]{1,0:T(8,128)(2,1)} %bitcast.122), custom_call_target="tpu_custom_call" | custom-call | flops 289406976 | bytes 2260992 | tf_op jit(solution)/shard_map/pixel_sums/pallas_call | solution.py:957
  40.3 5.1 %project.5 = (bf16[512,768]{1,0:T(8,128)(2,1)}, bf16[512,1536]{1,0:T(8,128)(2,1)}, bf16[512,768]{1,0:T(8,128)(2,1)}) custom-call(s32[1]{0:T(128)} %bitcast.7.refs_0_, bf16[512,768]{1,0:T(8,128)(2,1)} %bitcast.123, bf16[512,768]{1,0:T(8,128)(2,1)} %bitcast.130, f32[768]{0:T(1024)} %refs_3_.5, f32[768]{0:T(1024)} %refs_4_.7, f32[1,768]{1,0:T(1,128)} %fusion.15.refs_3_.refs_5_, ...), custom_call_target="tpu_custom_call" | custom-call | flops 301989888 | bytes 393216 | tf_op jit(solution)/shard_map/project/pallas_call | solution.py:65
  45.4 4.6 %collective-permute-done.3 = bf16[1,512,768]{2,1,0:T(8,128)(2,1)S(1)} collective-permute-done((bf16[1,512,768]{2,1,0:T(8,128)(2,1)S(1)}, bf16[1,512,768]{2,1,0:T(8,128)(2,1)S(1)}, u32[]{:S(2)}, u32[]{:S(2)}) %collective-permute-start.3) | collective-permute-done | bytes 786464 | tf_op jit(solution)/shard_map/ppermute | solution.py:1129
  52.3 5.1 %project.6 = (bf16[512,768]{1,0:T(8,128)(2,1)}, bf16[512,1536]{1,0:T(8,128)(2,1)}, bf16[512,768]{1,0:T(8,128)(2,1)}) custom-call(s32[1]{0:T(128)} %bitcast.15.refs_0_, bf16[512,768]{1,0:T(8,128)(2,1)} %bitcast.119, bf16[512,768]{1,0:T(8,128)(2,1)} %bitcast.124, f32[768]{0:T(1024)} %refs_3_.5, f32[768]{0:T(1024)} %refs_4_.7, ...), custom_call_target="tpu_custom_call" | custom-call | flops 301989888 | bytes 393216 | tf_op jit(solution)/shard_map/project/pallas_call | solution.py:65
  57.4 18.2 %attend.2 = (f32[1,768,512]{2,1,0:T(8,128)}, f32[1,6,2,512]{3,2,1,0:T(2,128)}) custom-call(bf16[1,512,768]{2,1,0:T(8,128)(2,1)} %bitcast.93, bf16[1,512,1536]{2,1,0:T(8,128)(2,1)} %bitcast.99, bf16[1,512,1536]{2,1,0:T(8,128)(2,1)} %bitcast.103, bf16[1,512,1536]{2,1,0:T(8,128)(2,1)} %bitcast.107, bf16[1,512,1536]{2,1,0:T(8,128)(2,1)} %bitcast.100, ...), custom_call_target="tpu_custom_call" | custom-call | flops 1207959552 | bytes 393216 | tf_op jit(solution)/shard_map/attend/pallas_call | solution.py:137
  76.5 5.1 %project.7 = (bf16[512,768]{1,0:T(8,128)(2,1)}, bf16[512,1536]{1,0:T(8,128)(2,1)}, bf16[512,768]{1,0:T(8,128)(2,1)}) custom-call(s32[1]{0:T(128)} %bitcast.15.refs_0_, bf16[512,768]{1,0:T(8,128)(2,1)} %bitcast.129, bf16[512,768]{1,0:T(8,128)(2,1)} %bitcast.120, f32[768]{0:T(1024)} %refs_3_.5, f32[768]{0:T(1024)} %refs_4_.7, ...), custom_call_target="tpu_custom_call" | custom-call | flops 301989888 | bytes 393216 | tf_op jit(solution)/shard_map/project/pallas_call | solution.py:65
  81.5 9.5 %attend.3 = (bf16[1,512,768]{2,1,0:T(8,128)(2,1)}, f32[1,6,2,512]{3,2,1,0:T(2,128)}) custom-call(bf16[1,512,768]{2,1,0:T(8,128)(2,1)} %bitcast.94, bf16[1,512,1536]{2,1,0:T(8,128)(2,1)} %bitcast.111, bf16[1,512,1536]{2,1,0:T(8,128)(2,1)} %bitcast.112, f32[1,768,512]{2,1,0:T(8,128)} %get-tuple-element.207.refs_3_, f32[1,6,2,512]{3,2,1,0:T(2,128)} %get-tuple-element.208.refs_4_), custom_call_target="tpu_custom_call" | custom-call | flops 402653184 | bytes 393216 | tf_op jit(solution)/shard_map/attend/pallas_call | solution.py:137
  91.1 28.5 %between.1 = (bf16[512,768]{1,0:T(8,128)(2,1)}, bf16[512,3072]{1,0:T(8,128)(2,1)}, bf16[512,3072]{1,0:T(8,128)(2,1)}, bf16[512,768]{1,0:T(8,128)(2,1)}, bf16[512...) custom-call(bf16[512,768]{1,0:T(8,128)(2,1)} %bitcast.83, ...), custom_call_target="tpu_custom_call" | custom-call | flops 1207959552 | bytes 1572864 | tf_op jit(solution)/shard_map/between/pallas_call | solution.py:444
  124.3 8.6 %down_grads.1 = (bf16[8,48,7168]{2,1,0:T(8,128)(2,1)}, bf16[8,48,7168]{2,1,0:T(8,128)(2,1)}) custom-call(s32[1]{0:T(128)} %bitcast.3.place_ref, bf16[512,3072]{1,0:T(8,128)(2,1)} %get-tuple-element.222.act_ref, bf16[512,768]{1,0:T(8,128)(2,1)} %get-tuple-element.223.down_ref), custom_call_target="tpu_custom_call" | custom-call | flops 301989888 | bytes 294912 | tf_op jit(solution)/shard_map/down_grads/pallas_call | solution.py:623
  132.9 10.6 %early_grads.1 = (bf16[8,48,7168]{2,1,0:T(8,128)(2,1)}, bf16[8,48,7168]{2,1,0:T(8,128)(2,1)}) custom-call(s32[1]{0:T(128)} %bitcast.3.place_ref, bf16[512,768]{1,0:T(8,128)(2,1)} %get-tuple-element.215.h_ref, bf16[512,768]{1,0:T(8,128)(2,1)} %bitcast.92, bf16[512,768]{1,0:T(8,128)(2,1)} %get-tuple-element.216.f_ref, ...), custom_call_target="tpu_custom_call", output_to_operand_aliasing={{0}: (8, {}), {1}: (9, {})} | custom-call | flops 3221225472 | bytes 10485760 | tf_op jit(solution)/shard_map/early_grads/pallas_call | solution.py:567
  145.5 15.5 %attend_back.4 = (f32[1,768,512]{2,1,0:T(8,128)}, bf16[1,512,1536]{2,1,0:T(8,128)(2,1)}, bf16[1,512,768]{2,1,0:T(8,128)(2,1)}, f32[1,2,768]{2,1,0:T(2,128)}) custom-call(bf16[1,512,768]{2,1,0:T(8,128)(2,1)} %bitcast.95, bf16[1,512,768]{2,1,0:T(8,128)(2,1)} %bitcast.115, ...), custom_call_target="tpu_custom_call", output_to_operand_aliasing={{0}: (9, {})} | custom-call | flops 805306368 | bytes 393216 | tf_op jit(solution)/shard_map/attend_back/pallas_call | solution.py:252
  160.9 4.6 %block_sums.6 = (bf16[4,2,24,3584]{3,2,1,0:T(8,128)(2,1)}, bf16[2,4,24,3584]{3,2,1,0:T(8,128)(2,1)}) custom-call(s32[3]{0:T(128)} %pad_add_fusion.where_ref, bf16[2,4,2,24,7168]{4,3,2,1,0:T(8,128)(2,1)} %bitcast.72, bf16[2,4,2,24,7168]{4,3,2,1,0:T(8,128)(2,1)} %bitcast.33.refs_1_.refs_3_.refs_4_.refs_5_, bf16[2,4,2,24,7168]{4,3,2,1,0:T(8,128)(2,1)} %bitcast.73, ...), custom_call_target="tpu_custom_call" | custom-call | flops 1048576 | bytes 1048576 | tf_op jit(solution)/shard_map/block_sums/pallas_call | solution.py:734
  165.5 4.6 %collective-permute-start.6 = (bf16[1,512,768]{2,1,0:T(8,128)(2,1)}, bf16[1,512,768]{2,1,0:T(8,128)(2,1)S(1)}, u32[]{:S(2)}, u32[]{:S(2)}) collective-permute-start(bf16[1,512,768]{2,1,0:T(8,128)(2,1)} %get-tuple-element.242), channel_id=1, source_target_pairs={{0,1},{3,2},{4,5},{7,6},{8,9},{11,10},{12,13},{15,14},{16,17},{19,... | collective-permute-start | bytes 2359304 | tf_op jit(solution)/shard_map/ppermute | solution.py:1241
  173.3 15.6 %attend_back.5 = (f32[1,768,512]{2,1,0:T(8,128)}, bf16[1,512,1536]{2,1,0:T(8,128)(2,1)}, bf16[1,512,768]{2,1,0:T(8,128)(2,1)}, f32[1,2,768]{2,1,0:T(2,128)}) custom-call(bf16[1,512,768]{2,1,0:T(8,128)(2,1)} %bitcast.96, bf16[1,512,768]{2,1,0:T(8,128)(2,1)} %bitcast.116, ...), custom_call_target="tpu_custom_call", output_to_operand_aliasing={{0}: (9, {})} | custom-call | flops 805306368 | bytes 393216 | tf_op jit(solution)/shard_map/attend_back/pallas_call | solution.py:252
  191.2 3.1 collective-permute-start.7
  195.9 15.5 %attend_back.6 = (f32[1,768,512]{2,1,0:T(8,128)}, bf16[1,512,1536]{2,1,0:T(8,128)(2,1)}, bf16[1,512,768]{2,1,0:T(8,128)(2,1)}, f32[1,2,768]{2,1,0:T(2,128)}) custom-call(bf16[1,512,768]{2,1,0:T(8,128)(2,1)} %bitcast.97, bf16[1,512,768]{2,1,0:T(8,128)(2,1)} %bitcast.117, ...), custom_call_target="tpu_custom_call", output_to_operand_aliasing={{0}: (9, {})} | custom-call | flops 805306368 | bytes 393216 | tf_op jit(solution)/shard_map/attend_back/pallas_call | solution.py:252
  211.4 3.9 %block_sums.7 = (bf16[4,24,3584]{2,1,0:T(8,128)(2,1)}, bf16[4,24,3584]{2,1,0:T(8,128)(2,1)}) custom-call(s32[3]{0:T(128)} %pad_add_fusion.where_ref, bf16[2,4,2,24,7168]{4,3,2,1,0:T(8,128)(2,1)} %bitcast.74, bf16[2,4,2,24,7168]{4,3,2,1,0:T(8,128)(2,1)} %bitcast.33.refs_1_.refs_3_.refs_4_.refs_5_, bf16[4,2,24,3584]{3,2,1,0:T(8,128)(2,1)} %collective-permute-done.9.refs_2_, ...), custom_call_target="tpu_custom_call" | custom-call | flops 1048576 | bytes 1048576 | tf_op jit(solution)/shard_map/block_sums/pallas_call | solution.py:734
  224.5 15.6 %attend_back.7 = (f32[1,768,512]{2,1,0:T(8,128)}, bf16[1,512,1536]{2,1,0:T(8,128)(2,1)}, bf16[1,512,768]{2,1,0:T(8,128)(2,1)}, f32[1,2,768]{2,1,0:T(2,128)}) custom-call(bf16[1,512,768]{2,1,0:T(8,128)(2,1)} %bitcast.98, bf16[1,512,768]{2,1,0:T(8,128)(2,1)} %bitcast.118, ...), custom_call_target="tpu_custom_call", output_to_operand_aliasing={{0}: (9, {})} | custom-call | flops 805306368 | bytes 393216 | tf_op jit(solution)/shard_map/attend_back/pallas_call | solution.py:252
  240.8 4.4 %query_back.1 = (bf16[1,768,512]{2,1,0:T(8,128)(2,1)}, f32[1,512,768]{2,1,0:T(8,128)}, f32[1,2,768]{2,1,0:T(2,128)}) custom-call(f32[1,768,512]{2,1,0:T(8,128)} %get-tuple-element.260.dq_ref, bf16[768,2304]{1,0:T(8,128)(2,1)} %w_ref.1, bf16[1,512,768]{2,1,0:T(8,128)(2,1)} %bitcast.85), custom_call_target="tpu_custom_call" | custom-call | flops 301989888 | bytes 393216 | tf_op jit(solution)/shard_map/query_back/pallas_call | solution.py:283
  246.8 13.4 %late_grads.1 = (bf16[8,48,2560]{2,1,0:T(8,128)(2,1)}, bf16[8,48,2560]{2,1,0:T(8,128)(2,1)}) custom-call(s32[1]{0:T(128)} %bitcast.3.place_ref, bf16[512,768]{1,0:T(8,128)(2,1)} %get-tuple-element.182.refs_0_, bf16[512,768]{1,0:T(8,128)(2,1)} %get-tuple-element.187.refs_1_, bf16[512,768]{1,0:T(8,128)(2,1)} %get-tuple-element.197.refs_2_, ...), custom_call_target="tpu_custom_call" | custom-call | flops 5435817984 | bytes 19660800 | tf_op jit(solution)/shard_map/late_grads/pallas_call | solution.py:678
  260.4 5.7 %block_sums.8 = (bf16[2,24,3584]{2,1,0:T(8,128)(2,1)}, bf16[2,24,3584]{2,1,0:T(8,128)(2,1)}, bf16[2,24,3584]{2,1,0:T(8,128)(2,1)}, bf16[2,24,3584]{2,1,0:T(8,128)(2,1)}) custom-call(s32[3]{0:T(128)} %pad_add_fusion.where_ref, bf16[2,4,2,24,7168]{4,3,2,1,0:T(8,128)(2,1)} %bitcast.76, bf16[2,4,2,24,7168]{4,3,2,1,0:T(8,128)(2,1)} %bitcast.33.refs_1_.refs_3_.refs_4_.refs_5_, ...), custom_call_target="tpu_custom_call" | custom-call | flops 1048576 | bytes 1048576 | tf_op jit(solution)/shard_map/block_sums/pallas_call | solution.py:734
  266.1 3.2 block_sums.9
  278.4 9.3 %blend.1 = bf16[512,4416]{1,0:T(8,128)(2,1)} custom-call(f32[512,128]{1,0:T(8,128)} %get-tuple-element.292.a_ref, f32[512,128]{1,0:T(8,128)} %get-tuple-element.293.b_ref, f32[512,128]{1,0:T(8,128)} %get-tuple-element.294.c_ref, bf16[2,512,4416]{2,1,0:T(8,128)(2,1)} %bitcast.79), custom_call_target="tpu_custom_call" | custom-call | flops 289406976 | bytes 2260992 | tf_op jit(solution)/shard_map/blend/pallas_call | solution.py:996
  287.8 3.0 block_sums.10
  291.8 3.3 fusion.21
  298.2 4.5 %block_sums.11 = (bf16[1,24,2560]{2,1,0:T(8,128)(2,1)}, bf16[1,24,2560]{2,1,0:T(8,128)(2,1)}, bf16[1,24,2560]{2,1,0:T(8,128)(2,1)}, bf16[1,24,2560]{2,1,0:T(8,128)(2,1)}) custom-call(s32[3]{0:T(128)} %pad_add_fusion.where_ref, bf16[2,4,2,24,2560]{4,3,2,1,0:T(8,128)(2,1)} %bitcast.90, bf16[2,4,2,24,2560]{4,3,2,1,0:T(8,128)(2,1)} %bitcast.43.refs_1_.refs_3_.refs_4_, ...), custom_call_target="tpu_custom_call" | custom-call | flops 1048576 | bytes 1048576 | tf_op jit(solution)/shard_map/block_sums/pallas_call | solution.py:734
  305.7 4.9 %collective-permute-done.20 = bf16[1,24,2560]{2,1,0:T(8,128)(2,1)S(1)} collective-permute-done((bf16[1,24,2560]{2,1,0:T(8,128)(2,1)}, bf16[1,24,2560]{2,1,0:T(8,128)(2,1)S(1)}, u32[]{:S(2)}, u32[]{:S(2)}) %collective-permute-start.20) | collective-permute-done | bytes 122912 | tf_op jit(solution)/shard_map/ppermute | solution.py:1013
  318.8 7.2 %collective-permute-done.28.refs_1_ = bf16[24,2560]{1,0:T(8,128)(2,1)S(1)} collective-permute-done((bf16[24,2560]{1,0:T(8,128)(2,1)S(1)}, bf16[24,2560]{1,0:T(8,128)(2,1)S(1)}, u32[]{:S(2)}, u32[]{:S(2)}) %collective-permute-start.28) | collective-permute-done | bytes 122912 | tf_op jit(solution)/shard_map/ppermute | solution.py:1013
  (166 shorter events, 66.9 us)
Async XLA Ops:
  0.7 22.2 %collective-permute-start = (bf16[1,512,768]{2,1,0:T(8,128)(2,1)}, bf16[1,512,768]{2,1,0:T(8,128)(2,1)S(1)}, u32[]{:S(2)}, u32[]{:S(2)}) collective-permute-start(bf16[1,512,768]{2,1,0:T(8,128)(2,1)} %bitcast.80), channel_id=1, source_target_pairs={{0,1},{1,2},{2,3},{4,5},{5,6},{6,7},{8,9},{9,10},{10,11},{12,13},{... | collective-permute-start | bytes 2359304 | tf_op jit(solution)/shard_map/ppermute | solution.py:1074
  5.8 21.1 %collective-permute-start.1 = (bf16[1,512,768]{2,1,0:T(8,128)(2,1)}, bf16[1,512,768]{2,1,0:T(8,128)(2,1)S(1)}, u32[]{:S(2)}, u32[]{:S(2)}) collective-permute-start(bf16[1,512,768]{2,1,0:T(8,128)(2,1)} %bitcast.81), channel_id=1, source_target_pairs={{3,2},{2,1},{1,0},{7,6},{6,5},{5,4},{11,10},{10,9},{9,8},{15,14},{... | collective-permute-start | bytes 2359304 | tf_op jit(solution)/shard_map/ppermute | solution.py:1075
  26.9 18.5 %collective-permute-start.2 = (bf16[1,512,768]{2,1,0:T(8,128)(2,1)S(1)}, bf16[1,512,768]{2,1,0:T(8,128)(2,1)S(1)}, u32[]{:S(2)}, u32[]{:S(2)}) collective-permute-start(bf16[1,512,768]{2,1,0:T(8,128)(2,1)S(1)} %collective-permute-done), channel_id=1, source_target_pairs={{1,2},{2,3},{5,6},{6,7},{9,10},{10,11},{13,14},{14,15},{17,18},{18... | collective-permute-start | bytes 2359304 | tf_op jit(solution)/shard_map/ppermute | solution.py:1128
  27.6 22.4 %collective-permute-start.3 = (bf16[1,512,768]{2,1,0:T(8,128)(2,1)S(1)}, bf16[1,512,768]{2,1,0:T(8,128)(2,1)S(1)}, u32[]{:S(2)}, u32[]{:S(2)}) collective-permute-start(bf16[1,512,768]{2,1,0:T(8,128)(2,1)S(1)} %collective-permute-done.1), channel_id=1, source_target_pairs={{2,1},{1,0},{6,5},{5,4},{10,9},{9,8},{14,13},{13,12},{18,17},{17,1... | collective-permute-start | bytes 2359304 | tf_op jit(solution)/shard_map/ppermute | solution.py:1129
  50.2 25.4 %collective-permute-start.4 = (bf16[1,512,768]{2,1,0:T(8,128)(2,1)S(1)}, bf16[1,512,768]{2,1,0:T(8,128)(2,1)S(1)}, u32[]{:S(2)}, u32[]{:S(2)}) collective-permute-start(bf16[1,512,768]{2,1,0:T(8,128)(2,1)S(1)} %add.184), channel_id=1, source_target_pairs={{2,3},{1,0},{6,7},{5,4},{10,11},{9,8},{14,15},{13,12},{18,19},{17,... | collective-permute-start | bytes 2359304 | tf_op jit(solution)/shard_map/ppermute | solution.py:1139
  143.5 17.4 %collective-permute-start.5 = (bf16[8,48,7168]{2,1,0:T(8,128)(2,1)}, bf16[8,48,7168]{2,1,0:T(8,128)(2,1)}, u32[]{:S(2)}, u32[]{:S(2)}) collective-permute-start(bf16[8,48,7168]{2,1,0:T(8,128)(2,1)} %get-tuple-element.236), channel_id=1, source_target_pairs={{0,8},{8,0},{16,24},{24,16},{1,9},{9,1},{17,25},{25,17},{2,10},{10... | collective-permute-start | bytes 16515080 | tf_op jit(solution)/shard_map/ppermute | solution.py:1013
  165.5 23.3 %collective-permute-start.6 = (bf16[1,512,768]{2,1,0:T(8,128)(2,1)}, bf16[1,512,768]{2,1,0:T(8,128)(2,1)S(1)}, u32[]{:S(2)}, u32[]{:S(2)}) collective-permute-start(bf16[1,512,768]{2,1,0:T(8,128)(2,1)} %get-tuple-element.242), channel_id=1, source_target_pairs={{0,1},{3,2},{4,5},{7,6},{8,9},{11,10},{12,13},{15,14},{16,17},{19,... | collective-permute-start | bytes 2359304 | tf_op jit(solution)/shard_map/ppermute | solution.py:1241
  170.2 41.2 %collective-permute-start.9 = (bf16[4,2,24,3584]{3,2,1,0:T(8,128)(2,1)}, bf16[4,2,24,3584]{3,2,1,0:T(8,128)(2,1)}, u32[]{:S(2)}, u32[]{:S(2)}) collective-permute-start(bf16[4,2,24,3584]{3,2,1,0:T(8,128)(2,1)} %get-tuple-element.247), channel_id=1, source_target_pairs={{0,4},{4,0},{1,5},{5,1},{2,6},{6,2},{3,7},{7,3},{8,12},{12,8},{9,1... | collective-permute-start | bytes 4128776 | tf_op jit(solution)/shard_map/ppermute | solution.py:1013
  171.7 39.6 %collective-permute-start.10 = (bf16[2,4,24,3584]{3,2,1,0:T(8,128)(2,1)}, bf16[2,4,24,3584]{3,2,1,0:T(8,128)(2,1)}, u32[]{:S(2)}, u32[]{:S(2)}) collective-permute-start(bf16[2,4,24,3584]{3,2,1,0:T(8,128)(2,1)} %get-tuple-element.248), channel_id=1, source_target_pairs={{0,16},{8,24},{16,0},{24,8},{1,17},{9,25},{17,1},{25,9},{2,18},{10... | collective-permute-start | bytes 4128776 | tf_op jit(solution)/shard_map/ppermute | solution.py:1013
  191.2 24.0 %collective-permute-start.7 = (bf16[1,512,768]{2,1,0:T(8,128)(2,1)}, bf16[1,512,768]{2,1,0:T(8,128)(2,1)}, u32[]{:S(2)}, u32[]{:S(2)}) collective-permute-start(bf16[1,512,768]{2,1,0:T(8,128)(2,1)} %fusion.5), channel_id=1, source_target_pairs={{0,1},{1,2},{4,5},{5,6},{8,9},{9,10},{12,13},{13,14},{16,17},{17,1... | collective-permute-start | bytes 2359304 | tf_op jit(solution)/shard_map/ppermute | solution.py:1247
  194.3 22.9 %collective-permute-start.8 = (bf16[1,512,768]{2,1,0:T(8,128)(2,1)}, bf16[1,512,768]{2,1,0:T(8,128)(2,1)}, u32[]{:S(2)}, u32[]{:S(2)}) collective-permute-start(bf16[1,512,768]{2,1,0:T(8,128)(2,1)} %fusion.5), channel_id=1, source_target_pairs={{3,2},{2,1},{7,6},{6,5},{11,10},{10,9},{15,14},{14,13},{19,18},{18... | collective-permute-start | bytes 2359304 | tf_op jit(solution)/shard_map/ppermute | solution.py:1248
  218.6 21.5 %collective-permute-start.11 = (bf16[1,512,768]{2,1,0:T(8,128)(2,1)S(1)}, bf16[1,512,768]{2,1,0:T(8,128)(2,1)S(1)}, u32[]{:S(2)}, u32[]{:S(2)}) collective-permute-start(bf16[1,512,768]{2,1,0:T(8,128)(2,1)S(1)} %fusion.6), channel_id=1, source_target_pairs={{0,1},{1,2},{2,3},{4,5},{5,6},{6,7},{8,9},{9,10},{10,11},{12,13},{... | collective-permute-start | bytes 2359304 | tf_op jit(solution)/shard_map/ppermute | solution.py:1256
  220.0 20.8 %collective-permute-start.12 = (bf16[1,512,768]{2,1,0:T(8,128)(2,1)S(1)}, bf16[1,512,768]{2,1,0:T(8,128)(2,1)S(1)}, u32[]{:S(2)}, u32[]{:S(2)}) collective-permute-start(bf16[1,512,768]{2,1,0:T(8,128)(2,1)S(1)} %add_convert_fusion), channel_id=1, source_target_pairs={{3,2},{2,1},{1,0},{7,6},{6,5},{5,4},{11,10},{10,9},{9,8},{15,14},{... | collective-permute-start | bytes 2359304 | tf_op jit(solution)/shard_map/ppermute | solution.py:1257
  221.3 18.8 %collective-permute-start.13 = (bf16[4,24,3584]{2,1,0:T(8,128)(2,1)}, bf16[4,24,3584]{2,1,0:T(8,128)(2,1)S(1)}, u32[]{:S(2)}, u32[]{:S(2)}) collective-permute-start(bf16[4,24,3584]{2,1,0:T(8,128)(2,1)} %get-tuple-element.258), channel_id=1, source_target_pairs={{0,16},{8,24},{16,0},{24,8},{1,17},{9,25},{17,1},{25,9},{2,18},{10... | collective-permute-start | bytes 2064392 | tf_op jit(solution)/shard_map/ppermute | solution.py:1013
  222.9 17.3 %collective-permute-start.14 = (bf16[4,24,3584]{2,1,0:T(8,128)(2,1)}, bf16[4,24,3584]{2,1,0:T(8,128)(2,1)}, u32[]{:S(2)}, u32[]{:S(2)}) collective-permute-start(bf16[4,24,3584]{2,1,0:T(8,128)(2,1)} %get-tuple-element.259), channel_id=1, source_target_pairs={{0,4},{4,0},{1,5},{5,1},{2,6},{6,2},{3,7},{7,3},{8,12},{12,8},{9,1... | collective-permute-start | bytes 2064392 | tf_op jit(solution)/shard_map/ppermute | solution.py:1013
  260.2 5.9 %collective-permute-start.15 = (bf16[8,48,2560]{2,1,0:T(8,128)(2,1)}, bf16[8,48,2560]{2,1,0:T(8,128)(2,1)}, u32[]{:S(2)}, u32[]{:S(2)}) collective-permute-start(bf16[8,48,2560]{2,1,0:T(8,128)(2,1)} %get-tuple-element.277), channel_id=1, source_target_pairs={{0,8},{8,0},{16,24},{24,16},{1,9},{9,1},{17,25},{25,17},{2,10},{10... | collective-permute-start | bytes 5898248 | tf_op jit(solution)/shard_map/ppermute | solution.py:1013
  269.3 18.4 %collective-permute-start.16 = (bf16[2,2,24,2560]{3,2,1,0:T(8,128)(2,1)}, bf16[2,2,24,2560]{3,2,1,0:T(8,128)(2,1)}, u32[]{:S(2)}, u32[]{:S(2)}) collective-permute-start(bf16[2,2,24,2560]{3,2,1,0:T(8,128)(2,1)} %get-tuple-element.290), channel_id=1, source_target_pairs={{0,4},{4,0},{1,5},{5,1},{2,6},{6,2},{3,7},{7,3},{8,12},{12,8},{9,1... | collective-permute-start | bytes 1474568 | tf_op jit(solution)/shard_map/ppermute | solution.py:1013
  270.8 16.9 %collective-permute-start.17 = (bf16[2,2,24,2560]{3,2,1,0:T(8,128)(2,1)}, bf16[2,2,24,2560]{3,2,1,0:T(8,128)(2,1)}, u32[]{:S(2)}, u32[]{:S(2)}) collective-permute-start(bf16[2,2,24,2560]{3,2,1,0:T(8,128)(2,1)} %get-tuple-element.291), channel_id=1, source_target_pairs={{0,16},{8,24},{16,0},{24,8},{1,17},{9,25},{17,1},{25,9},{2,18},{10... | collective-permute-start | bytes 1474568 | tf_op jit(solution)/shard_map/ppermute | solution.py:1013
  274.0 38.7 %collective-permute-start.24 = (bf16[2,24,3584]{2,1,0:T(8,128)(2,1)}, bf16[2,24,3584]{2,1,0:T(8,128)(2,1)}, u32[]{:S(2)}, u32[]{:S(2)}) collective-permute-start(bf16[2,24,3584]{2,1,0:T(8,128)(2,1)} %get-tuple-element.323), channel_id=1, source_target_pairs={{0,3},{1,2},{2,1},{3,0},{4,7},{5,6},{6,5},{7,4},{8,11},{9,10},{10,... | collective-permute-start | bytes 1032200 | tf_op jit(solution)/shard_map/ppermute | solution.py:1013
  275.4 37.3 %collective-permute-start.23 = (bf16[2,24,3584]{2,1,0:T(8,128)(2,1)}, bf16[2,24,3584]{2,1,0:T(8,128)(2,1)}, u32[]{:S(2)}, u32[]{:S(2)}) collective-permute-start(bf16[2,24,3584]{2,1,0:T(8,128)(2,1)} %get-tuple-element.322), channel_id=1, source_target_pairs={{0,2},{1,3},{2,0},{3,1},{4,6},{5,7},{6,4},{7,5},{8,10},{9,11},{10,... | collective-permute-start | bytes 1032200 | tf_op jit(solution)/shard_map/ppermute | solution.py:1013
  277.1 35.7 %collective-permute-start.22 = (bf16[2,24,3584]{2,1,0:T(8,128)(2,1)}, bf16[2,24,3584]{2,1,0:T(8,128)(2,1)}, u32[]{:S(2)}, u32[]{:S(2)}) collective-permute-start(bf16[2,24,3584]{2,1,0:T(8,128)(2,1)} %get-tuple-element.321), channel_id=1, source_target_pairs={{0,1},{1,0},{2,3},{3,2},{4,5},{5,4},{6,7},{7,6},{8,9},{9,8},{10,11... | collective-permute-start | bytes 1032200 | tf_op jit(solution)/shard_map/ppermute | solution.py:1013
  290.8 7.3 %collective-permute-start.18 = (bf16[2,24,2560]{2,1,0:T(8,128)(2,1)}, bf16[2,24,2560]{2,1,0:T(8,128)(2,1)}, u32[]{:S(2)}, u32[]{:S(2)}) collective-permute-start(bf16[2,24,2560]{2,1,0:T(8,128)(2,1)} %get-tuple-element.302), channel_id=1, source_target_pairs={{0,16},{8,24},{16,0},{24,8},{1,17},{9,25},{17,1},{25,9},{2,18},{10... | collective-permute-start | bytes 737288 | tf_op jit(solution)/shard_map/ppermute | solution.py:1013
  291.2 7.0 %collective-permute-start.19 = (bf16[2,24,2560]{2,1,0:T(8,128)(2,1)}, bf16[2,24,2560]{2,1,0:T(8,128)(2,1)}, u32[]{:S(2)}, u32[]{:S(2)}) collective-permute-start(bf16[2,24,2560]{2,1,0:T(8,128)(2,1)} %get-tuple-element.303), channel_id=1, source_target_pairs={{0,4},{4,0},{1,5},{5,1},{2,6},{6,2},{3,7},{7,3},{8,12},{12,8},{9,1... | collective-permute-start | bytes 737288 | tf_op jit(solution)/shard_map/ppermute | solution.py:1013
  302.7 7.9 %collective-permute-start.20 = (bf16[1,24,2560]{2,1,0:T(8,128)(2,1)}, bf16[1,24,2560]{2,1,0:T(8,128)(2,1)S(1)}, u32[]{:S(2)}, u32[]{:S(2)}) collective-permute-start(bf16[1,24,2560]{2,1,0:T(8,128)(2,1)} %get-tuple-element.317), channel_id=1, source_target_pairs={{0,1},{1,0},{2,3},{3,2},{4,5},{5,4},{6,7},{7,6},{8,9},{9,8},{10,11... | collective-permute-start | bytes 368648 | tf_op jit(solution)/shard_map/ppermute | solution.py:1013
  303.7 9.1 %collective-permute-start.21 = (bf16[1,24,2560]{2,1,0:T(8,128)(2,1)}, bf16[1,24,2560]{2,1,0:T(8,128)(2,1)S(1)}, u32[]{:S(2)}, u32[]{:S(2)}) collective-permute-start(bf16[1,24,2560]{2,1,0:T(8,128)(2,1)} %get-tuple-element.318), channel_id=1, source_target_pairs={{0,2},{1,3},{2,0},{3,1},{4,6},{5,7},{6,4},{7,5},{8,10},{9,11},{10,... | collective-permute-start | bytes 368648 | tf_op jit(solution)/shard_map/ppermute | solution.py:1013
  310.6 7.4 %collective-permute-start.27 = (bf16[1,24,2560]{2,1,0:T(8,128)(2,1)}, bf16[1,24,2560]{2,1,0:T(8,128)(2,1)S(1)}, u32[]{:S(2)}, u32[]{:S(2)}) collective-permute-start(bf16[1,24,2560]{2,1,0:T(8,128)(2,1)} %get-tuple-element.327), channel_id=1, source_target_pairs={{0,3},{1,2},{2,1},{3,0},{4,7},{5,6},{6,5},{7,4},{8,11},{9,10},{10,... | collective-permute-start | bytes 368648 | tf_op jit(solution)/shard_map/ppermute | solution.py:1013
  314.2 11.8 %collective-permute-start.25 = (bf16[2,24,3584]{2,1,0:T(8,128)(2,1)S(1)}, bf16[2,24,3584]{2,1,0:T(8,128)(2,1)S(1)}, u32[]{:S(2)}, u32[]{:S(2)}) collective-permute-start(bf16[2,24,3584]{2,1,0:T(8,128)(2,1)S(1)} %add_convert_fusion.3.refs_0_), channel_id=1, source_target_pairs={{0,16},{8,24},{16,0},{24,8},{1,17},{9,25},{17,1},{25,9},{2,18},{10... | collective-permute-start | bytes 1032200 | tf_op jit(solution)/shard_map/ppermute | solution.py:1013
  315.5 10.5 %collective-permute-start.26 = (bf16[2,24,3584]{2,1,0:T(8,128)(2,1)S(1)}, bf16[2,24,3584]{2,1,0:T(8,128)(2,1)S(1)}, u32[]{:S(2)}, u32[]{:S(2)}) collective-permute-start(bf16[2,24,3584]{2,1,0:T(8,128)(2,1)S(1)} %add_convert_fusion.3.refs_0_), channel_id=1, source_target_pairs={{0,8},{8,0},{16,24},{24,16},{1,9},{9,1},{17,25},{25,17},{2,10},{10... | collective-permute-start | bytes 1032200 | tf_op jit(solution)/shard_map/ppermute | solution.py:1013
  318.1 7.9 %collective-permute-start.28 = (bf16[24,2560]{1,0:T(8,128)(2,1)S(1)}, bf16[24,2560]{1,0:T(8,128)(2,1)S(1)}, u32[]{:S(2)}, u32[]{:S(2)}) collective-permute-start(bf16[24,2560]{1,0:T(8,128)(2,1)S(1)} %fusion.14.refs_0_), channel_id=1, source_target_pairs={{0,16},{8,24},{16,0},{24,8},{1,17},{9,25},{17,1},{25,9},{2,18},{10... | collective-permute-start | bytes 368648 | tf_op jit(solution)/shard_map/ppermute | solution.py:1013
  318.8 7.2 %collective-permute-start.29 = (bf16[24,2560]{1,0:T(8,128)(2,1)S(1)}, bf16[24,2560]{1,0:T(8,128)(2,1)S(1)}, u32[]{:S(2)}, u32[]{:S(2)}) collective-permute-start(bf16[24,2560]{1,0:T(8,128)(2,1)S(1)} %fusion.14.refs_0_), channel_id=1, source_target_pairs={{0,8},{8,0},{16,24},{24,16},{1,9},{9,1},{17,25},{25,17},{2,10},{10... | collective-permute-start | bytes 368648 | tf_op jit(solution)/shard_map/ppermute | solution.py:1013
  326.1 1.7 collective-permute-start.31
  326.1 5.3 %collective-permute-start.30 = (bf16[24,2560]{1,0:T(8,128)(2,1)S(1)}, bf16[24,2560]{1,0:T(8,128)(2,1)S(1)}, u32[]{:S(2)}, u32[]{:S(2)}) collective-permute-start(bf16[24,2560]{1,0:T(8,128)(2,1)S(1)} %collective-permute-done.28.refs_1_), channel_id=1, source_target_pairs={{0,8},{8,0},{16,24},{24,16},{1,9},{9,1},{17,25},{25,17},{2,10},{10... | collective-permute-start | bytes 368648 | tf_op jit(solution)/shard_map/ppermute | solution.py:1013
  (34 other events, 271.3 us)

commit v3 on v2

--- a/solution.py
+++ b/solution.py
@@ -340,7 +340,7 @@
     gain = gain_ref[...][None]
     hidden = (normed * gain + shift_ref[...][None]).astype(BF)
     hidden_ref[...] = hidden
-    wide = 1024
+    wide = 1536
     steps = wu_ref.shape[1] // wide
     sum_ref[...] = residual + bd_ref[...][None]
 
@@ -889,7 +889,7 @@
             for count in (2 * RESULT_FIELDS, RESULT_FIELDS, 1, 1, 1, 4)
         ],
         scratch_shapes=[pltpu.VMEM((4 * rows, 256), F32)],
-        compiler_params=PARAMS,
+        compiler_params=FULL,
         name="early_unpack",
         cost_estimate=pl.CostEstimate(flops=1 << 20, transcendentals=0, bytes_accessed=1 << 20),
     )(place, *pieces)

time: 341 us -> 340 us (level)
    unnamed x69 -> x63, local copies, waits for them, and re-layouts: 10 us -> 10.7 us
where the time goes in v3:
time: 340 us; the launch traced here: 334 us
  Pallas kernels  225 us (66%)
  starting transfers between devices  43.5 us (13%)
  waiting for transfers between devices  26.3 us (8%)
  other arithmetic  20.9 us (6%)
  local copies, waits for them, and re-layouts  16 us (5%)
    pallas_call x4, Pallas kernels, attend_back(): pl.pallas_call(attend_back_kernel, grid=(frames, pairs), in_specs=in_spec...  62.2 us
    pallas_call x2, Pallas kernels, attend(): pl.pallas_call(functools.partial(attend_kernel, count, chained, final), g...  27.7 us
    pallas_call x1, Pallas kernels, between(): pl.pallas_call(between_kernel, grid=(rows // block,), in_specs=[row(width...  27.3 us
    pallas_call x6, Pallas kernels, block_sums(): pl.pallas_call(functools.partial(block_sums_kernel, counts, dealt), grid_...  24.9 us
    ppermute x22, starting transfers between devices, swap(): return lax.ppermute(values, axis, [(i, i ^ bit) for i in range(count)])  21.7 us
    pallas_call x4, Pallas kernels, project(): pl.pallas_call(functools.partial(project_kernel, own), grid=(rows // bloc...  21 us
    ppermute x22, waiting for transfers between devices, swap(): return lax.ppermute(values, axis, [(i, i ^ bit) for i in range(count)])  16.6 us
    pallas_call x1, Pallas kernels, late_grads(): pl.pallas_call(functools.partial(late_grads_kernel, count), grid=(3 * thi...  13.4 us
  transfers between devices with their start and end apart: 32, of which 11 were waited for; matrix products, arithmetic and copies ran while one was open for 8% of the time, Pallas kernels for 41%

profile of v3, /device:TPU:0, one launch (start us, length us, event | category | flops | bytes accessed | tf_op | source)
XLA Modules:
  0.0 334.1 jit_solution(12924530464340541328)
XLA Ops:
  0.7 5.1 %collective-permute-start = (bf16[1,512,768]{2,1,0:T(8,128)(2,1)}, bf16[1,512,768]{2,1,0:T(8,128)(2,1)S(1)}, u32[]{:S(2)}, u32[]{:S(2)}) collective-permute-start(bf16[1,512,768]{2,1,0:T(8,128)(2,1)} %bitcast.80), channel_id=1, source_target_pairs={{0,1},{1,2},{2,3},{4,5},{5,6},{6,7},{8,9},{9,10},{10,11},{12,13},{... | collective-permute-start | bytes 2359304 | tf_op jit(solution)/shard_map/ppermute | solution.py:1074
  7.8 8.3 %copy.41 = bf16[1,32,16,2,4416]{4,2,1,3,0:T(8,128)(2,1)} copy(bf16[1,32,16,2,4416]{4,3,2,1,0:T(2,128)(2,1)} %param.21) | data formatting | bytes 18087936 | tf_op args[3]
  16.7 5.8 %project.4 = (bf16[512,768]{1,0:T(8,128)(2,1)}, bf16[512,1536]{1,0:T(8,128)(2,1)}, bf16[512,768]{1,0:T(8,128)(2,1)}) custom-call(bf16[512,768]{1,0:T(8,128)(2,1)} %bitcast.82, f32[768]{0:T(1024)} %refs_3_.5, f32[768]{0:T(1024)} %refs_4_.7, f32[1,768]{1,0:T(1,128)} %fusion.15.refs_3_.refs_5_, bf16[768,2304]{1,0:T(8,128)(2,1)} %w_ref.1, ...), custom_call_target="tpu_custom_call" | custom-call | flops 301989888 | bytes 393216 | tf_op jit(solution)/shard_map/project/pallas_call | solution.py:65
  22.9 4.1 %collective-permute-done.1 = bf16[1,512,768]{2,1,0:T(8,128)(2,1)S(1)} collective-permute-done((bf16[1,512,768]{2,1,0:T(8,128)(2,1)}, bf16[1,512,768]{2,1,0:T(8,128)(2,1)S(1)}, u32[]{:S(2)}, u32[]{:S(2)}) %collective-permute-start.1) | collective-permute-done | bytes 786464 | tf_op jit(solution)/shard_map/ppermute | solution.py:1075
  30.0 10.3 %pixel_sums.1 = (f32[512,128]{1,0:T(8,128)}, f32[512,128]{1,0:T(8,128)}, f32[512,128]{1,0:T(8,128)}) custom-call(bf16[2,512,4416]{2,1,0:T(8,128)(2,1)} %bitcast.78, bf16[512,4416]{1,0:T(8,128)(2,1)} %bitcast.122), custom_call_target="tpu_custom_call" | custom-call | flops 289406976 | bytes 2260992 | tf_op jit(solution)/shard_map/pixel_sums/pallas_call | solution.py:957
  40.3 5.1 %project.5 = (bf16[512,768]{1,0:T(8,128)(2,1)}, bf16[512,1536]{1,0:T(8,128)(2,1)}, bf16[512,768]{1,0:T(8,128)(2,1)}) custom-call(s32[1]{0:T(128)} %bitcast.7.refs_0_, bf16[512,768]{1,0:T(8,128)(2,1)} %bitcast.123, bf16[512,768]{1,0:T(8,128)(2,1)} %bitcast.130, f32[768]{0:T(1024)} %refs_3_.5, f32[768]{0:T(1024)} %refs_4_.7, f32[1,768]{1,0:T(1,128)} %fusion.15.refs_3_.refs_5_, ...), custom_call_target="tpu_custom_call" | custom-call | flops 301989888 | bytes 393216 | tf_op jit(solution)/shard_map/project/pallas_call | solution.py:65
  45.4 4.6 %collective-permute-done.3 = bf16[1,512,768]{2,1,0:T(8,128)(2,1)S(1)} collective-permute-done((bf16[1,512,768]{2,1,0:T(8,128)(2,1)S(1)}, bf16[1,512,768]{2,1,0:T(8,128)(2,1)S(1)}, u32[]{:S(2)}, u32[]{:S(2)}) %collective-permute-start.3) | collective-permute-done | bytes 786464 | tf_op jit(solution)/shard_map/ppermute | solution.py:1129
  52.3 5.1 %project.6 = (bf16[512,768]{1,0:T(8,128)(2,1)}, bf16[512,1536]{1,0:T(8,128)(2,1)}, bf16[512,768]{1,0:T(8,128)(2,1)}) custom-call(s32[1]{0:T(128)} %bitcast.15.refs_0_, bf16[512,768]{1,0:T(8,128)(2,1)} %bitcast.119, bf16[512,768]{1,0:T(8,128)(2,1)} %bitcast.124, f32[768]{0:T(1024)} %refs_3_.5, f32[768]{0:T(1024)} %refs_4_.7, ...), custom_call_target="tpu_custom_call" | custom-call | flops 301989888 | bytes 393216 | tf_op jit(solution)/shard_map/project/pallas_call | solution.py:65
  57.4 18.2 %attend.2 = (f32[1,768,512]{2,1,0:T(8,128)}, f32[1,6,2,512]{3,2,1,0:T(2,128)}) custom-call(bf16[1,512,768]{2,1,0:T(8,128)(2,1)} %bitcast.93, bf16[1,512,1536]{2,1,0:T(8,128)(2,1)} %bitcast.99, bf16[1,512,1536]{2,1,0:T(8,128)(2,1)} %bitcast.103, bf16[1,512,1536]{2,1,0:T(8,128)(2,1)} %bitcast.107, bf16[1,512,1536]{2,1,0:T(8,128)(2,1)} %bitcast.100, ...), custom_call_target="tpu_custom_call" | custom-call | flops 1207959552 | bytes 393216 | tf_op jit(solution)/shard_map/attend/pallas_call | solution.py:137
  76.5 5.1 %project.7 = (bf16[512,768]{1,0:T(8,128)(2,1)}, bf16[512,1536]{1,0:T(8,128)(2,1)}, bf16[512,768]{1,0:T(8,128)(2,1)}) custom-call(s32[1]{0:T(128)} %bitcast.15.refs_0_, bf16[512,768]{1,0:T(8,128)(2,1)} %bitcast.129, bf16[512,768]{1,0:T(8,128)(2,1)} %bitcast.120, f32[768]{0:T(1024)} %refs_3_.5, f32[768]{0:T(1024)} %refs_4_.7, ...), custom_call_target="tpu_custom_call" | custom-call | flops 301989888 | bytes 393216 | tf_op jit(solution)/shard_map/project/pallas_call | solution.py:65
  81.6 9.6 %attend.3 = (bf16[1,512,768]{2,1,0:T(8,128)(2,1)}, f32[1,6,2,512]{3,2,1,0:T(2,128)}) custom-call(bf16[1,512,768]{2,1,0:T(8,128)(2,1)} %bitcast.94, bf16[1,512,1536]{2,1,0:T(8,128)(2,1)} %bitcast.111, bf16[1,512,1536]{2,1,0:T(8,128)(2,1)} %bitcast.112, f32[1,768,512]{2,1,0:T(8,128)} %get-tuple-element.207.refs_3_, f32[1,6,2,512]{3,2,1,0:T(2,128)} %get-tuple-element.208.refs_4_), custom_call_target="tpu_custom_call" | custom-call | flops 402653184 | bytes 393216 | tf_op jit(solution)/shard_map/attend/pallas_call | solution.py:137
  91.1 27.3 %between.1 = (bf16[512,768]{1,0:T(8,128)(2,1)}, bf16[512,3072]{1,0:T(8,128)(2,1)}, bf16[512,3072]{1,0:T(8,128)(2,1)}, bf16[512,768]{1,0:T(8,128)(2,1)}, bf16[512...) custom-call(bf16[512,768]{1,0:T(8,128)(2,1)} %bitcast.83, ...), custom_call_target="tpu_custom_call" | custom-call | flops 1207959552 | bytes 1572864 | tf_op jit(solution)/shard_map/between/pallas_call | solution.py:444
  123.1 8.5 %down_grads.1 = (bf16[8,48,7168]{2,1,0:T(8,128)(2,1)}, bf16[8,48,7168]{2,1,0:T(8,128)(2,1)}) custom-call(s32[1]{0:T(128)} %bitcast.3.place_ref, bf16[512,3072]{1,0:T(8,128)(2,1)} %get-tuple-element.222.act_ref, bf16[512,768]{1,0:T(8,128)(2,1)} %get-tuple-element.223.down_ref), custom_call_target="tpu_custom_call" | custom-call | flops 301989888 | bytes 294912 | tf_op jit(solution)/shard_map/down_grads/pallas_call | solution.py:623
  131.6 10.6 %early_grads.1 = (bf16[8,48,7168]{2,1,0:T(8,128)(2,1)}, bf16[8,48,7168]{2,1,0:T(8,128)(2,1)}) custom-call(s32[1]{0:T(128)} %bitcast.3.place_ref, bf16[512,768]{1,0:T(8,128)(2,1)} %get-tuple-element.215.h_ref, bf16[512,768]{1,0:T(8,128)(2,1)} %bitcast.92, bf16[512,768]{1,0:T(8,128)(2,1)} %get-tuple-element.216.f_ref, ...), custom_call_target="tpu_custom_call", output_to_operand_aliasing={{0}: (8, {}), {1}: (9, {})} | custom-call | flops 3221225472 | bytes 10485760 | tf_op jit(solution)/shard_map/early_grads/pallas_call | solution.py:567
  144.2 15.5 %attend_back.4 = (f32[1,768,512]{2,1,0:T(8,128)}, bf16[1,512,1536]{2,1,0:T(8,128)(2,1)}, bf16[1,512,768]{2,1,0:T(8,128)(2,1)}, f32[1,2,768]{2,1,0:T(2,128)}) custom-call(bf16[1,512,768]{2,1,0:T(8,128)(2,1)} %bitcast.95, bf16[1,512,768]{2,1,0:T(8,128)(2,1)} %bitcast.115, ...), custom_call_target="tpu_custom_call", output_to_operand_aliasing={{0}: (9, {})} | custom-call | flops 805306368 | bytes 393216 | tf_op jit(solution)/shard_map/attend_back/pallas_call | solution.py:252
  159.7 4.6 %block_sums.6 = (bf16[4,2,24,3584]{3,2,1,0:T(8,128)(2,1)}, bf16[2,4,24,3584]{3,2,1,0:T(8,128)(2,1)}) custom-call(s32[3]{0:T(128)} %pad_add_fusion.where_ref, bf16[2,4,2,24,7168]{4,3,2,1,0:T(8,128)(2,1)} %bitcast.72, bf16[2,4,2,24,7168]{4,3,2,1,0:T(8,128)(2,1)} %bitcast.33.refs_1_.refs_3_.refs_4_.refs_5_, bf16[2,4,2,24,7168]{4,3,2,1,0:T(8,128)(2,1)} %bitcast.73, ...), custom_call_target="tpu_custom_call" | custom-call | flops 1048576 | bytes 1048576 | tf_op jit(solution)/shard_map/block_sums/pallas_call | solution.py:734
  164.3 4.6 %collective-permute-start.6 = (bf16[1,512,768]{2,1,0:T(8,128)(2,1)}, bf16[1,512,768]{2,1,0:T(8,128)(2,1)S(1)}, u32[]{:S(2)}, u32[]{:S(2)}) collective-permute-start(bf16[1,512,768]{2,1,0:T(8,128)(2,1)} %get-tuple-element.242), channel_id=1, source_target_pairs={{0,1},{3,2},{4,5},{7,6},{8,9},{11,10},{12,13},{15,14},{16,17},{19,... | collective-permute-start | bytes 2359304 | tf_op jit(solution)/shard_map/ppermute | solution.py:1241
  172.0 15.6 %attend_back.5 = (f32[1,768,512]{2,1,0:T(8,128)}, bf16[1,512,1536]{2,1,0:T(8,128)(2,1)}, bf16[1,512,768]{2,1,0:T(8,128)(2,1)}, f32[1,2,768]{2,1,0:T(2,128)}) custom-call(bf16[1,512,768]{2,1,0:T(8,128)(2,1)} %bitcast.96, bf16[1,512,768]{2,1,0:T(8,128)(2,1)} %bitcast.116, ...), custom_call_target="tpu_custom_call", output_to_operand_aliasing={{0}: (9, {})} | custom-call | flops 805306368 | bytes 393216 | tf_op jit(solution)/shard_map/attend_back/pallas_call | solution.py:252
  190.0 3.1 collective-permute-start.7
  194.6 15.5 %attend_back.6 = (f32[1,768,512]{2,1,0:T(8,128)}, bf16[1,512,1536]{2,1,0:T(8,128)(2,1)}, bf16[1,512,768]{2,1,0:T(8,128)(2,1)}, f32[1,2,768]{2,1,0:T(2,128)}) custom-call(bf16[1,512,768]{2,1,0:T(8,128)(2,1)} %bitcast.97, bf16[1,512,768]{2,1,0:T(8,128)(2,1)} %bitcast.117, ...), custom_call_target="tpu_custom_call", output_to_operand_aliasing={{0}: (9, {})} | custom-call | flops 805306368 | bytes 393216 | tf_op jit(solution)/shard_map/attend_back/pallas_call | solution.py:252
  210.1 3.9 %block_sums.7 = (bf16[4,24,3584]{2,1,0:T(8,128)(2,1)}, bf16[4,24,3584]{2,1,0:T(8,128)(2,1)}) custom-call(s32[3]{0:T(128)} %pad_add_fusion.where_ref, bf16[2,4,2,24,7168]{4,3,2,1,0:T(8,128)(2,1)} %bitcast.74, bf16[2,4,2,24,7168]{4,3,2,1,0:T(8,128)(2,1)} %bitcast.33.refs_1_.refs_3_.refs_4_.refs_5_, bf16[4,2,24,3584]{3,2,1,0:T(8,128)(2,1)} %collective-permute-done.9.refs_2_, ...), custom_call_target="tpu_custom_call" | custom-call | flops 1048576 | bytes 1048576 | tf_op jit(solution)/shard_map/block_sums/pallas_call | solution.py:734
  223.2 15.6 %attend_back.7 = (f32[1,768,512]{2,1,0:T(8,128)}, bf16[1,512,1536]{2,1,0:T(8,128)(2,1)}, bf16[1,512,768]{2,1,0:T(8,128)(2,1)}, f32[1,2,768]{2,1,0:T(2,128)}) custom-call(bf16[1,512,768]{2,1,0:T(8,128)(2,1)} %bitcast.98, bf16[1,512,768]{2,1,0:T(8,128)(2,1)} %bitcast.118, ...), custom_call_target="tpu_custom_call", output_to_operand_aliasing={{0}: (9, {})} | custom-call | flops 805306368 | bytes 393216 | tf_op jit(solution)/shard_map/attend_back/pallas_call | solution.py:252
  239.6 4.4 %query_back.1 = (bf16[1,768,512]{2,1,0:T(8,128)(2,1)}, f32[1,512,768]{2,1,0:T(8,128)}, f32[1,2,768]{2,1,0:T(2,128)}) custom-call(f32[1,768,512]{2,1,0:T(8,128)} %get-tuple-element.260.dq_ref, bf16[768,2304]{1,0:T(8,128)(2,1)} %w_ref.1, bf16[1,512,768]{2,1,0:T(8,128)(2,1)} %bitcast.85), custom_call_target="tpu_custom_call" | custom-call | flops 301989888 | bytes 393216 | tf_op jit(solution)/shard_map/query_back/pallas_call | solution.py:283
  245.6 13.4 %late_grads.1 = (bf16[8,48,2560]{2,1,0:T(8,128)(2,1)}, bf16[8,48,2560]{2,1,0:T(8,128)(2,1)}) custom-call(s32[1]{0:T(128)} %bitcast.3.place_ref, bf16[512,768]{1,0:T(8,128)(2,1)} %get-tuple-element.182.refs_0_, bf16[512,768]{1,0:T(8,128)(2,1)} %get-tuple-element.187.refs_1_, bf16[512,768]{1,0:T(8,128)(2,1)} %get-tuple-element.197.refs_2_, ...), custom_call_target="tpu_custom_call" | custom-call | flops 5435817984 | bytes 19660800 | tf_op jit(solution)/shard_map/late_grads/pallas_call | solution.py:678
  259.1 5.7 %block_sums.8 = (bf16[2,24,3584]{2,1,0:T(8,128)(2,1)}, bf16[2,24,3584]{2,1,0:T(8,128)(2,1)}, bf16[2,24,3584]{2,1,0:T(8,128)(2,1)}, bf16[2,24,3584]{2,1,0:T(8,128)(2,1)}) custom-call(s32[3]{0:T(128)} %pad_add_fusion.where_ref, bf16[2,4,2,24,7168]{4,3,2,1,0:T(8,128)(2,1)} %bitcast.76, bf16[2,4,2,24,7168]{4,3,2,1,0:T(8,128)(2,1)} %bitcast.33.refs_1_.refs_3_.refs_4_.refs_5_, ...), custom_call_target="tpu_custom_call" | custom-call | flops 1048576 | bytes 1048576 | tf_op jit(solution)/shard_map/block_sums/pallas_call | solution.py:734
  264.9 3.2 block_sums.9
  277.2 9.3 %blend.1 = bf16[512,4416]{1,0:T(8,128)(2,1)} custom-call(f32[512,128]{1,0:T(8,128)} %get-tuple-element.292.a_ref, f32[512,128]{1,0:T(8,128)} %get-tuple-element.293.b_ref, f32[512,128]{1,0:T(8,128)} %get-tuple-element.294.c_ref, bf16[2,512,4416]{2,1,0:T(8,128)(2,1)} %bitcast.79), custom_call_target="tpu_custom_call" | custom-call | flops 289406976 | bytes 2260992 | tf_op jit(solution)/shard_map/blend/pallas_call | solution.py:996
  286.5 3.0 block_sums.10
  290.6 3.3 fusion.21
  297.0 4.5 %block_sums.11 = (bf16[1,24,2560]{2,1,0:T(8,128)(2,1)}, bf16[1,24,2560]{2,1,0:T(8,128)(2,1)}, bf16[1,24,2560]{2,1,0:T(8,128)(2,1)}, bf16[1,24,2560]{2,1,0:T(8,128)(2,1)}) custom-call(s32[3]{0:T(128)} %pad_add_fusion.where_ref, bf16[2,4,2,24,2560]{4,3,2,1,0:T(8,128)(2,1)} %bitcast.90, bf16[2,4,2,24,2560]{4,3,2,1,0:T(8,128)(2,1)} %bitcast.43.refs_1_.refs_3_.refs_4_, ...), custom_call_target="tpu_custom_call" | custom-call | flops 1048576 | bytes 1048576 | tf_op jit(solution)/shard_map/block_sums/pallas_call | solution.py:734
  304.5 5.0 %collective-permute-done.20 = bf16[1,24,2560]{2,1,0:T(8,128)(2,1)S(1)} collective-permute-done((bf16[1,24,2560]{2,1,0:T(8,128)(2,1)}, bf16[1,24,2560]{2,1,0:T(8,128)(2,1)S(1)}, u32[]{:S(2)}, u32[]{:S(2)}) %collective-permute-start.20) | collective-permute-done | bytes 122912 | tf_op jit(solution)/shard_map/ppermute | solution.py:1013
  317.5 8.1 %collective-permute-done.28.refs_1_ = bf16[24,2560]{1,0:T(8,128)(2,1)} collective-permute-done((bf16[24,2560]{1,0:T(8,128)(2,1)S(1)}, bf16[24,2560]{1,0:T(8,128)(2,1)}, u32[]{:S(2)}, u32[]{:S(2)}) %collective-permute-start.28) | collective-permute-done | bytes 122912 | tf_op jit(solution)/shard_map/ppermute | solution.py:1013
  (160 shorter events, 66.2 us)
Async XLA Ops:
  0.7 22.2 %collective-permute-start = (bf16[1,512,768]{2,1,0:T(8,128)(2,1)}, bf16[1,512,768]{2,1,0:T(8,128)(2,1)S(1)}, u32[]{:S(2)}, u32[]{:S(2)}) collective-permute-start(bf16[1,512,768]{2,1,0:T(8,128)(2,1)} %bitcast.80), channel_id=1, source_target_pairs={{0,1},{1,2},{2,3},{4,5},{5,6},{6,7},{8,9},{9,10},{10,11},{12,13},{... | collective-permute-start | bytes 2359304 | tf_op jit(solution)/shard_map/ppermute | solution.py:1074
  5.8 21.1 %collective-permute-start.1 = (bf16[1,512,768]{2,1,0:T(8,128)(2,1)}, bf16[1,512,768]{2,1,0:T(8,128)(2,1)S(1)}, u32[]{:S(2)}, u32[]{:S(2)}) collective-permute-start(bf16[1,512,768]{2,1,0:T(8,128)(2,1)} %bitcast.81), channel_id=1, source_target_pairs={{3,2},{2,1},{1,0},{7,6},{6,5},{5,4},{11,10},{10,9},{9,8},{15,14},{... | collective-permute-start | bytes 2359304 | tf_op jit(solution)/shard_map/ppermute | solution.py:1075
  26.9 18.5 %collective-permute-start.2 = (bf16[1,512,768]{2,1,0:T(8,128)(2,1)S(1)}, bf16[1,512,768]{2,1,0:T(8,128)(2,1)S(1)}, u32[]{:S(2)}, u32[]{:S(2)}) collective-permute-start(bf16[1,512,768]{2,1,0:T(8,128)(2,1)S(1)} %collective-permute-done), channel_id=1, source_target_pairs={{1,2},{2,3},{5,6},{6,7},{9,10},{10,11},{13,14},{14,15},{17,18},{18... | collective-permute-start | bytes 2359304 | tf_op jit(solution)/shard_map/ppermute | solution.py:1128
  27.6 22.4 %collective-permute-start.3 = (bf16[1,512,768]{2,1,0:T(8,128)(2,1)S(1)}, bf16[1,512,768]{2,1,0:T(8,128)(2,1)S(1)}, u32[]{:S(2)}, u32[]{:S(2)}) collective-permute-start(bf16[1,512,768]{2,1,0:T(8,128)(2,1)S(1)} %collective-permute-done.1), channel_id=1, source_target_pairs={{2,1},{1,0},{6,5},{5,4},{10,9},{9,8},{14,13},{13,12},{18,17},{17,1... | collective-permute-start | bytes 2359304 | tf_op jit(solution)/shard_map/ppermute | solution.py:1129
  50.2 25.4 %collective-permute-start.4 = (bf16[1,512,768]{2,1,0:T(8,128)(2,1)S(1)}, bf16[1,512,768]{2,1,0:T(8,128)(2,1)S(1)}, u32[]{:S(2)}, u32[]{:S(2)}) collective-permute-start(bf16[1,512,768]{2,1,0:T(8,128)(2,1)S(1)} %add.184), channel_id=1, source_target_pairs={{2,3},{1,0},{6,7},{5,4},{10,11},{9,8},{14,15},{13,12},{18,19},{17,... | collective-permute-start | bytes 2359304 | tf_op jit(solution)/shard_map/ppermute | solution.py:1139
  142.3 17.4 %collective-permute-start.5 = (bf16[8,48,7168]{2,1,0:T(8,128)(2,1)}, bf16[8,48,7168]{2,1,0:T(8,128)(2,1)}, u32[]{:S(2)}, u32[]{:S(2)}) collective-permute-start(bf16[8,48,7168]{2,1,0:T(8,128)(2,1)} %get-tuple-element.236), channel_id=1, source_target_pairs={{0,8},{8,0},{16,24},{24,16},{1,9},{9,1},{17,25},{25,17},{2,10},{10... | collective-permute-start | bytes 16515080 | tf_op jit(solution)/shard_map/ppermute | solution.py:1013
  164.3 23.3 %collective-permute-start.6 = (bf16[1,512,768]{2,1,0:T(8,128)(2,1)}, bf16[1,512,768]{2,1,0:T(8,128)(2,1)S(1)}, u32[]{:S(2)}, u32[]{:S(2)}) collective-permute-start(bf16[1,512,768]{2,1,0:T(8,128)(2,1)} %get-tuple-element.242), channel_id=1, source_target_pairs={{0,1},{3,2},{4,5},{7,6},{8,9},{11,10},{12,13},{15,14},{16,17},{19,... | collective-permute-start | bytes 2359304 | tf_op jit(solution)/shard_map/ppermute | solution.py:1241
  168.9 41.2 %collective-permute-start.9 = (bf16[4,2,24,3584]{3,2,1,0:T(8,128)(2,1)}, bf16[4,2,24,3584]{3,2,1,0:T(8,128)(2,1)}, u32[]{:S(2)}, u32[]{:S(2)}) collective-permute-start(bf16[4,2,24,3584]{3,2,1,0:T(8,128)(2,1)} %get-tuple-element.247), channel_id=1, source_target_pairs={{0,4},{4,0},{1,5},{5,1},{2,6},{6,2},{3,7},{7,3},{8,12},{12,8},{9,1... | collective-permute-start | bytes 4128776 | tf_op jit(solution)/shard_map/ppermute | solution.py:1013
  170.5 39.6 %collective-permute-start.10 = (bf16[2,4,24,3584]{3,2,1,0:T(8,128)(2,1)}, bf16[2,4,24,3584]{3,2,1,0:T(8,128)(2,1)}, u32[]{:S(2)}, u32[]{:S(2)}) collective-permute-start(bf16[2,4,24,3584]{3,2,1,0:T(8,128)(2,1)} %get-tuple-element.248), channel_id=1, source_target_pairs={{0,16},{8,24},{16,0},{24,8},{1,17},{9,25},{17,1},{25,9},{2,18},{10... | collective-permute-start | bytes 4128776 | tf_op jit(solution)/shard_map/ppermute | solution.py:1013
  190.0 24.0 %collective-permute-start.7 = (bf16[1,512,768]{2,1,0:T(8,128)(2,1)}, bf16[1,512,768]{2,1,0:T(8,128)(2,1)}, u32[]{:S(2)}, u32[]{:S(2)}) collective-permute-start(bf16[1,512,768]{2,1,0:T(8,128)(2,1)} %fusion.5), channel_id=1, source_target_pairs={{0,1},{1,2},{4,5},{5,6},{8,9},{9,10},{12,13},{13,14},{16,17},{17,1... | collective-permute-start | bytes 2359304 | tf_op jit(solution)/shard_map/ppermute | solution.py:1247
  193.0 23.0 %collective-permute-start.8 = (bf16[1,512,768]{2,1,0:T(8,128)(2,1)}, bf16[1,512,768]{2,1,0:T(8,128)(2,1)}, u32[]{:S(2)}, u32[]{:S(2)}) collective-permute-start(bf16[1,512,768]{2,1,0:T(8,128)(2,1)} %fusion.5), channel_id=1, source_target_pairs={{3,2},{2,1},{7,6},{6,5},{11,10},{10,9},{15,14},{14,13},{19,18},{18... | collective-permute-start | bytes 2359304 | tf_op jit(solution)/shard_map/ppermute | solution.py:1248
  217.4 21.5 %collective-permute-start.11 = (bf16[1,512,768]{2,1,0:T(8,128)(2,1)S(1)}, bf16[1,512,768]{2,1,0:T(8,128)(2,1)S(1)}, u32[]{:S(2)}, u32[]{:S(2)}) collective-permute-start(bf16[1,512,768]{2,1,0:T(8,128)(2,1)S(1)} %fusion.6), channel_id=1, source_target_pairs={{0,1},{1,2},{2,3},{4,5},{5,6},{6,7},{8,9},{9,10},{10,11},{12,13},{... | collective-permute-start | bytes 2359304 | tf_op jit(solution)/shard_map/ppermute | solution.py:1256
  218.8 20.8 %collective-permute-start.12 = (bf16[1,512,768]{2,1,0:T(8,128)(2,1)S(1)}, bf16[1,512,768]{2,1,0:T(8,128)(2,1)S(1)}, u32[]{:S(2)}, u32[]{:S(2)}) collective-permute-start(bf16[1,512,768]{2,1,0:T(8,128)(2,1)S(1)} %add_convert_fusion), channel_id=1, source_target_pairs={{3,2},{2,1},{1,0},{7,6},{6,5},{5,4},{11,10},{10,9},{9,8},{15,14},{... | collective-permute-start | bytes 2359304 | tf_op jit(solution)/shard_map/ppermute | solution.py:1257
  220.1 18.8 %collective-permute-start.13 = (bf16[4,24,3584]{2,1,0:T(8,128)(2,1)}, bf16[4,24,3584]{2,1,0:T(8,128)(2,1)S(1)}, u32[]{:S(2)}, u32[]{:S(2)}) collective-permute-start(bf16[4,24,3584]{2,1,0:T(8,128)(2,1)} %get-tuple-element.258), channel_id=1, source_target_pairs={{0,16},{8,24},{16,0},{24,8},{1,17},{9,25},{17,1},{25,9},{2,18},{10... | collective-permute-start | bytes 2064392 | tf_op jit(solution)/shard_map/ppermute | solution.py:1013
  221.6 17.2 %collective-permute-start.14 = (bf16[4,24,3584]{2,1,0:T(8,128)(2,1)}, bf16[4,24,3584]{2,1,0:T(8,128)(2,1)}, u32[]{:S(2)}, u32[]{:S(2)}) collective-permute-start(bf16[4,24,3584]{2,1,0:T(8,128)(2,1)} %get-tuple-element.259), channel_id=1, source_target_pairs={{0,4},{4,0},{1,5},{5,1},{2,6},{6,2},{3,7},{7,3},{8,12},{12,8},{9,1... | collective-permute-start | bytes 2064392 | tf_op jit(solution)/shard_map/ppermute | solution.py:1013
  259.0 5.9 %collective-permute-start.15 = (bf16[8,48,2560]{2,1,0:T(8,128)(2,1)}, bf16[8,48,2560]{2,1,0:T(8,128)(2,1)}, u32[]{:S(2)}, u32[]{:S(2)}) collective-permute-start(bf16[8,48,2560]{2,1,0:T(8,128)(2,1)} %get-tuple-element.277), channel_id=1, source_target_pairs={{0,8},{8,0},{16,24},{24,16},{1,9},{9,1},{17,25},{25,17},{2,10},{10... | collective-permute-start | bytes 5898248 | tf_op jit(solution)/shard_map/ppermute | solution.py:1013
  268.1 18.4 %collective-permute-start.16 = (bf16[2,2,24,2560]{3,2,1,0:T(8,128)(2,1)}, bf16[2,2,24,2560]{3,2,1,0:T(8,128)(2,1)}, u32[]{:S(2)}, u32[]{:S(2)}) collective-permute-start(bf16[2,2,24,2560]{3,2,1,0:T(8,128)(2,1)} %get-tuple-element.290), channel_id=1, source_target_pairs={{0,4},{4,0},{1,5},{5,1},{2,6},{6,2},{3,7},{7,3},{8,12},{12,8},{9,1... | collective-permute-start | bytes 1474568 | tf_op jit(solution)/shard_map/ppermute | solution.py:1013
  269.6 16.9 %collective-permute-start.17 = (bf16[2,2,24,2560]{3,2,1,0:T(8,128)(2,1)}, bf16[2,2,24,2560]{3,2,1,0:T(8,128)(2,1)}, u32[]{:S(2)}, u32[]{:S(2)}) collective-permute-start(bf16[2,2,24,2560]{3,2,1,0:T(8,128)(2,1)} %get-tuple-element.291), channel_id=1, source_target_pairs={{0,16},{8,24},{16,0},{24,8},{1,17},{9,25},{17,1},{25,9},{2,18},{10... | collective-permute-start | bytes 1474568 | tf_op jit(solution)/shard_map/ppermute | solution.py:1013
  272.8 38.7 %collective-permute-start.24 = (bf16[2,24,3584]{2,1,0:T(8,128)(2,1)}, bf16[2,24,3584]{2,1,0:T(8,128)(2,1)S(1)}, u32[]{:S(2)}, u32[]{:S(2)}) collective-permute-start(bf16[2,24,3584]{2,1,0:T(8,128)(2,1)} %get-tuple-element.323), channel_id=1, source_target_pairs={{0,3},{1,2},{2,1},{3,0},{4,7},{5,6},{6,5},{7,4},{8,11},{9,10},{10,... | collective-permute-start | bytes 1032200 | tf_op jit(solution)/shard_map/ppermute | solution.py:1013
  274.1 37.3 %collective-permute-start.23 = (bf16[2,24,3584]{2,1,0:T(8,128)(2,1)}, bf16[2,24,3584]{2,1,0:T(8,128)(2,1)}, u32[]{:S(2)}, u32[]{:S(2)}) collective-permute-start(bf16[2,24,3584]{2,1,0:T(8,128)(2,1)} %get-tuple-element.322), channel_id=1, source_target_pairs={{0,2},{1,3},{2,0},{3,1},{4,6},{5,7},{6,4},{7,5},{8,10},{9,11},{10,... | collective-permute-start | bytes 1032200 | tf_op jit(solution)/shard_map/ppermute | solution.py:1013
  275.8 36.3 %collective-permute-start.22 = (bf16[2,24,3584]{2,1,0:T(8,128)(2,1)}, bf16[2,24,3584]{2,1,0:T(8,128)(2,1)}, u32[]{:S(2)}, u32[]{:S(2)}) collective-permute-start(bf16[2,24,3584]{2,1,0:T(8,128)(2,1)} %get-tuple-element.321), channel_id=1, source_target_pairs={{0,1},{1,0},{2,3},{3,2},{4,5},{5,4},{6,7},{7,6},{8,9},{9,8},{10,11... | collective-permute-start | bytes 1032200 | tf_op jit(solution)/shard_map/ppermute | solution.py:1013
  289.5 7.3 %collective-permute-start.18 = (bf16[2,24,2560]{2,1,0:T(8,128)(2,1)}, bf16[2,24,2560]{2,1,0:T(8,128)(2,1)}, u32[]{:S(2)}, u32[]{:S(2)}) collective-permute-start(bf16[2,24,2560]{2,1,0:T(8,128)(2,1)} %get-tuple-element.302), channel_id=1, source_target_pairs={{0,16},{8,24},{16,0},{24,8},{1,17},{9,25},{17,1},{25,9},{2,18},{10... | collective-permute-start | bytes 737288 | tf_op jit(solution)/shard_map/ppermute | solution.py:1013
  290.0 7.0 %collective-permute-start.19 = (bf16[2,24,2560]{2,1,0:T(8,128)(2,1)}, bf16[2,24,2560]{2,1,0:T(8,128)(2,1)}, u32[]{:S(2)}, u32[]{:S(2)}) collective-permute-start(bf16[2,24,2560]{2,1,0:T(8,128)(2,1)} %get-tuple-element.303), channel_id=1, source_target_pairs={{0,4},{4,0},{1,5},{5,1},{2,6},{6,2},{3,7},{7,3},{8,12},{12,8},{9,1... | collective-permute-start | bytes 737288 | tf_op jit(solution)/shard_map/ppermute | solution.py:1013
  301.5 8.0 %collective-permute-start.20 = (bf16[1,24,2560]{2,1,0:T(8,128)(2,1)}, bf16[1,24,2560]{2,1,0:T(8,128)(2,1)S(1)}, u32[]{:S(2)}, u32[]{:S(2)}) collective-permute-start(bf16[1,24,2560]{2,1,0:T(8,128)(2,1)} %get-tuple-element.317), channel_id=1, source_target_pairs={{0,1},{1,0},{2,3},{3,2},{4,5},{5,4},{6,7},{7,6},{8,9},{9,8},{10,11... | collective-permute-start | bytes 368648 | tf_op jit(solution)/shard_map/ppermute | solution.py:1013
  302.5 9.0 %collective-permute-start.21 = (bf16[1,24,2560]{2,1,0:T(8,128)(2,1)}, bf16[1,24,2560]{2,1,0:T(8,128)(2,1)S(1)}, u32[]{:S(2)}, u32[]{:S(2)}) collective-permute-start(bf16[1,24,2560]{2,1,0:T(8,128)(2,1)} %get-tuple-element.318), channel_id=1, source_target_pairs={{0,2},{1,3},{2,0},{3,1},{4,6},{5,7},{6,4},{7,5},{8,10},{9,11},{10,... | collective-permute-start | bytes 368648 | tf_op jit(solution)/shard_map/ppermute | solution.py:1013
  309.4 7.4 %collective-permute-start.27 = (bf16[1,24,2560]{2,1,0:T(8,128)(2,1)}, bf16[1,24,2560]{2,1,0:T(8,128)(2,1)S(1)}, u32[]{:S(2)}, u32[]{:S(2)}) collective-permute-start(bf16[1,24,2560]{2,1,0:T(8,128)(2,1)} %get-tuple-element.327), channel_id=1, source_target_pairs={{0,3},{1,2},{2,1},{3,0},{4,7},{5,6},{6,5},{7,4},{8,11},{9,10},{10,... | collective-permute-start | bytes 368648 | tf_op jit(solution)/shard_map/ppermute | solution.py:1013
  313.7 12.0 %collective-permute-start.25 = (bf16[2,24,3584]{2,1,0:T(8,128)(2,1)S(1)}, bf16[2,24,3584]{2,1,0:T(8,128)(2,1)S(1)}, u32[]{:S(2)}, u32[]{:S(2)}) collective-permute-start(bf16[2,24,3584]{2,1,0:T(8,128)(2,1)S(1)} %add_convert_fusion.3.refs_0_), channel_id=1, source_target_pairs={{0,16},{8,24},{16,0},{24,8},{1,17},{9,25},{17,1},{25,9},{2,18},{10... | collective-permute-start | bytes 1032200 | tf_op jit(solution)/shard_map/ppermute | solution.py:1013
  315.1 10.6 %collective-permute-start.26 = (bf16[2,24,3584]{2,1,0:T(8,128)(2,1)S(1)}, bf16[2,24,3584]{2,1,0:T(8,128)(2,1)S(1)}, u32[]{:S(2)}, u32[]{:S(2)}) collective-permute-start(bf16[2,24,3584]{2,1,0:T(8,128)(2,1)S(1)} %add_convert_fusion.3.refs_0_), channel_id=1, source_target_pairs={{0,8},{8,0},{16,24},{24,16},{1,9},{9,1},{17,25},{25,17},{2,10},{10... | collective-permute-start | bytes 1032200 | tf_op jit(solution)/shard_map/ppermute | solution.py:1013
  316.9 8.8 %collective-permute-start.28 = (bf16[24,2560]{1,0:T(8,128)(2,1)S(1)}, bf16[24,2560]{1,0:T(8,128)(2,1)}, u32[]{:S(2)}, u32[]{:S(2)}) collective-permute-start(bf16[24,2560]{1,0:T(8,128)(2,1)S(1)} %fusion.14.refs_0_), channel_id=1, source_target_pairs={{0,16},{8,24},{16,0},{24,8},{1,17},{9,25},{17,1},{25,9},{2,18},{10... | collective-permute-start | bytes 368648 | tf_op jit(solution)/shard_map/ppermute | solution.py:1013
  317.5 8.1 %collective-permute-start.29 = (bf16[24,2560]{1,0:T(8,128)(2,1)S(1)}, bf16[24,2560]{1,0:T(8,128)(2,1)S(1)}, u32[]{:S(2)}, u32[]{:S(2)}) collective-permute-start(bf16[24,2560]{1,0:T(8,128)(2,1)S(1)} %fusion.14.refs_0_), channel_id=1, source_target_pairs={{0,8},{8,0},{16,24},{24,16},{1,9},{9,1},{17,25},{25,17},{2,10},{10... | collective-permute-start | bytes 368648 | tf_op jit(solution)/shard_map/ppermute | solution.py:1013
  325.7 1.8 collective-permute-start.31
  326.4 4.1 %collective-permute-start.30 = (bf16[24,2560]{1,0:T(8,128)(2,1)}, bf16[24,2560]{1,0:T(8,128)(2,1)}, u32[]{:S(2)}, u32[]{:S(2)}) collective-permute-start(bf16[24,2560]{1,0:T(8,128)(2,1)} %collective-permute-done.28.refs_1_), channel_id=1, source_target_pairs={{0,8},{8,0},{16,24},{24,16},{1,9},{9,1},{17,25},{25,17},{2,10},{10... | collective-permute-start | bytes 368648 | tf_op jit(solution)/shard_map/ppermute | solution.py:1013
  (31 other events, 233.0 us)
